TPU v7x, 32 devices: a whole 2x2x4 slice. The times are simulated.
32 devices in a mesh: gx: 8 (over y, x, core), gy: 4 (over z).
Axes of the slice: x: 2, y: 2, z: 4, core: 2. Of those that a mesh axis runs over, the one named last changes fastest.
Arguments:
- block_input: bfloat16 [32, 40, 56, 256], P(('gx', 'gy')), may hold values from 0 to 6, as said below
- mid_first: bfloat16 [32, 40, 3584], P(('gx', 'gy')), may hold values from 0 to 6, as said below
- mid_second: bfloat16 [32, 40, 3584], P(('gx', 'gy')), may hold values from 0 to 18, as said below
- out_grad: bfloat16 [32, 40, 56, 256], P(('gx', 'gy')), may hold values from -6 to 6
- params: float32 [64, 1088], replicated, may hold values from -18 to 18
- velocity: float32 [64, 1088], P('gx'), may hold values from -1.8 to 1.8
Outputs:
- input_grad: bfloat16 [32, 40, 56, 256], P(('gx', 'gy'))
- new_velocity: float32 [64, 1088], P('gx')
- next_weights: float32 [64, 1088], replicated
Inputs may be any that keep to these rules, and one draw needn't show every extreme that they name: `block_input`: ReLU outputs: nonnegative, about half of the entries zero. `mid_first`: ReLU outputs: nonnegative, about half of the entries zero. `mid_second`: ReLU outputs: nonnegative, about half of the entries zero.
All inputs are finite; a program needn't handle non-finite values.
Results may differ from a plain program's by a relative error of at most 0.0074.
Values sent between devices are 32-bit elements; how exact they have to be, the bound alone decides.
No kernel may reach another device: no remote copies, remote signals or barrier semaphores. Data moves between devices by JAX's collectives and lax.ppermute only.
A program may use at most 64 MiB of HBM per device.

v0:
```python
import math

import jax
import jax.numpy as jnp
from jax import lax
from jax.sharding import PartitionSpec as P

C_IN = 256
C_MID = 64


learn_rate = 0.5
momentum = 0.9
norm_eps = 1e-06


def tap_patches(field):
    img_height, img_width = (field.shape[0], field.shape[1])
    padded = jnp.pad(field, ((1, 1), (1, 1), (0, 0)))
    pieces = [
        padded[tap_row : tap_row + img_height, tap_col : tap_col + img_width]
        for tap_row in range(3)
        for tap_col in range(3)
    ]
    return jnp.concatenate(pieces, axis=2).reshape(img_height * img_width, 9 * field.shape[2])


def tap_sum(spread):
    img_height, img_width = (spread.shape[0], spread.shape[1])
    padded = jnp.pad(spread, ((1, 1), (1, 1), (0, 0), (0, 0)))
    result = jnp.zeros((img_height, img_width, spread.shape[3]), jnp.float32)
    for tap_row in range(3):
        for tap_col in range(3):
            result = (
                result
                + padded[
                    2 - tap_row : 2 - tap_row + img_height,
                    2 - tap_col : 2 - tap_col + img_width,
                    3 * tap_row + tap_col,
                ]
            )
    return result


def outer_sum(left, right):
    return lax.dot_general(
        left, right, (((0,), (0,)), ((), ())), preferred_element_type=jnp.float32
    )


def layer_squares(matrix):
    return jnp.stack(
        [
            jnp.sum(matrix[:, :C_IN] ** 2),
            jnp.sum(matrix[:, C_IN : C_IN + 9 * C_MID] ** 2),
            jnp.sum(matrix[:, C_IN + 9 * C_MID :] ** 2),
        ]
    )


def trust_columns(trust_ratio):
    return jnp.concatenate(
        [
            jnp.broadcast_to(trust_ratio[0], (C_IN,)),
            jnp.broadcast_to(trust_ratio[1], (9 * C_MID,)),
            jnp.broadcast_to(trust_ratio[2], (C_IN,)),
        ]
    )


def shards(block_input, mid_first, mid_second, out_grad, params, velocity):
    img_height, img_width = (block_input.shape[1], block_input.shape[2])
    pixels = img_height * img_width
    scale_one = 1.0 / math.sqrt(C_IN)
    scale_two = 1.0 / math.sqrt(9 * C_MID)
    scale_three = 1.0 / math.sqrt(C_MID)
    weights = params.astype(jnp.bfloat16)
    w_first = weights[:, :C_IN]
    w_second = weights[:, C_IN : C_IN + 9 * C_MID]
    w_third = weights[:, C_IN + 9 * C_MID :]
    input_flat = block_input.reshape(pixels, C_IN)
    out_flat = out_grad.reshape(pixels, C_IN)
    first_field = mid_first.reshape(img_height, img_width, C_MID)
    second_flat = mid_second.reshape(pixels, C_MID)
    back_second = (
        lax.dot_general(
            out_flat, w_third, (((1,), (1,)), ((), ())), preferred_element_type=jnp.float32
        )
        * scale_three
    )
    back_second = jnp.where(second_flat > 0, back_second, 0.0).astype(jnp.bfloat16)
    spread = jnp.dot(back_second, w_second, preferred_element_type=jnp.float32) * scale_two
    back_first = tap_sum(spread.reshape(img_height, img_width, 9, C_MID))
    back_first = (
        jnp.where(first_field > 0, back_first, 0.0).astype(jnp.bfloat16).reshape(pixels, C_MID)
    )
    input_grad = (
        out_flat.astype(jnp.float32)
        + scale_one * jnp.dot(back_first, w_first, preferred_element_type=jnp.float32)
    ).astype(jnp.bfloat16)
    patches = tap_patches(first_field)
    strips = lax.axis_size("gx") * lax.axis_size("gy")
    mean_factor = 1.0 / strips
    row_count = C_MID // lax.axis_size("gx")
    row_start = lax.axis_index("gx") * row_count
    blocks = [
        scale_one * outer_sum(back_first, input_flat),
        scale_two * outer_sum(back_second, patches),
        scale_three * outer_sum(second_flat, out_flat),
    ]
    own_grad = lax.psum_scatter(
        jnp.concatenate(blocks, axis=1) * mean_factor, "gx", scatter_dimension=0, tiled=True
    )
    own_grad = lax.psum(own_grad, "gy")
    grad_squares = lax.psum(layer_squares(own_grad), "gx")
    trust_ratio = jnp.sqrt(layer_squares(params)) / (jnp.sqrt(grad_squares) + norm_eps)
    own_params = lax.dynamic_slice_in_dim(params, row_start, row_count, 0)
    new_velocity = momentum * velocity + learn_rate * trust_columns(trust_ratio)[None, :] * own_grad
    new_shard = own_params - new_velocity
    next_weights = lax.all_gather(new_shard, "gx", axis=0, tiled=True)
    return (input_grad.reshape(1, img_height, img_width, C_IN), new_velocity, next_weights)


def solution(mesh):
    return jax.shard_map(
        shards,
        mesh=mesh,
        in_specs=(
            P(("gx", "gy"), None, None, None),
            P(("gx", "gy"), None, None),
            P(("gx", "gy"), None, None),
            P(("gx", "gy"), None, None, None),
            P(),
            P("gx", None),
        ),
        out_specs=(P(("gx", "gy"), None, None, None), P("gx", None), P()),
        check_vma=False,
    )
```

profile of v0, /device:TPU:0, one launch (start us, length us, event | category | flops | bytes accessed | tf_op | source)
XLA Modules:
  0.0 199.2 jit_solution(6847218130558249291)
XLA Ops:
  7.2 1.4 reshape.159
  8.7 2.2 %reshape.164 = bf16[40,56,64]{2,1,0:T(8,128)(2,1)} reshape(bf16[1,40,3584]{2,1,0:T(8,128)(2,1)} %param.7) | data formatting | bytes 573440 | tf_op jit(solution)/shard_map/reshape | solution.py:83
  10.9 0.7 convert_element_type.26
  11.6 1.3 reshape.160
  12.9 0.9 copy.35
  13.9 1.0 convolution_multiply_fusion.4
  14.9 2.2 %copy.37 = bf16[40,56,64]{1,0,2:T(8,128)(2,1)} copy(bf16[40,56,64]{2,1,0:T(8,128)(2,1)} %reshape.164) | data formatting | bytes 573440 | tf_op jit(solution)/shard_map/reshape | solution.py:83
  17.1 6.7 %pad_slice_fusion.8 = (bf16[40,56,64]{1,0,2:T(8,128)(2,1)}, bf16[40,56,64]{1,0,2:T(8,128)(2,1)}, bf16[40,56,64]{1,0,2:T(8,128)(2,1)}, bf16[40,56,64]{1,0,2:T(8,1...) fusion(bf16[40,56,64]{1,0,2:T(8,128)(2,1)} %copy.37), kind=kLoop, calls=%fused_computation.26 | loop fusion | bytes 2580480 | tf_op jit(solution)/shard_map/slice | solution.py:21
  23.8 2.2 %copy.53 = bf16[40,56,64]{2,1,0:T(8,128)(2,1)} copy(bf16[40,56,64]{1,0,2:T(8,128)(2,1)} %get-tuple-element.9) | data formatting | bytes 573440 | tf_op jit(solution)/shard_map/concatenate | solution.py:25
  26.0 2.2 %copy.47 = bf16[40,56,64]{2,1,0:T(8,128)(2,1)} copy(bf16[40,56,64]{1,0,2:T(8,128)(2,1)} %get-tuple-element.10) | data formatting | bytes 573440 | tf_op jit(solution)/shard_map/concatenate | solution.py:25
  28.2 2.2 %copy.48 = bf16[40,56,64]{2,1,0:T(8,128)(2,1)} copy(bf16[40,56,64]{1,0,2:T(8,128)(2,1)} %get-tuple-element.11) | data formatting | bytes 573440 | tf_op jit(solution)/shard_map/concatenate | solution.py:25
  30.5 2.2 %copy.49 = bf16[40,56,64]{2,1,0:T(8,128)(2,1)} copy(bf16[40,56,64]{1,0,2:T(8,128)(2,1)} %get-tuple-element.12) | data formatting | bytes 573440 | tf_op jit(solution)/shard_map/concatenate | solution.py:25
  32.7 2.2 %copy.50 = bf16[40,56,64]{2,1,0:T(8,128)(2,1)} copy(bf16[40,56,64]{1,0,2:T(8,128)(2,1)} %get-tuple-element.13) | data formatting | bytes 573440 | tf_op jit(solution)/shard_map/concatenate | solution.py:25
  35.0 2.2 %copy.51 = bf16[40,56,64]{2,1,0:T(8,128)(2,1)} copy(bf16[40,56,64]{1,0,2:T(8,128)(2,1)} %get-tuple-element.14) | data formatting | bytes 573440 | tf_op jit(solution)/shard_map/concatenate | solution.py:25
  37.2 2.2 %copy.52 = bf16[40,56,64]{2,1,0:T(8,128)(2,1)} copy(bf16[40,56,64]{1,0,2:T(8,128)(2,1)} %get-tuple-element.15) | data formatting | bytes 573440 | tf_op jit(solution)/shard_map/concatenate | solution.py:25
  39.5 1.2 copy.46
  40.7 1.5 fusion.3
  42.2 3.2 %convolution_multiply_fusion = f32[2240,576]{0,1:T(8,128)} fusion(bf16[2240,64]{0,1:T(8,128)(2,1)S(1)} %fusion.3, bf16[64,1088]{1,0:T(8,128)(2,1)S(1)} %copy-done.4), kind=kOutput, calls=%fused_computation.8 | convolution fusion | flops 166440960 | bytes 5537792 | tf_op jit(solution)/shard_map/dot_general | solution.py:92
  45.4 7.0 %concatenate.38 = bf16[2240,576]{1,0:T(8,128)(2,1)} concatenate(bf16[2240,64]{1,0:T(8,128)(2,1)} %bitcast.50, bf16[2240,64]{1,0:T(8,128)(2,1)} %bitcast.44, bf16[2240,64]{1,0:T(8,128)(2,1)} %bitcast.45, bf16[2240,64]{1,0:T(8,128)(2,1)} %bitcast.46, bf16[2240,64]{1,0:T(8,128)(2,1)S(1)} %reshape.159, bf16[2240,64]{1,0:T(8,128)(2,1)} %bitcast.47, bf16[2240,64]{1,0:T(8,128)(2,1)} %bitcast.48, ...), dimensions={1} | concatenate | bytes 5160960 | tf_op jit(solution)/shard_map/concatenate | solution.py:25
  52.5 3.1 %convolution_multiply_fusion.3 = f32[64,576]{1,0:T(8,128)} fusion(bf16[2240,64]{0,1:T(8,128)(2,1)S(1)} %fusion.3, bf16[2240,576]{1,0:T(8,128)(2,1)} %concatenate.38), kind=kOutput, calls=%fused_computation.23 | convolution fusion | flops 165187584 | bytes 3014656 | tf_op jit(solution)/shard_map/dot_general | solution.py:46
  55.6 10.5 %reshape.161 = f32[40,56,9,64]{1,0,3,2:T(8,128)} reshape(f32[2240,576]{0,1:T(8,128)} %convolution_multiply_fusion) | data formatting | bytes 10321920 | tf_op jit(solution)/shard_map/reshape | solution.py:93
  66.1 6.5 %fusion.11 = bf16[40,56,1,64]{1,0,3,2:T(8,128)(2,1)S(1)} fusion(f32[40,56,9,64]{1,0,3,2:T(8,128)} %reshape.161), kind=kLoop, calls=%fused_computation.22 | loop fusion | flops 1290240 | bytes 13393920 | tf_op jit(solution)/shard_map/add | solution.py:35
  72.6 1.2 copy.36
  73.8 2.1 %reshape.172 = bf16[1,40,3584]{2,1,0:T(8,128)(2,1)} reshape(bf16[40,56,1,64]{3,1,0,2:T(8,128)(2,1)} %copy.36) | data formatting | bytes 573440 | tf_op jit(solution)/shard_map/add | solution.py:35
  75.9 1.8 select_convert_fusion.1
  77.8 2.1 %convert_element_type.31 = bf16[2240,64]{1,0:T(8,128)(2,1)} reshape(bf16[1,40,3584]{2,1,0:T(8,128)(2,1)} %select_convert_fusion.1) | data formatting | bytes 573440 | tf_op jit(solution)/shard_map/convert_element_type | solution.py:95
  79.9 2.0 %convolution_multiply_fusion.5 = f32[64,256]{1,0:T(8,128)} fusion(bf16[2240,64]{1,0:T(8,128)(2,1)} %convert_element_type.31, bf16[2240,256]{1,0:T(8,128)(2,1)S(1)} %bitcast.39), kind=kOutput, calls=%fused_computation.25 | convolution fusion | flops 73416704 | bytes 1499136 | tf_op jit(solution)/shard_map/dot_general | solution.py:46
  81.9 1.7 concatenate.39
  83.7 1.7 broadcast_multiply_fusion
  85.4 0.9 copy.34
  86.3 1.2 reshape.171
  87.5 2.6 %fusion.1 = bf16[2240,256]{1,0:T(8,128)(2,1)} fusion(bf16[2240,256]{1,0:T(8,128)(2,1)S(1)} %bitcast.42, bf16[2240,64]{0,1:T(8,128)(2,1)} %reshape.171, bf16[2240,64]{0,1:T(8,128)(2,1)} %copy.34, bf16[64,1088]{1,0:T(8,128)(2,1)} %convert_element_type.26), kind=kOutput, calls=%fused_computation.11 | convolution fusion | flops 76267520 | bytes 2916352 | tf_op jit(solution)/shard_map/dot_general | solution.py:99
  90.1 0.7 multiply_reduce_fusion.2
  92.0 0.6 multiply_reduce_fusion
  92.7 49.0 %all-reduce.5.cloned.1.call-done = f32[64,1088]{1,0:T(8,128)} async-done(((f32[64,1088]{1,0:T(8,128)}), f32[64,1088]{1,0:T(8,128)}) %all-reduce.5.cloned.1.call-update) | async-done | bytes 278544
  141.6 0.8 constant_dynamic-slice_fusion
  142.4 19.4 %psum.14 = f32[8,1088]{1,0:T(8,128)S(1)} all-reduce(f32[8,1088]{1,0:T(8,128)S(1)} %constant_dynamic-slice_fusion), channel_id=1, replica_groups=mesh['gx'=8,'gy'=4] {'gy'}, use_global_device_ids=true, to_apply=%region_4.5 | all-reduce | flops 8704 | bytes 69632 | tf_op jit(solution)/shard_map/psum | solution.py:114
  161.8 0.6 fusion.17
  162.4 0.7 fusion.19
  163.1 2.0 pad_maximum_fusion
  165.1 11.8 %psum.15 = f32[3]{0:T(128)S(1)} all-reduce(f32[3]{0:T(128)S(1)} %pad_maximum_fusion), channel_id=1, replica_groups=mesh['gx'=8,'gy'=4] {'gx'}, use_global_device_ids=true, to_apply=%region_8.9 | all-reduce | flops 3 | bytes 24 | tf_op jit(solution)/shard_map/psum | solution.py:115
  176.9 1.9 fusion.20
  178.8 0.7 fusion.23
  179.5 0.6 broadcast_in_dim.22
  180.1 0.7 broadcast_in_dim.20
  180.8 0.6 broadcast_in_dim.21
  182.2 9.4 %all_gather.3 = f32[64,1088]{1,0:T(8,128)S(1)} all-gather(f32[8,1088]{1,0:T(8,128)S(1)} %get-tuple-element.7), channel_id=1, replica_groups=mesh['gx'=8,'gy'=4] {'gx'}, dimensions={0}, use_global_device_ids=true | all-gather | bytes 313344 | tf_op jit(solution)/shard_map/all_gather | solution.py:120
  191.6 0.7 copy.56
  (20 shorter events, 1.4 us)
Async XLA Ops:
  7.2 72.7 %copy-start = (bf16[1,40,56,256]{3,2,1,0:T(8,128)(2,1)S(1)}, bf16[1,40,56,256]{3,2,1,0:T(8,128)(2,1)}, u32[]{:S(2)}) copy-start(bf16[1,40,56,256]{3,2,1,0:T(8,128)(2,1)} %param.6) | copy-start | bytes 3440644
  7.2 3.7 %copy-start.2 = (f32[64,1088]{1,0:T(8,128)S(1)}, f32[64,1088]{1,0:T(8,128)}, u32[]{:S(2)}) copy-start(f32[64,1088]{1,0:T(8,128)} %param.10) | copy-start | bytes 835588
  7.2 134.4 %all-reduce.5.cloned.1.call-start = ((), (), s32[]{:S(2)}) async-start(), calls=%async_computation | async-start | bytes 589824
  8.7 5.2 %copy-start.1 = (bf16[1,40,56,256]{3,2,1,0:T(8,128)(2,1)S(1)}, bf16[1,40,56,256]{3,2,1,0:T(8,128)(2,1)}, u32[]{:S(2)}) copy-start(bf16[1,40,56,256]{3,2,1,0:T(8,128)(2,1)} %param.9) | copy-start | bytes 3440644
  40.7 1.5 copy-start.4
  87.5 2.6 %copy-start.3 = (f32[64,1088]{1,0:T(8,128)S(1)}, f32[64,1088]{1,0:T(8,128)}, u32[]{:S(2)}) copy-start(f32[64,1088]{1,0:T(8,128)} %param.10) | copy-start | bytes 835588
  87.5 3.3 %copy-start.6 = (u32[32]{0:T(128)S(1)}, u32[32]{0:T(128)}, u32[]{:S(2)}) copy-start(u32[32]{0:T(128)} %constant.46) | copy-start | bytes 388
  87.5 94.1 %copy-start.5 = (f32[8,1088]{1,0:T(8,128)S(1)}, f32[8,1088]{1,0:T(8,128)}, u32[]{:S(2)}) copy-start(f32[8,1088]{1,0:T(8,128)} %param.11) | copy-start | bytes 104452
Sparse Core Ops, SparseCore 0:
  85.5 56.0 all-reduce.4
where the time goes:
time: 201 us; the launch traced here: 199 us
  local copies, waits for them, and re-layouts  63.4 us (32%)
  waiting for transfers between devices  49 us (24%)
  blocking collectives  40.6 us (20%)
  other arithmetic  17.8 us (9%)
  between operations  14.8 us (7%)
  matrix products  13.5 us (7%)
    unnamed x2, waiting for transfers between devices  49 us
    concatenate x9, local copies, waits for them, and re-layouts, tap_patches(): jnp.concatenate(pieces, axis=2)  23.9 us
    psum x1, blocking collectives, shards(): own_grad = lax.psum(own_grad, 'gy')  19.4 us
    psum x1, blocking collectives, shards(): grad_squares = lax.psum(layer_squares(own_grad), 'gx')  11.8 us
    reshape x1, local copies, waits for them, and re-layouts, shards(): back_first = tap_sum(spread.reshape(img_height, img_width, 9, C_MID))  10.5 us
    all_gather x1, blocking collectives, shards(): next_weights = lax.all_gather(new_shard, 'gx', axis=0, tiled=True)  9.42 us
    reshape x4, local copies, waits for them, and re-layouts, shards(): first_field = mid_first.reshape(img_height, img_width, C_MID)  6.84 us
    slice x1, local copies, waits for them, and re-layouts, tap_patches(): padded[tap_row:tap_row + img_height, tap_col:tap_col + img_width]  6.67 us
  transfers between devices with their start and end apart: 1, of which 1 were waited for; matrix products, arithmetic and copies ran while one was open for 3% of the time, Pallas kernels for 0%

commit v1 on v0

v1 whole, which is shorter than its diff:
```python
import functools
import math

import jax
import jax.numpy as jnp
from jax import lax
from jax.experimental import pallas as pl
from jax.experimental.pallas import tpu as pltpu
from jax.sharding import PartitionSpec as P

learn_rate = 0.5
momentum = 0.9
norm_eps = 1e-06

F32 = jnp.float32
BF16 = jnp.bfloat16


def divisor_up_to(number, limit):
    return max(d for d in range(1, limit + 1) if number % d == 0)


def spread_pixels(src_ref, dst_ref, base, height, width, mid):
    low = lax.broadcasted_iota(jnp.int32, (height, 2 * mid), 1) < mid
    for pair in range(width // 2):
        slab = src_ref[:, 2 * mid * pair : 2 * mid * (pair + 1)].astype(F32)
        turned = pltpu.roll(slab, mid, 1)
        dst_ref[pl.ds(base + 2 * pair, height, stride=width), :] = jnp.where(low, slab, turned)
        dst_ref[pl.ds(base + 2 * pair + 1, height, stride=width), :] = jnp.where(low, turned, slab)


def grad_kernel(
    core_ref, x_ref, first_ref, second_ref, out_ref, params_ref,
    keep_ref, send_ref, back_ref,
    first_px, second_px, bs_px, spread_px, bs_cols, first_rows, second_bf, taps_ref,
    *, height, width, strips, rows,
):
    c_in = x_ref.shape[1]
    mid = params_ref.shape[0]
    pixels = height * width
    pad = 8
    s_one, s_two, s_three = (1.0 / math.sqrt(n) for n in (c_in, 9 * mid, mid))
    block_rows = divisor_up_to(height, 8)
    step = block_rows * width
    chunks = [slice(k * step, (k + 1) * step) for k in range(height // block_rows)]
    low = lax.broadcasted_iota(jnp.int32, (step, 2 * mid), 1) < mid
    column = lax.broadcasted_iota(jnp.int32, (step, 2 * mid), 0) % width

    w_all = params_ref[...].astype(BF16)
    w_third = w_all[:, c_in + 9 * mid :]
    w_third = jnp.concatenate([w_third, w_third], axis=0)
    taps_ref[...] = jnp.zeros_like(taps_ref)
    for r in range(3):
        for q in range(3):
            t = 3 * r + q
            taps_ref[q * mid : (q + 1) * mid, r * mid : (r + 1) * mid] = params_ref[
                :, c_in + t * mid : c_in + (t + 1) * mid
            ].astype(BF16)

    spread_pixels(second_ref, second_px, 0, height, width, mid)
    first_px[:width, :] = jnp.zeros((width, 2 * mid), F32)
    first_px[width + pixels :, :] = jnp.zeros((width, 2 * mid), F32)
    spread_pixels(first_ref, first_px, width, height, width, mid)

    for c in chunks:
        back = lax.dot_general(out_ref[c, :], w_third, (((1,), (1,)), ((), ())), preferred_element_type=F32)
        second = second_px[c, :]
        bs_px[pad + c.start : pad + c.stop, :] = jnp.where(second > 0, back * s_three, 0.0)
        second_bf[c, :] = second.astype(BF16)

    spread_px[:width, :] = jnp.zeros((width, 4 * mid), F32)
    spread_px[width + pixels :, :] = jnp.zeros((width, 4 * mid), F32)
    for c in chunks:
        here = bs_px[pad + c.start : pad + c.stop, :]
        after = jnp.where(column < width - 1, bs_px[pad + 1 + c.start : pad + 1 + c.stop, :], 0.0)
        before = jnp.where(column > 0, bs_px[pad - 1 + c.start : pad - 1 + c.stop, :], 0.0)
        cols = jnp.concatenate([jnp.where(low, after, here), before], axis=1).astype(BF16)
        bs_cols[c, :] = cols
        spread_px[width + c.start : width + c.stop, :] = jnp.dot(cols, taps_ref[...], preferred_element_type=F32)
        above = first_px[c, :]
        level = first_px[width + c.start : width + c.stop, :]
        below = first_px[2 * width + c.start : 2 * width + c.stop, :]
        first_rows[c, :] = jnp.concatenate([jnp.where(low, above, level), below], axis=1).astype(BF16)

    for c in chunks:
        top = spread_px[2 * width + c.start : 2 * width + c.stop, : 2 * mid]
        centre = pltpu.roll(spread_px[width + c.start : width + c.stop, : 2 * mid], mid, 1)
        bottom = spread_px[c, 2 * mid :]
        total = (top + centre + bottom) * s_two
        total = jnp.where(first_px[width + c.start : width + c.stop, :] > 0, total, 0.0)
        back_ref[c, :] = total[:, :mid].astype(BF16)

    def outer(left, right):
        return lax.dot_general(left, right, (((0,), (0,)), ((), ())), preferred_element_type=F32)

    grad_one = outer(back_ref[...], x_ref[...]) * (s_one / strips)
    grad_two = outer(bs_cols[...], first_rows[...]) * (s_two / strips)
    grad_three = outer(second_bf[...], out_ref[...])[:mid] * (s_three / strips)

    def put(ref, parity):
        for k in range(mid // (2 * rows)):
            lo = (2 * k + parity) * rows
            ref[k, :, :c_in] = grad_one[lo : lo + rows]
            for r in range(3):
                for q in range(3):
                    t = 3 * r + q
                    ref[k, :, c_in + t * mid : c_in + (t + 1) * mid] = grad_two[
                        q * mid + lo : q * mid + lo + rows, r * mid : (r + 1) * mid
                    ]
            ref[k, :, c_in + 9 * mid :] = grad_three[lo : lo + rows]

    for own in range(2):

        @pl.when(core_ref[0] == own)
        def _():
            put(keep_ref, own)
            put(send_ref, 1 - own)


def input_grad_kernel(back_ref, out_ref, params_ref, result_ref):
    c_in = out_ref.shape[1]
    w_first = params_ref[:, :c_in].astype(BF16)
    change = jnp.dot(back_ref[...], w_first, preferred_element_type=F32)
    result_ref[...] = (out_ref[...].astype(F32) + (1.0 / math.sqrt(c_in)) * change).astype(BF16)


def update_kernel(
    place_ref, own_ref, other_ref, own_velocity_ref, other_velocity_ref, params_ref,
    velocity_ref, weights_ref, *, c_in, mid,
):
    core = place_ref[0]
    pair = place_ref[1]
    halves, rows, width = own_ref.shape
    lane = lax.broadcasted_iota(jnp.int32, (1, 1, width), 2)
    edges = (0, c_in, c_in + 9 * mid, width)

    def column_squares(ref):
        return jnp.sum(jnp.sum(ref[...] ** 2, axis=0, keepdims=True), axis=1, keepdims=True)

    grad_squares = column_squares(own_ref) + column_squares(other_ref)
    param_squares = column_squares(params_ref)
    factor = jnp.zeros((1, 1, width), F32)
    for start, stop in zip(edges[:-1], edges[1:]):
        inside = jnp.logical_and(lane >= start, lane < stop)

        def total(squares):
            return jnp.sum(jnp.where(inside, squares, 0.0), axis=2, keepdims=True)

        trust = jnp.sqrt(total(param_squares)) / (jnp.sqrt(total(grad_squares)) + norm_eps)
        factor = jnp.where(inside, learn_rate * trust, factor)
    factor = factor[0]
    for k in range(halves):
        for parity, grad, speed in ((core, own_ref, own_velocity_ref), (1 - core, other_ref, other_velocity_ref)):
            tile = 2 * k + parity
            weights_ref[tile] = params_ref[tile] - (momentum * speed[k ^ pair] + factor * grad[k])
    velocity_ref[...] = momentum * own_velocity_ref[0] + factor * own_ref[pair]


def full_vmem(count):
    return [pl.BlockSpec(memory_space=pltpu.VMEM) for _ in range(count)]


def flip(value, axis, bit):
    return lax.ppermute(value, axis, [(i, i ^ bit) for i in range(lax.axis_size(axis))])


def sum_over(value, axis):
    size = lax.axis_size(axis)
    bit = 1
    while size % (2 * bit) == 0:
        value = value + flip(value, axis, bit)
        bit *= 2
    terms = [value]
    for turn in range(1, size // bit):
        terms.append(lax.ppermute(value, axis, [(i, (i + turn * bit) % size) for i in range(size)]))
    return sum(terms[1:], terms[0])


def shards(block_input, mid_first, mid_second, out_grad, params, velocity):
    _, height, width, c_in = block_input.shape
    mid, row = params.shape
    pixels = height * width
    group = lax.axis_size("gx")
    rows = mid // group
    halves = group // 2
    strips = group * lax.axis_size("gy")
    place = lax.axis_index("gx")
    core = place % 2
    pair = place // 2
    out_flat = out_grad.reshape(pixels, c_in)

    keep, send, back_first = pl.pallas_call(
        functools.partial(grad_kernel, height=height, width=width, strips=strips, rows=rows),
        out_shape=(
            jax.ShapeDtypeStruct((halves, rows, row), F32),
            jax.ShapeDtypeStruct((halves, rows, row), F32),
            jax.ShapeDtypeStruct((pixels, mid), BF16),
        ),
        in_specs=[pl.BlockSpec(memory_space=pltpu.SMEM)] + full_vmem(5),
        out_specs=tuple(full_vmem(3)),
        scratch_shapes=[
            pltpu.VMEM((pixels + 2 * width, 2 * mid), F32),
            pltpu.VMEM((pixels, 2 * mid), F32),
            pltpu.VMEM((pixels + 16, 2 * mid), F32),
            pltpu.VMEM((pixels + 2 * width, 4 * mid), F32),
            pltpu.VMEM((pixels, 4 * mid), BF16),
            pltpu.VMEM((pixels, 4 * mid), BF16),
            pltpu.VMEM((pixels, 2 * mid), BF16),
            pltpu.VMEM((4 * mid, 4 * mid), BF16),
        ],
        name="grads",
    )(
        core.reshape(1),
        block_input.reshape(pixels, c_in),
        mid_first.reshape(height, width * mid),
        mid_second.reshape(height, width * mid),
        out_flat,
        params,
    )

    block = pixels // 4
    input_grad = pl.pallas_call(
        input_grad_kernel,
        out_shape=jax.ShapeDtypeStruct((pixels, c_in), BF16),
        grid=(pixels // block,),
        in_specs=[
            pl.BlockSpec((block, mid), lambda i: (i, 0)),
            pl.BlockSpec((block, c_in), lambda i: (i, 0)),
            pl.BlockSpec((mid, row), lambda i: (0, 0)),
        ],
        out_specs=pl.BlockSpec((block, c_in), lambda i: (i, 0)),
        cost_estimate=pl.CostEstimate(
            flops=2 * pixels * mid * c_in, bytes_accessed=2 * pixels * (2 * c_in + mid), transcendentals=0
        ),
        name="input_grad",
    )(back_first, out_flat, params)

    total = keep + flip(send, "gx", 1)
    speeds = velocity.reshape(1, rows, row)
    bit = 2
    while bit < group:
        total = total + flip(total, "gx", bit)
        speeds = jnp.concatenate([speeds, flip(speeds, "gx", bit)], axis=0)
        bit *= 2
    total = sum_over(total, "gy")
    both = flip(jnp.concatenate([total, speeds], axis=0), "gx", 1)

    new_velocity, next_weights = pl.pallas_call(
        functools.partial(update_kernel, c_in=c_in, mid=mid),
        out_shape=(
            jax.ShapeDtypeStruct((rows, row), F32),
            jax.ShapeDtypeStruct((group, rows, row), F32),
        ),
        in_specs=[pl.BlockSpec(memory_space=pltpu.SMEM)] + full_vmem(5),
        out_specs=tuple(full_vmem(2)),
        name="update",
    )(
        jnp.stack([core, pair]),
        total,
        both[:halves],
        speeds,
        both[halves:],
        params.reshape(group, rows, row),
    )
    return (input_grad.reshape(1, height, width, c_in), new_velocity, next_weights.reshape(mid, row))


def solution(mesh):
    return jax.shard_map(
        shards,
        mesh=mesh,
        in_specs=(
            P(("gx", "gy"), None, None, None),
            P(("gx", "gy"), None, None),
            P(("gx", "gy"), None, None),
            P(("gx", "gy"), None, None, None),
            P(),
            P("gx", None),
        ),
        out_specs=(P(("gx", "gy"), None, None, None), P("gx", None), P()),
        check_vma=False,
    )
```

time: 201 us -> 42.7 us (0.21)
  local copies, waits for them, and re-layouts: 63.4 us -> 0.75 us
  blocking collectives: 40.6 us -> 0 us
  waiting for transfers between devices: 49 us -> 14 us
  other arithmetic: 17.8 us -> 2.35 us
  between operations: 14.8 us -> 0.7 us
  matrix products: 13.5 us -> 0 us
  starting transfers between devices: 0.04 us -> 13.3 us
  Pallas kernels: 0 us -> 11.4 us
    unnamed x2 -> x0, waiting for transfers between devices: 49 us -> none
    psum x2 -> x0, blocking collectives: 31.2 us -> none  [the longest x1 19.4 us: shards(): own_grad = lax.psum(own_grad, 'gy')]
    concatenate x11 -> x0, local copies, waits for them, and re-layouts: 25.8 us -> none  [the longest x9 23.9 us: tap_patches(): jnp.concatenate(pieces, axis=2)]
    reshape x7 -> x0, local copies, waits for them, and re-layouts: 19.6 us -> none  [the longest x1 10.5 us: shards(): back_first = tap_sum(spread.reshape(img_height, img_width, 9, C_MID))]
    ppermute x0 -> x8, waiting for transfers between devices: none -> 14 us  [flip(): lax.ppermute(value, axis, [(i, i ^ bit) for i in range(lax.axis_size(axis...]
    dot_general x6 -> x0, matrix products: 13.5 us -> none  [the longest x3 6.14 us: outer_sum(): lax.dot_general(left, right, (((0,), (0,)), ((), ())), preferred_element_...]
    ppermute x0 -> x8, starting transfers between devices: none -> 13.3 us  [flip(): lax.ppermute(value, axis, [(i, i ^ bit) for i in range(lax.axis_size(axis...]
    pallas_call x0 -> x3, Pallas kernels: none -> 11.4 us  [the longest x1 5.1 us: shards(): pl.pallas_call(functools.partial(grad_kernel, height=height, width=width,...]
  transfers between devices with their start and end apart: 1 -> 8, of which waited for: 1 -> 5; matrix products, arithmetic and copies ran while one was open for 3% -> 3% of each run, Pallas kernels for 0% -> 10%
where the time goes in v1:
time: 42.7 us; the launch traced here: 42.5 us
  waiting for transfers between devices  14 us (33%)
  starting transfers between devices  13.3 us (31%)
  Pallas kernels  11.4 us (27%)
  other arithmetic  2.35 us (6%)
  local copies, waits for them, and re-layouts  0.75 us (2%)
  between operations  0.7 us (2%)
    ppermute x8, waiting for transfers between devices, flip(): lax.ppermute(value, axis, [(i, i ^ bit) for i in range(lax.axis_size(axis...  14 us
    ppermute x8, starting transfers between devices, flip(): lax.ppermute(value, axis, [(i, i ^ bit) for i in range(lax.axis_size(axis...  13.3 us
    pallas_call x1, Pallas kernels, shards(): pl.pallas_call(functools.partial(grad_kernel, height=height, width=width,...  5.1 us
    pallas_call x1, Pallas kernels, shards(): pl.pallas_call(input_grad_kernel, out_shape=jax.ShapeDtypeStruct((pixels,...  4.11 us
    pallas_call x1, Pallas kernels, shards(): pl.pallas_call(functools.partial(update_kernel, c_in=c_in, mid=mid), out_...  2.18 us
    add x1, other arithmetic, shards(): total = keep + flip(send, 'gx', 1)  0.93 us
  transfers between devices with their start and end apart: 8, of which 5 were waited for; matrix products, arithmetic and copies ran while one was open for 3% of the time, Pallas kernels for 10%

profile of v1, /device:TPU:0, one launch (start us, length us, event | category | flops | bytes accessed | tf_op | source)
XLA Modules:
  0.0 42.5 jit_solution(13002579694123242386)
XLA Ops:
  0.6 5.1 %grads.1 = (f32[4,8,1088]{2,1,0:T(8,128)}, f32[4,8,1088]{2,1,0:T(8,128)}, bf16[2240,64]{1,0:T(8,128)(2,1)}) custom-call(s32[1]{0:T(128)} %bitcast.core_ref, bf16[2240,256]{1,0:T(8,128)(2,1)} %bitcast.14, bf16[40,3584]{1,0:T(8,128)(2,1)} %bitcast.19, bf16[40,3584]{1,0:T(8,128)(2,1)} %bitcast.20, bf16[2240,256]{1,0:T(8,128)(2,1)} %bitcast.10, ...), custom_call_target="tpu_custom_call" | custom-call | tf_op jit(solution)/shard_map/grads/pallas_call | solution.py:192
  5.7 0.0 copy-start.1
  5.7 0.5 %collective-permute-start = (f32[4,8,1088]{2,1,0:T(8,128)}, f32[4,8,1088]{2,1,0:T(8,128)S(1)}, u32[]{:S(2)}, u32[]{:S(2)}) collective-permute-start(f32[4,8,1088]{2,1,0:T(8,128)} %get-tuple-element.10), channel_id=1, source_target_pairs={{0,4},{4,0},{8,12},{12,8},{16,20},{20,16},{24,28},{28,24},{1,5},{5... | collective-permute-start | bytes 417800 | tf_op jit(solution)/shard_map/ppermute | solution.py:164
  6.2 1.2 %collective-permute-done = f32[4,8,1088]{2,1,0:T(8,128)S(1)} collective-permute-done((f32[4,8,1088]{2,1,0:T(8,128)}, f32[4,8,1088]{2,1,0:T(8,128)S(1)}, u32[]{:S(2)}, u32[]{:S(2)}) %collective-permute-start) | collective-permute-done | bytes 139296 | tf_op jit(solution)/shard_map/ppermute | solution.py:164
  7.5 0.9 %add.21 = f32[4,8,1088]{2,1,0:T(8,128)S(1)} add(f32[4,8,1088]{2,1,0:T(8,128)} %get-tuple-element.9, f32[4,8,1088]{2,1,0:T(8,128)S(1)} %collective-permute-done) | non-fusion elementwise | flops 34816 | bytes 417792 | tf_op jit(solution)/shard_map/add | solution.py:238
  8.4 2.9 %collective-permute-start.1 = (f32[4,8,1088]{2,1,0:T(8,128)S(1)}, f32[4,8,1088]{2,1,0:T(8,128)S(1)}, u32[]{:S(2)}, u32[]{:S(2)}) collective-permute-start(f32[4,8,1088]{2,1,0:T(8,128)S(1)} %add.21), channel_id=1, source_target_pairs={{0,8},{4,12},{8,0},{12,4},{16,24},{20,28},{24,16},{28,20},{1,9},{5... | collective-permute-start | bytes 417800 | tf_op jit(solution)/shard_map/ppermute | solution.py:164
  11.3 4.2 %collective-permute-done.1 = f32[4,8,1088]{2,1,0:T(8,128)S(1)} collective-permute-done((f32[4,8,1088]{2,1,0:T(8,128)S(1)}, f32[4,8,1088]{2,1,0:T(8,128)S(1)}, u32[]{:S(2)}, u32[]{:S(2)}) %collective-permute-start.1) | collective-permute-done | bytes 139296 | tf_op jit(solution)/shard_map/ppermute | solution.py:164
  15.5 1.8 %collective-permute-start.2 = (f32[4,8,1088]{2,1,0:T(8,128)S(1)}, f32[4,8,1088]{2,1,0:T(8,128)S(1)}, u32[]{:S(2)}, u32[]{:S(2)}) collective-permute-start(f32[4,8,1088]{2,1,0:T(8,128)S(1)} %add.22), channel_id=1, source_target_pairs={{0,16},{4,20},{8,24},{12,28},{16,0},{20,4},{24,8},{28,12},{1,17},{... | collective-permute-start | bytes 417800 | tf_op jit(solution)/shard_map/ppermute | solution.py:164
  17.3 3.5 %collective-permute-done.2 = f32[4,8,1088]{2,1,0:T(8,128)S(1)} collective-permute-done((f32[4,8,1088]{2,1,0:T(8,128)S(1)}, f32[4,8,1088]{2,1,0:T(8,128)S(1)}, u32[]{:S(2)}, u32[]{:S(2)}) %collective-permute-start.2) | collective-permute-done | bytes 139296 | tf_op jit(solution)/shard_map/ppermute | solution.py:164
  20.9 1.7 %collective-permute-start.3 = (f32[4,8,1088]{2,1,0:T(8,128)S(1)}, f32[4,8,1088]{2,1,0:T(8,128)S(1)}, u32[]{:S(2)}, u32[]{:S(2)}) collective-permute-start(f32[4,8,1088]{2,1,0:T(8,128)S(1)} %add.23), channel_id=1, source_target_pairs={{0,1},{1,0},{2,3},{3,2},{4,5},{5,4},{6,7},{7,6},{8,9},{9,8},{10,11... | collective-permute-start | bytes 417800 | tf_op jit(solution)/shard_map/ppermute | solution.py:164
  22.6 0.0 copy-done.1
  22.6 1.5 %collective-permute-start.5 = (f32[1,8,1088]{2,1,0:T(8,128)S(1)}, f32[1,8,1088]{2,1,0:T(8,128)S(1)}, u32[]{:S(2)}, u32[]{:S(2)}) collective-permute-start(f32[1,8,1088]{2,1,0:T(8,128)S(1)} %bitcast.15), channel_id=1, source_target_pairs={{0,8},{4,12},{8,0},{12,4},{16,24},{20,28},{24,16},{28,20},{1,9},{5... | collective-permute-start | bytes 104456 | tf_op jit(solution)/shard_map/ppermute | solution.py:164
  24.1 2.0 %collective-permute-done.3 = f32[4,8,1088]{2,1,0:T(8,128)S(1)} collective-permute-done((f32[4,8,1088]{2,1,0:T(8,128)S(1)}, f32[4,8,1088]{2,1,0:T(8,128)S(1)}, u32[]{:S(2)}, u32[]{:S(2)}) %collective-permute-start.3) | collective-permute-done | bytes 139296 | tf_op jit(solution)/shard_map/ppermute | solution.py:164
  26.1 3.2 %collective-permute-start.4 = (f32[4,8,1088]{2,1,0:T(8,128)S(1)}, f32[4,8,1088]{2,1,0:T(8,128)S(1)}, u32[]{:S(2)}, u32[]{:S(2)}) collective-permute-start(f32[4,8,1088]{2,1,0:T(8,128)S(1)} %add.24), channel_id=1, source_target_pairs={{0,2},{1,3},{2,0},{3,1},{4,6},{5,7},{6,4},{7,5},{8,10},{9,11},{10,... | collective-permute-start | bytes 417800 | tf_op jit(solution)/shard_map/ppermute | solution.py:164
  29.3 0.0 collective-permute-done.5
  29.3 1.6 %collective-permute-start.6 = (f32[2,8,1088]{2,1,0:T(8,128)S(1)}, f32[2,8,1088]{2,1,0:T(8,128)S(1)}, u32[]{:S(2)}, u32[]{:S(2)}) collective-permute-start(f32[2,8,1088]{2,1,0:T(8,128)S(1)} %pad_maximum_fusion.2), channel_id=1, source_target_pairs={{0,16},{4,20},{8,24},{12,28},{16,0},{20,4},{24,8},{28,12},{1,17},{... | collective-permute-start | bytes 208904 | tf_op jit(solution)/shard_map/ppermute | solution.py:164
  30.9 3.1 %collective-permute-done.4 = f32[4,8,1088]{2,1,0:T(8,128)S(1)} collective-permute-done((f32[4,8,1088]{2,1,0:T(8,128)S(1)}, f32[4,8,1088]{2,1,0:T(8,128)S(1)}, u32[]{:S(2)}, u32[]{:S(2)}) %collective-permute-start.4) | collective-permute-done | bytes 139296 | tf_op jit(solution)/shard_map/ppermute | solution.py:164
  34.0 0.0 copy-start
  34.0 0.0 collective-permute-done.6
  34.1 0.1 collective-permute-start.7
  34.1 0.6 %pad_add_fusion.place_ref = s32[2]{0:T(128)} fusion(s32[1]{0:T(128)} %bitcast.6, s32[1]{0:T(128)} %bitcast.core_ref), kind=kLoop, calls=%fused_computation.3 | loop fusion | flops 2 | bytes 16 | tf_op jit(solution)/shard_map/stack | solution.py:258
  34.8 4.1 %input_grad.1 = bf16[2240,256]{1,0:T(8,128)(2,1)} custom-call(bf16[2240,64]{1,0:T(8,128)(2,1)} %get-tuple-element.8.back_ref, bf16[2240,256]{1,0:T(8,128)(2,1)} %bitcast.11, f32[64,1088]{1,0:T(8,128)} %params_ref.3), custom_call_target="tpu_custom_call" | custom-call | flops 73400320 | bytes 2580480 | tf_op jit(solution)/shard_map/input_grad/pallas_call | solution.py:222
  38.9 0.0 copy-done
  38.9 0.7 %pad_maximum_fusion.1.own_velocity_ref = f32[4,8,1088]{2,1,0:T(8,128)} fusion(f32[2,8,1088]{2,1,0:T(8,128)S(1)} %collective-permute-done.6, f32[1,8,1088]{2,1,0:T(8,128)S(1)} %collective-permute-done.5, f32[1,8,1088]{2,1,0:T(8,128)S(1)} %bitcast.18), kind=kLoop, calls=%fused_computation.1 | loop fusion | flops 69632 | bytes 278528 | tf_op jit(solution)/shard_map/concatenate | solution.py:243
  39.6 0.0 collective-permute-done.7
  39.6 0.7 %fusion = (f32[4,8,1088]{2,1,0:T(8,128)}, f32[4,8,1088]{2,1,0:T(8,128)}) fusion(f32[8,8,1088]{2,1,0:T(8,128)S(1)} %collective-permute-done.7), kind=kLoop, calls=%fused_computation.4 | loop fusion | bytes 557056 | tf_op jit(solution)/shard_map/slice | solution.py:262
  40.3 2.2 %update.1 = (f32[8,1088]{1,0:T(8,128)}, f32[8,8,1088]{2,1,0:T(8,128)}) custom-call(s32[2]{0:T(128)} %pad_add_fusion.place_ref, f32[4,8,1088]{2,1,0:T(8,128)} %copy-done, f32[4,8,1088]{2,1,0:T(8,128)} %get-tuple-element.14.other_ref, f32[4,8,1088]{2,1,0:T(8,128)} %pad_maximum_fusion.1.own_velocity_ref, f32[4,8,1088]{2,1,0:T(8,128)} %get-tuple-element.13.other_velocity_ref, ...), custom_call_target="tpu_custom_call" | custom-call | tf_op jit(solution)/shard_map/update/pallas_call | solution.py:248
  (6 shorter events, 0.1 us)
Async XLA Ops:
  5.7 16.9 %copy-start.1 = (f32[8,1088]{1,0:T(8,128)S(1)}, f32[8,1088]{1,0:T(8,128)}, u32[]{:S(2)}) copy-start(f32[8,1088]{1,0:T(8,128)} %param.11) | copy-start | bytes 104452
  5.7 1.7 %collective-permute-start = (f32[4,8,1088]{2,1,0:T(8,128)}, f32[4,8,1088]{2,1,0:T(8,128)S(1)}, u32[]{:S(2)}, u32[]{:S(2)}) collective-permute-start(f32[4,8,1088]{2,1,0:T(8,128)} %get-tuple-element.10), channel_id=1, source_target_pairs={{0,4},{4,0},{8,12},{12,8},{16,20},{20,16},{24,28},{28,24},{1,5},{5... | collective-permute-start | bytes 417800 | tf_op jit(solution)/shard_map/ppermute | solution.py:164
  8.4 7.1 %collective-permute-start.1 = (f32[4,8,1088]{2,1,0:T(8,128)S(1)}, f32[4,8,1088]{2,1,0:T(8,128)S(1)}, u32[]{:S(2)}, u32[]{:S(2)}) collective-permute-start(f32[4,8,1088]{2,1,0:T(8,128)S(1)} %add.21), channel_id=1, source_target_pairs={{0,8},{4,12},{8,0},{12,4},{16,24},{20,28},{24,16},{28,20},{1,9},{5... | collective-permute-start | bytes 417800 | tf_op jit(solution)/shard_map/ppermute | solution.py:164
  15.5 5.4 %collective-permute-start.2 = (f32[4,8,1088]{2,1,0:T(8,128)S(1)}, f32[4,8,1088]{2,1,0:T(8,128)S(1)}, u32[]{:S(2)}, u32[]{:S(2)}) collective-permute-start(f32[4,8,1088]{2,1,0:T(8,128)S(1)} %add.22), channel_id=1, source_target_pairs={{0,16},{4,20},{8,24},{12,28},{16,0},{20,4},{24,8},{28,12},{1,17},{... | collective-permute-start | bytes 417800 | tf_op jit(solution)/shard_map/ppermute | solution.py:164
  20.9 5.2 %collective-permute-start.3 = (f32[4,8,1088]{2,1,0:T(8,128)S(1)}, f32[4,8,1088]{2,1,0:T(8,128)S(1)}, u32[]{:S(2)}, u32[]{:S(2)}) collective-permute-start(f32[4,8,1088]{2,1,0:T(8,128)S(1)} %add.23), channel_id=1, source_target_pairs={{0,1},{1,0},{2,3},{3,2},{4,5},{5,4},{6,7},{7,6},{8,9},{9,8},{10,11... | collective-permute-start | bytes 417800 | tf_op jit(solution)/shard_map/ppermute | solution.py:164
  22.6 6.7 %collective-permute-start.5 = (f32[1,8,1088]{2,1,0:T(8,128)S(1)}, f32[1,8,1088]{2,1,0:T(8,128)S(1)}, u32[]{:S(2)}, u32[]{:S(2)}) collective-permute-start(f32[1,8,1088]{2,1,0:T(8,128)S(1)} %bitcast.15), channel_id=1, source_target_pairs={{0,8},{4,12},{8,0},{12,4},{16,24},{20,28},{24,16},{28,20},{1,9},{5... | collective-permute-start | bytes 104456 | tf_op jit(solution)/shard_map/ppermute | solution.py:164
  26.1 7.9 %collective-permute-start.4 = (f32[4,8,1088]{2,1,0:T(8,128)S(1)}, f32[4,8,1088]{2,1,0:T(8,128)S(1)}, u32[]{:S(2)}, u32[]{:S(2)}) collective-permute-start(f32[4,8,1088]{2,1,0:T(8,128)S(1)} %add.24), channel_id=1, source_target_pairs={{0,2},{1,3},{2,0},{3,1},{4,6},{5,7},{6,4},{7,5},{8,10},{9,11},{10,... | collective-permute-start | bytes 417800 | tf_op jit(solution)/shard_map/ppermute | solution.py:164
  29.3 4.7 %collective-permute-start.6 = (f32[2,8,1088]{2,1,0:T(8,128)S(1)}, f32[2,8,1088]{2,1,0:T(8,128)S(1)}, u32[]{:S(2)}, u32[]{:S(2)}) collective-permute-start(f32[2,8,1088]{2,1,0:T(8,128)S(1)} %pad_maximum_fusion.2), channel_id=1, source_target_pairs={{0,16},{4,20},{8,24},{12,28},{16,0},{20,4},{24,8},{28,12},{1,17},{... | collective-permute-start | bytes 208904 | tf_op jit(solution)/shard_map/ppermute | solution.py:164
  34.0 4.9 %copy-start = (f32[4,8,1088]{2,1,0:T(8,128)}, f32[4,8,1088]{2,1,0:T(8,128)S(1)}, u32[]{:S(2)}) copy-start(f32[4,8,1088]{2,1,0:T(8,128)S(1)} %add.25.own_ref) | copy-start | bytes 417796
  34.1 5.5 %collective-permute-start.7 = (f32[8,8,1088]{2,1,0:T(8,128)S(1)}, f32[8,8,1088]{2,1,0:T(8,128)S(1)}, u32[]{:S(2)}, u32[]{:S(2)}) collective-permute-start(f32[8,8,1088]{2,1,0:T(8,128)S(1)} %pad_maximum_fusion), channel_id=1, source_target_pairs={{0,4},{4,0},{8,12},{12,8},{16,20},{20,16},{24,28},{28,24},{1,5},{5... | collective-permute-start | bytes 835592 | tf_op jit(solution)/shard_map/ppermute | solution.py:164

commit v2 on v1

--- a/solution.py
+++ b/solution.py
@@ -30,7 +30,7 @@
 
 
 def grad_kernel(
-    core_ref, x_ref, first_ref, second_ref, out_ref, params_ref,
+    place_ref, x_ref, first_ref, second_ref, out_ref, params_ref,
     keep_ref, send_ref, back_ref,
     first_px, second_px, bs_px, spread_px, bs_cols, first_rows, second_bf, taps_ref,
     *, height, width, strips, rows,
@@ -111,13 +111,14 @@
 
     for own in range(2):
 
-        @pl.when(core_ref[0] == own)
+        @pl.when(place_ref[0] % 2 == own)
         def _():
             put(keep_ref, own)
             put(send_ref, 1 - own)
 
 
-def input_grad_kernel(back_ref, out_ref, params_ref, result_ref):
+def input_grad_kernel(back_ref, out_ref, params_ref, *rest):
+    result_ref = rest[-1]
     c_in = out_ref.shape[1]
     w_first = params_ref[:, :c_in].astype(BF16)
     change = jnp.dot(back_ref[...], w_first, preferred_element_type=F32)
@@ -125,11 +126,11 @@
 
 
 def update_kernel(
-    place_ref, own_ref, other_ref, own_velocity_ref, other_velocity_ref, params_ref,
+    place_ref, own_ref, other_ref, own_speed_ref, other_speed_ref, params_ref,
     velocity_ref, weights_ref, *, c_in, mid,
 ):
-    core = place_ref[0]
-    pair = place_ref[1]
+    core = place_ref[0] % 2
+    pair = place_ref[0] // 2
     halves, rows, width = own_ref.shape
     lane = lax.broadcasted_iota(jnp.int32, (1, 1, width), 2)
     edges = (0, c_in, c_in + 9 * mid, width)
@@ -150,30 +151,46 @@
         factor = jnp.where(inside, learn_rate * trust, factor)
     factor = factor[0]
     for k in range(halves):
-        for parity, grad, speed in ((core, own_ref, own_velocity_ref), (1 - core, other_ref, other_velocity_ref)):
+        for parity, grad, speed in ((core, own_ref, own_speed_ref), (1 - core, other_ref, other_speed_ref)):
             tile = 2 * k + parity
             weights_ref[tile] = params_ref[tile] - (momentum * speed[k ^ pair] + factor * grad[k])
-    velocity_ref[...] = momentum * own_velocity_ref[0] + factor * own_ref[pair]
+    velocity_ref[...] = momentum * own_speed_ref[0] + factor * own_ref[pair]
 
 
 def full_vmem(count):
     return [pl.BlockSpec(memory_space=pltpu.VMEM) for _ in range(count)]
 
 
+def in_vmem(*arrays):
+    return [pltpu.with_memory_space_constraint(a, pltpu.VMEM) for a in arrays]
+
+
 def flip(value, axis, bit):
     return lax.ppermute(value, axis, [(i, i ^ bit) for i in range(lax.axis_size(axis))])
 
 
-def sum_over(value, axis):
-    size = lax.axis_size(axis)
+def exchange_steps(group, depth):
+    across = [(0, 1 << b) for b in range(1, group.bit_length() - 1)]
+    along = []
     bit = 1
-    while size % (2 * bit) == 0:
-        value = value + flip(value, axis, bit)
+    while depth % (2 * bit) == 0:
+        along.append((1, bit))
         bit *= 2
-    terms = [value]
-    for turn in range(1, size // bit):
-        terms.append(lax.ppermute(value, axis, [(i, (i + turn * bit) % size) for i in range(size)]))
-    return sum(terms[1:], terms[0])
+    steps = []
+    for one, two in zip(across, along):
+        steps += [(one, two), (two, one)]
+    common = min(len(across), len(along))
+    steps += [(one, one) for one in across[common:] + along[common:]]
+    pairs = []
+    for step in steps:
+        table = []
+        for g in range(group):
+            for z in range(depth):
+                axis, flipped = step[g % 2]
+                to_g, to_z = (g ^ flipped, z) if axis == 0 else (g, z ^ flipped)
+                table.append((g * depth + z, to_g * depth + to_z))
+        pairs.append(table)
+    return pairs, bit
 
 
 def shards(block_input, mid_first, mid_second, out_grad, params, velocity):
@@ -181,21 +198,17 @@
     mid, row = params.shape
     pixels = height * width
     group = lax.axis_size("gx")
+    depth = lax.axis_size("gy")
     rows = mid // group
     halves = group // 2
-    strips = group * lax.axis_size("gy")
-    place = lax.axis_index("gx")
-    core = place % 2
-    pair = place // 2
+    strips = group * depth
+    place = lax.axis_index("gx").reshape(1)
     out_flat = out_grad.reshape(pixels, c_in)
+    half = pltpu.VMEM((halves, rows, row), F32)
 
     keep, send, back_first = pl.pallas_call(
         functools.partial(grad_kernel, height=height, width=width, strips=strips, rows=rows),
-        out_shape=(
-            jax.ShapeDtypeStruct((halves, rows, row), F32),
-            jax.ShapeDtypeStruct((halves, rows, row), F32),
-            jax.ShapeDtypeStruct((pixels, mid), BF16),
-        ),
+        out_shape=(half, half, pltpu.VMEM((pixels, mid), BF16)),
         in_specs=[pl.BlockSpec(memory_space=pltpu.SMEM)] + full_vmem(5),
         out_specs=tuple(full_vmem(3)),
         scratch_shapes=[
@@ -210,7 +223,7 @@
         ],
         name="grads",
     )(
-        core.reshape(1),
+        place,
         block_input.reshape(pixels, c_in),
         mid_first.reshape(height, width * mid),
         mid_second.reshape(height, width * mid),
@@ -218,32 +231,52 @@
         params,
     )
 
-    block = pixels // 4
-    input_grad = pl.pallas_call(
-        input_grad_kernel,
-        out_shape=jax.ShapeDtypeStruct((pixels, c_in), BF16),
-        grid=(pixels // block,),
-        in_specs=[
-            pl.BlockSpec((block, mid), lambda i: (i, 0)),
-            pl.BlockSpec((block, c_in), lambda i: (i, 0)),
-            pl.BlockSpec((mid, row), lambda i: (0, 0)),
-        ],
-        out_specs=pl.BlockSpec((block, c_in), lambda i: (i, 0)),
-        cost_estimate=pl.CostEstimate(
-            flops=2 * pixels * mid * c_in, bytes_accessed=2 * pixels * (2 * c_in + mid), transcendentals=0
-        ),
-        name="input_grad",
-    )(back_first, out_flat, params)
+    pieces = 2
+    block = pixels // (2 * pieces)
+
+    def input_grad_piece(piece, earlier):
+        first = 2 * piece
+        operands = [back_first, out_flat, params] + ([] if earlier is None else [earlier])
+        return pl.pallas_call(
+            input_grad_kernel,
+            out_shape=jax.ShapeDtypeStruct((pixels, c_in), BF16),
+            grid=(2,),
+            in_specs=[
+                pl.BlockSpec((block, mid), lambda i: (first + i, 0)),
+                pl.BlockSpec((block, c_in), lambda i: (first + i, 0)),
+                pl.BlockSpec((mid, row), lambda i: (0, 0)),
+                pl.BlockSpec(memory_space=pl.ANY),
+            ][: len(operands)],
+            out_specs=pl.BlockSpec((block, c_in), lambda i: (first + i, 0)),
+            input_output_aliases={} if earlier is None else {3: 0},
+            cost_estimate=pl.CostEstimate(
+                flops=2 * pixels * mid * c_in // pieces,
+                bytes_accessed=2 * pixels * (2 * c_in + mid) // pieces,
+                transcendentals=0,
+            ),
+            name="input_grad",
+        )(*operands)
 
     total = keep + flip(send, "gx", 1)
     speeds = velocity.reshape(1, rows, row)
     bit = 2
     while bit < group:
-        total = total + flip(total, "gx", bit)
         speeds = jnp.concatenate([speeds, flip(speeds, "gx", bit)], axis=0)
         bit *= 2
-    total = sum_over(total, "gy")
-    both = flip(jnp.concatenate([total, speeds], axis=0), "gx", 1)
+    other_speeds = flip(speeds, "gx", 1)
+    input_grad = None
+    steps, bit = exchange_steps(group, depth)
+    for number, table in enumerate(steps):
+        total = total + lax.ppermute(total, ("gx", "gy"), table)
+        if number < pieces:
+            input_grad = input_grad_piece(number, input_grad)
+            total, input_grad = lax.optimization_barrier((total, input_grad))
+    turned = [
+        lax.ppermute(total, "gy", [(i, (i + turn * bit) % depth) for i in range(depth)])
+        for turn in range(1, depth // bit)
+    ]
+    total = sum(turned, total)
+    other = flip(total, "gx", 1)
 
     new_velocity, next_weights = pl.pallas_call(
         functools.partial(update_kernel, c_in=c_in, mid=mid),
@@ -254,14 +287,7 @@
         in_specs=[pl.BlockSpec(memory_space=pltpu.SMEM)] + full_vmem(5),
         out_specs=tuple(full_vmem(2)),
         name="update",
-    )(
-        jnp.stack([core, pair]),
-        total,
-        both[:halves],
-        speeds,
-        both[halves:],
-        params.reshape(group, rows, row),
-    )
+    )(place, *in_vmem(total, other, speeds, other_speeds, params.reshape(group, rows, row)))
     return (input_grad.reshape(1, height, width, c_in), new_velocity, next_weights.reshape(mid, row))
 
 

time: 42.7 us -> 34.8 us (0.81)
  waiting for transfers between devices: 14 us -> 11.4 us
  other arithmetic: 2.35 us -> 0.12 us
  Pallas kernels: 11.4 us -> 9.73 us
  starting transfers between devices: 13.3 us -> 11.9 us
    ppermute x8 -> x5, waiting for transfers between devices: 14 us -> 2.36 us  [flip(): lax.ppermute(value, axis, [(i, i ^ bit) for i in range(lax.axis_size(axis...]
    ppermute x8 -> x5, starting transfers between devices: 13.3 us -> 2.68 us  [flip(): lax.ppermute(value, axis, [(i, i ^ bit) for i in range(lax.axis_size(axis...]
    ppermute x0 -> x4, starting transfers between devices: none -> 9.21 us  [shards(): total = total + lax.ppermute(total, ('gx', 'gy'), table)]
    ppermute x0 -> x4, waiting for transfers between devices: none -> 9.01 us  [shards(): total = total + lax.ppermute(total, ('gx', 'gy'), table)]
    pallas_call x1, Pallas kernels: 2.18 us -> 0.91 us  [shards(): pl.pallas_call(functools.partial(update_kernel, c_in=c_in, mid=mid), out_...]
    add x1, other arithmetic: 0.93 us -> 0.02 us  [shards(): total = keep + flip(send, 'gx', 1)]
    pallas_call x1, Pallas kernels: 5.1 us -> 4.2 us  [shards(): pl.pallas_call(functools.partial(grad_kernel, height=height, width=width,...]
    unnamed x4 -> x6, local copies, waits for them, and re-layouts: 0.01 us -> 0.81 us
  transfers between devices with their start and end apart: 8 -> 9, of which waited for: 5 -> 5; matrix products, arithmetic and copies ran while one was open for 3% -> 0% of each run, Pallas kernels for 10% -> 13%
where the time goes in v2:
time: 34.8 us; the launch traced here: 34.6 us
  starting transfers between devices  11.9 us (34%)
  waiting for transfers between devices  11.4 us (33%)
  Pallas kernels  9.73 us (28%)
  local copies, waits for them, and re-layouts  0.81 us (2%)
  between operations  0.71 us (2%)
    ppermute x4, starting transfers between devices, shards(): total = total + lax.ppermute(total, ('gx', 'gy'), table)  9.21 us
    ppermute x4, waiting for transfers between devices, shards(): total = total + lax.ppermute(total, ('gx', 'gy'), table)  9.01 us
    pallas_call x2, Pallas kernels, input_grad_piece(): pl.pallas_call(input_grad_kernel, out_shape=jax.ShapeDtypeStruct((pixels,...  4.61 us
    pallas_call x1, Pallas kernels, shards(): pl.pallas_call(functools.partial(grad_kernel, height=height, width=width,...  4.2 us
    ppermute x5, starting transfers between devices, flip(): lax.ppermute(value, axis, [(i, i ^ bit) for i in range(lax.axis_size(axis...  2.68 us
    ppermute x5, waiting for transfers between devices, flip(): lax.ppermute(value, axis, [(i, i ^ bit) for i in range(lax.axis_size(axis...  2.36 us
    pallas_call x1, Pallas kernels, shards(): pl.pallas_call(functools.partial(update_kernel, c_in=c_in, mid=mid), out_...  0.91 us
    unnamed x6, local copies, waits for them, and re-layouts  0.81 us
  transfers between devices with their start and end apart: 9, of which 5 were waited for; matrix products, arithmetic and copies ran while one was open for 0% of the time, Pallas kernels for 13%

profile of v2, /device:TPU:0, one launch (start us, length us, event | category | flops | bytes accessed | tf_op | source)
XLA Modules:
  0.0 34.6 jit_solution(7800839229169726144)
XLA Ops:
  0.6 4.2 %grads.1 = (f32[4,8,1088]{2,1,0:T(8,128)S(1)}, f32[4,8,1088]{2,1,0:T(8,128)S(1)}, bf16[2240,64]{1,0:T(8,128)(2,1)S(1)}) custom-call(s32[1]{0:T(128)} %bitcast.place_ref, bf16[2240,256]{1,0:T(8,128)(2,1)} %bitcast.14, bf16[40,3584]{1,0:T(8,128)(2,1)} %bitcast.15, bf16[40,3584]{1,0:T(8,128)(2,1)} %bitcast.16, bf16[2240,256]{1,0:T(8,128)(2,1)} %bitcast.10, ...), custom_call_target="tpu_custom_call" | custom-call | tf_op jit(solution)/shard_map/grads/pallas_call | solution.py:209
  4.8 0.0 copy-start.1
  4.9 0.8 %copy-done.1 = bf16[2240,64]{1,0:T(8,128)(2,1)} copy-done((bf16[2240,64]{1,0:T(8,128)(2,1)}, bf16[2240,64]{1,0:T(8,128)(2,1)S(1)}, u32[]{:S(2)}) %copy-start.1) | copy-done | bytes 286744
  5.7 0.5 %collective-permute-start = (f32[4,8,1088]{2,1,0:T(8,128)S(1)}, f32[4,8,1088]{2,1,0:T(8,128)S(1)}, u32[]{:S(2)}, u32[]{:S(2)}) collective-permute-start(f32[4,8,1088]{2,1,0:T(8,128)S(1)} %get-tuple-element.13), channel_id=1, source_target_pairs={{0,4},{4,0},{8,12},{12,8},{16,20},{20,16},{24,28},{28,24},{1,5},{5... | collective-permute-start | bytes 417800 | tf_op jit(solution)/shard_map/ppermute | solution.py:169
  6.2 1.0 %collective-permute-done = f32[4,8,1088]{2,1,0:T(8,128)S(1)} collective-permute-done((f32[4,8,1088]{2,1,0:T(8,128)S(1)}, f32[4,8,1088]{2,1,0:T(8,128)S(1)}, u32[]{:S(2)}, u32[]{:S(2)}) %collective-permute-start) | collective-permute-done | bytes 139296 | tf_op jit(solution)/shard_map/ppermute | solution.py:169
  7.2 2.9 %collective-permute-start.1 = (f32[4,8,1088]{2,1,0:T(8,128)S(1)}, f32[4,8,1088]{2,1,0:T(8,128)S(1)}, u32[]{:S(2)}, u32[]{:S(2)}) collective-permute-start(f32[4,8,1088]{2,1,0:T(8,128)S(1)} %add.15), channel_id=1, source_target_pairs={{0,8},{1,9},{2,10},{3,11},{4,5},{5,4},{6,7},{7,6},{8,0},{9,1},{10,... | collective-permute-start | bytes 417800 | tf_op jit(solution)/shard_map/ppermute | solution.py:270
  10.1 0.0 copy-start.2
  10.1 2.3 %input_grad.2.rest_0_ = bf16[2240,256]{1,0:T(8,128)(2,1)} custom-call(bf16[2240,64]{1,0:T(8,128)(2,1)} %copy-done.1, bf16[2240,256]{1,0:T(8,128)(2,1)} %bitcast.11, f32[64,1088]{1,0:T(8,128)} %params_ref.5), custom_call_target="tpu_custom_call" | custom-call | flops 36700160 | bytes 1290240 | tf_op jit(solution)/shard_map/input_grad/pallas_call | solution.py:240
  12.4 0.8 %collective-permute-done.1 = f32[4,8,1088]{2,1,0:T(8,128)S(1)} collective-permute-done((f32[4,8,1088]{2,1,0:T(8,128)S(1)}, f32[4,8,1088]{2,1,0:T(8,128)S(1)}, u32[]{:S(2)}, u32[]{:S(2)}) %collective-permute-start.1) | collective-permute-done | bytes 139296 | tf_op jit(solution)/shard_map/ppermute | solution.py:270
  13.2 2.2 %collective-permute-start.2 = (f32[4,8,1088]{2,1,0:T(8,128)S(1)}, f32[4,8,1088]{2,1,0:T(8,128)S(1)}, u32[]{:S(2)}, u32[]{:S(2)}) collective-permute-start(f32[4,8,1088]{2,1,0:T(8,128)S(1)} %add.16), channel_id=1, source_target_pairs={{0,1},{1,0},{2,3},{3,2},{4,12},{5,13},{6,14},{7,15},{8,9},{9,8},{1... | collective-permute-start | bytes 417800 | tf_op jit(solution)/shard_map/ppermute | solution.py:270
  15.4 0.0 copy-done.2
  15.4 1.5 %collective-permute-start.6 = (f32[1,8,1088]{2,1,0:T(8,128)S(1)}, f32[1,8,1088]{2,1,0:T(8,128)S(1)}, u32[]{:S(2)}, u32[]{:S(2)}) collective-permute-start(f32[1,8,1088]{2,1,0:T(8,128)S(1)} %bitcast.17), channel_id=1, source_target_pairs={{0,8},{4,12},{8,0},{12,4},{16,24},{20,28},{24,16},{28,20},{1,9},{5... | collective-permute-start | bytes 104456 | tf_op jit(solution)/shard_map/ppermute | solution.py:169
  16.9 2.3 %input_grad.3 = bf16[2240,256]{1,0:T(8,128)(2,1)} custom-call(bf16[2240,64]{1,0:T(8,128)(2,1)} %copy-done.1, bf16[2240,256]{1,0:T(8,128)(2,1)} %bitcast.12, f32[64,1088]{1,0:T(8,128)} %params_ref.5, bf16[2240,256]{1,0:T(8,128)(2,1)} %input_grad.2.rest_0_), custom_call_target="tpu_custom_call", output_to_operand_aliasing={{}: (3, {})} | custom-call | flops 36700160 | bytes 1290240 | tf_op jit(solution)/shard_map/input_grad/pallas_call | solution.py:240
  19.2 0.0 copy-start
  19.2 0.0 collective-permute-done.2
  19.2 1.6 %collective-permute-start.3 = (f32[4,8,1088]{2,1,0:T(8,128)S(1)}, f32[4,8,1088]{2,1,0:T(8,128)S(1)}, u32[]{:S(2)}, u32[]{:S(2)}) collective-permute-start(f32[4,8,1088]{2,1,0:T(8,128)S(1)} %add.17), channel_id=1, source_target_pairs={{0,16},{1,17},{2,18},{3,19},{4,6},{5,7},{6,4},{7,5},{8,24},{9,25},... | collective-permute-start | bytes 417800 | tf_op jit(solution)/shard_map/ppermute | solution.py:270
  20.8 0.0 collective-permute-done.6
  20.8 0.6 %collective-permute-start.7 = (f32[2,8,1088]{2,1,0:T(8,128)S(1)}, f32[2,8,1088]{2,1,0:T(8,128)S(1)}, u32[]{:S(2)}, u32[]{:S(2)}) collective-permute-start(f32[2,8,1088]{2,1,0:T(8,128)S(1)} %pad_maximum_fusion.1), channel_id=1, source_target_pairs={{0,16},{4,20},{8,24},{12,28},{16,0},{20,4},{24,8},{28,12},{1,17},{... | collective-permute-start | bytes 208904 | tf_op jit(solution)/shard_map/ppermute | solution.py:169
  21.4 3.2 %collective-permute-done.3 = f32[4,8,1088]{2,1,0:T(8,128)S(1)} collective-permute-done((f32[4,8,1088]{2,1,0:T(8,128)S(1)}, f32[4,8,1088]{2,1,0:T(8,128)S(1)}, u32[]{:S(2)}, u32[]{:S(2)}) %collective-permute-start.3) | collective-permute-done | bytes 139296 | tf_op jit(solution)/shard_map/ppermute | solution.py:270
  24.6 2.5 %collective-permute-start.4 = (f32[4,8,1088]{2,1,0:T(8,128)S(1)}, f32[4,8,1088]{2,1,0:T(8,128)S(1)}, u32[]{:S(2)}, u32[]{:S(2)}) collective-permute-start(f32[4,8,1088]{2,1,0:T(8,128)S(1)} %add.18), channel_id=1, source_target_pairs={{0,2},{1,3},{2,0},{3,1},{4,20},{5,21},{6,22},{7,23},{8,10},{9,11},... | collective-permute-start | bytes 417800 | tf_op jit(solution)/shard_map/ppermute | solution.py:270
  27.1 0.0 collective-permute-done.7
  27.1 0.1 collective-permute-start.8
  27.2 5.0 %collective-permute-done.4 = f32[4,8,1088]{2,1,0:T(8,128)S(1)} collective-permute-done((f32[4,8,1088]{2,1,0:T(8,128)S(1)}, f32[4,8,1088]{2,1,0:T(8,128)S(1)}, u32[]{:S(2)}, u32[]{:S(2)}) %collective-permute-start.4) | collective-permute-done | bytes 139296 | tf_op jit(solution)/shard_map/ppermute | solution.py:270
  32.3 0.1 collective-permute-start.5
  32.4 0.0 collective-permute-done.8.other_speed_ref
  32.4 1.3 %collective-permute-done.5.other_ref = f32[4,8,1088]{2,1,0:T(8,128)S(1)} collective-permute-done((f32[4,8,1088]{2,1,0:T(8,128)S(1)}, f32[4,8,1088]{2,1,0:T(8,128)S(1)}, u32[]{:S(2)}, u32[]{:S(2)}) %collective-permute-start.5) | collective-permute-done | bytes 139296 | tf_op jit(solution)/shard_map/ppermute | solution.py:169
  33.7 0.0 copy-done
  33.7 0.9 %update.1 = (f32[8,1088]{1,0:T(8,128)}, f32[8,8,1088]{2,1,0:T(8,128)}) custom-call(s32[1]{0:T(128)} %bitcast.place_ref, f32[4,8,1088]{2,1,0:T(8,128)S(1)} %add.19.own_ref, f32[4,8,1088]{2,1,0:T(8,128)S(1)} %collective-permute-done.5.other_ref, f32[4,8,1088]{2,1,0:T(8,128)S(1)} %pad_maximum_fusion.own_speed_ref, ...), custom_call_target="tpu_custom_call" | custom-call | tf_op jit(solution)/shard_map/update/pallas_call | solution.py:281
  (7 shorter events, 0.1 us)
Async XLA Ops:
  4.8 0.8 %copy-start.1 = (bf16[2240,64]{1,0:T(8,128)(2,1)}, bf16[2240,64]{1,0:T(8,128)(2,1)S(1)}, u32[]{:S(2)}) copy-start(bf16[2240,64]{1,0:T(8,128)(2,1)S(1)} %get-tuple-element.14.back_ref) | copy-start | bytes 860164
  5.7 1.5 %collective-permute-start = (f32[4,8,1088]{2,1,0:T(8,128)S(1)}, f32[4,8,1088]{2,1,0:T(8,128)S(1)}, u32[]{:S(2)}, u32[]{:S(2)}) collective-permute-start(f32[4,8,1088]{2,1,0:T(8,128)S(1)} %get-tuple-element.13), channel_id=1, source_target_pairs={{0,4},{4,0},{8,12},{12,8},{16,20},{20,16},{24,28},{28,24},{1,5},{5... | collective-permute-start | bytes 417800 | tf_op jit(solution)/shard_map/ppermute | solution.py:169
  7.2 6.0 %collective-permute-start.1 = (f32[4,8,1088]{2,1,0:T(8,128)S(1)}, f32[4,8,1088]{2,1,0:T(8,128)S(1)}, u32[]{:S(2)}, u32[]{:S(2)}) collective-permute-start(f32[4,8,1088]{2,1,0:T(8,128)S(1)} %add.15), channel_id=1, source_target_pairs={{0,8},{1,9},{2,10},{3,11},{4,5},{5,4},{6,7},{7,6},{8,0},{9,1},{10,... | collective-permute-start | bytes 417800 | tf_op jit(solution)/shard_map/ppermute | solution.py:270
  10.1 5.3 %copy-start.2 = (f32[8,1088]{1,0:T(8,128)S(1)}, f32[8,1088]{1,0:T(8,128)}, u32[]{:S(2)}) copy-start(f32[8,1088]{1,0:T(8,128)} %param.11) | copy-start | bytes 104452
  13.2 6.0 %collective-permute-start.2 = (f32[4,8,1088]{2,1,0:T(8,128)S(1)}, f32[4,8,1088]{2,1,0:T(8,128)S(1)}, u32[]{:S(2)}, u32[]{:S(2)}) collective-permute-start(f32[4,8,1088]{2,1,0:T(8,128)S(1)} %add.16), channel_id=1, source_target_pairs={{0,1},{1,0},{2,3},{3,2},{4,12},{5,13},{6,14},{7,15},{8,9},{9,8},{1... | collective-permute-start | bytes 417800 | tf_op jit(solution)/shard_map/ppermute | solution.py:270
  15.4 5.4 %collective-permute-start.6 = (f32[1,8,1088]{2,1,0:T(8,128)S(1)}, f32[1,8,1088]{2,1,0:T(8,128)S(1)}, u32[]{:S(2)}, u32[]{:S(2)}) collective-permute-start(f32[1,8,1088]{2,1,0:T(8,128)S(1)} %bitcast.17), channel_id=1, source_target_pairs={{0,8},{4,12},{8,0},{12,4},{16,24},{20,28},{24,16},{28,20},{1,9},{5... | collective-permute-start | bytes 104456 | tf_op jit(solution)/shard_map/ppermute | solution.py:169
  19.2 14.5 %copy-start = (f32[64,1088]{1,0:T(8,128)S(1)}, f32[64,1088]{1,0:T(8,128)}, u32[]{:S(2)}) copy-start(f32[64,1088]{1,0:T(8,128)} %params_ref.5) | copy-start | bytes 835588
  19.2 5.3 %collective-permute-start.3 = (f32[4,8,1088]{2,1,0:T(8,128)S(1)}, f32[4,8,1088]{2,1,0:T(8,128)S(1)}, u32[]{:S(2)}, u32[]{:S(2)}) collective-permute-start(f32[4,8,1088]{2,1,0:T(8,128)S(1)} %add.17), channel_id=1, source_target_pairs={{0,16},{1,17},{2,18},{3,19},{4,6},{5,7},{6,4},{7,5},{8,24},{9,25},... | collective-permute-start | bytes 417800 | tf_op jit(solution)/shard_map/ppermute | solution.py:270
  20.8 6.3 %collective-permute-start.7 = (f32[2,8,1088]{2,1,0:T(8,128)S(1)}, f32[2,8,1088]{2,1,0:T(8,128)S(1)}, u32[]{:S(2)}, u32[]{:S(2)}) collective-permute-start(f32[2,8,1088]{2,1,0:T(8,128)S(1)} %pad_maximum_fusion.1), channel_id=1, source_target_pairs={{0,16},{4,20},{8,24},{12,28},{16,0},{20,4},{24,8},{28,12},{1,17},{... | collective-permute-start | bytes 208904 | tf_op jit(solution)/shard_map/ppermute | solution.py:169
  24.6 7.7 %collective-permute-start.4 = (f32[4,8,1088]{2,1,0:T(8,128)S(1)}, f32[4,8,1088]{2,1,0:T(8,128)S(1)}, u32[]{:S(2)}, u32[]{:S(2)}) collective-permute-start(f32[4,8,1088]{2,1,0:T(8,128)S(1)} %add.18), channel_id=1, source_target_pairs={{0,2},{1,3},{2,0},{3,1},{4,20},{5,21},{6,22},{7,23},{8,10},{9,11},... | collective-permute-start | bytes 417800 | tf_op jit(solution)/shard_map/ppermute | solution.py:270
  27.1 5.2 %collective-permute-start.8 = (f32[4,8,1088]{2,1,0:T(8,128)S(1)}, f32[4,8,1088]{2,1,0:T(8,128)S(1)}, u32[]{:S(2)}, u32[]{:S(2)}) collective-permute-start(f32[4,8,1088]{2,1,0:T(8,128)S(1)} %pad_maximum_fusion.own_speed_ref), channel_id=1, source_target_pairs={{0,4},{4,0},{8,12},{12,8},{16,20},{20,16},{24,28},{28,24},{1,5},{5... | collective-permute-start | bytes 417800 | tf_op jit(solution)/shard_map/ppermute | solution.py:169
  32.3 1.4 %collective-permute-start.5 = (f32[4,8,1088]{2,1,0:T(8,128)S(1)}, f32[4,8,1088]{2,1,0:T(8,128)S(1)}, u32[]{:S(2)}, u32[]{:S(2)}) collective-permute-start(f32[4,8,1088]{2,1,0:T(8,128)S(1)} %add.19.own_ref), channel_id=1, source_target_pairs={{0,4},{4,0},{8,12},{12,8},{16,20},{20,16},{24,28},{28,24},{1,5},{5... | collective-permute-start | bytes 417800 | tf_op jit(solution)/shard_map/ppermute | solution.py:169

commit v3 on v2

--- a/solution.py
+++ b/solution.py
@@ -236,7 +236,7 @@
 
     def input_grad_piece(piece, earlier):
         first = 2 * piece
-        operands = [back_first, out_flat, params] + ([] if earlier is None else [earlier])
+        operands = [*in_vmem(back_first), out_flat, params] + ([] if earlier is None else [earlier])
         return pl.pallas_call(
             input_grad_kernel,
             out_shape=jax.ShapeDtypeStruct((pixels, c_in), BF16),
@@ -259,17 +259,17 @@
 
     total = keep + flip(send, "gx", 1)
     speeds = velocity.reshape(1, rows, row)
-    bit = 2
-    while bit < group:
-        speeds = jnp.concatenate([speeds, flip(speeds, "gx", bit)], axis=0)
-        bit *= 2
+    bit = group // 2
+    while bit > 1:
+        speeds = jnp.stack([speeds, flip(speeds, "gx", bit)], axis=1).reshape(-1, rows, row)
+        bit //= 2
     other_speeds = flip(speeds, "gx", 1)
     input_grad = None
     steps, bit = exchange_steps(group, depth)
     for number, table in enumerate(steps):
         total = total + lax.ppermute(total, ("gx", "gy"), table)
-        if number < pieces:
-            input_grad = input_grad_piece(number, input_grad)
+        if number in (0, len(steps) - 1):
+            input_grad = input_grad_piece(min(number, 1), input_grad)
             total, input_grad = lax.optimization_barrier((total, input_grad))
     turned = [
         lax.ppermute(total, "gy", [(i, (i + turn * bit) % depth) for i in range(depth)])

time: 34.8 us -> 33.4 us (0.960)
  waiting for transfers between devices: 11.4 us -> 8.81 us
  starting transfers between devices: 11.9 us -> 14 us
  local copies, waits for them, and re-layouts: 0.81 us -> 0.02 us
    ppermute x4, waiting for transfers between devices: 9.01 us -> 6.44 us  [shards(): total = total + lax.ppermute(total, ('gx', 'gy'), table)]
    ppermute x5, starting transfers between devices: 2.68 us -> 3.79 us  [flip(): lax.ppermute(value, axis, [(i, i ^ bit) for i in range(lax.axis_size(axis...]
    ppermute x4, starting transfers between devices: 9.21 us -> 10.2 us  [shards(): total = total + lax.ppermute(total, ('gx', 'gy'), table)]
    unnamed x6 -> x4, local copies, waits for them, and re-layouts: 0.81 us -> 0.01 us
  transfers between devices with their start and end apart: 9 -> 9, of which waited for: 5 -> 6; matrix products, arithmetic and copies ran while one was open for 0% -> 0% of each run, Pallas kernels for 13% -> 13%
where the time goes in v3:
time: 33.4 us; the launch traced here: 33.2 us
  starting transfers between devices  14 us (42%)
  Pallas kernels  9.56 us (29%)
  waiting for transfers between devices  8.81 us (26%)
  between operations  0.72 us (2%)
    ppermute x4, starting transfers between devices, shards(): total = total + lax.ppermute(total, ('gx', 'gy'), table)  10.2 us
    ppermute x4, waiting for transfers between devices, shards(): total = total + lax.ppermute(total, ('gx', 'gy'), table)  6.44 us
    pallas_call x2, Pallas kernels, input_grad_piece(): pl.pallas_call(input_grad_kernel, out_shape=jax.ShapeDtypeStruct((pixels,...  4.45 us
    pallas_call x1, Pallas kernels, shards(): pl.pallas_call(functools.partial(grad_kernel, height=height, width=width,...  4.2 us
    ppermute x5, starting transfers between devices, flip(): lax.ppermute(value, axis, [(i, i ^ bit) for i in range(lax.axis_size(axis...  3.79 us
    ppermute x5, waiting for transfers between devices, flip(): lax.ppermute(value, axis, [(i, i ^ bit) for i in range(lax.axis_size(axis...  2.36 us
    pallas_call x1, Pallas kernels, shards(): pl.pallas_call(functools.partial(update_kernel, c_in=c_in, mid=mid), out_...  0.91 us
  transfers between devices with their start and end apart: 9, of which 6 were waited for; matrix products, arithmetic and copies ran while one was open for 0% of the time, Pallas kernels for 13%

profile of v3, /device:TPU:0, one launch (start us, length us, event | category | flops | bytes accessed | tf_op | source)
XLA Modules:
  0.0 33.2 jit_solution(11155127023048006953)
XLA Ops:
  0.6 4.2 %grads.1 = (f32[4,8,1088]{2,1,0:T(8,128)S(1)}, f32[4,8,1088]{2,1,0:T(8,128)S(1)}, bf16[2240,64]{1,0:T(8,128)(2,1)S(1)}) custom-call(s32[1]{0:T(128)} %bitcast.place_ref, bf16[2240,256]{1,0:T(8,128)(2,1)} %bitcast.24, bf16[40,3584]{1,0:T(8,128)(2,1)} %bitcast.25, bf16[40,3584]{1,0:T(8,128)(2,1)} %bitcast.26, bf16[2240,256]{1,0:T(8,128)(2,1)} %bitcast.20, ...), custom_call_target="tpu_custom_call" | custom-call | tf_op jit(solution)/shard_map/grads/pallas_call | solution.py:209
  4.8 0.6 %collective-permute-start = (f32[4,8,1088]{2,1,0:T(8,128)S(1)}, f32[4,8,1088]{2,1,0:T(8,128)S(1)}, u32[]{:S(2)}, u32[]{:S(2)}) collective-permute-start(f32[4,8,1088]{2,1,0:T(8,128)S(1)} %get-tuple-element.13), channel_id=1, source_target_pairs={{0,4},{4,0},{8,12},{12,8},{16,20},{20,16},{24,28},{28,24},{1,5},{5... | collective-permute-start | bytes 417800 | tf_op jit(solution)/shard_map/ppermute | solution.py:169
  5.4 1.0 %collective-permute-done = f32[4,8,1088]{2,1,0:T(8,128)S(1)} collective-permute-done((f32[4,8,1088]{2,1,0:T(8,128)S(1)}, f32[4,8,1088]{2,1,0:T(8,128)S(1)}, u32[]{:S(2)}, u32[]{:S(2)}) %collective-permute-start) | collective-permute-done | bytes 139296 | tf_op jit(solution)/shard_map/ppermute | solution.py:169
  6.4 2.9 %collective-permute-start.1 = (f32[4,8,1088]{2,1,0:T(8,128)S(1)}, f32[4,8,1088]{2,1,0:T(8,128)S(1)}, u32[]{:S(2)}, u32[]{:S(2)}) collective-permute-start(f32[4,8,1088]{2,1,0:T(8,128)S(1)} %add.15), channel_id=1, source_target_pairs={{0,8},{1,9},{2,10},{3,11},{4,5},{5,4},{6,7},{7,6},{8,0},{9,1},{10,... | collective-permute-start | bytes 417800 | tf_op jit(solution)/shard_map/ppermute | solution.py:270
  9.3 0.0 copy-start.1
  9.3 2.2 %input_grad.2.rest_0_ = bf16[2240,256]{1,0:T(8,128)(2,1)} custom-call(bf16[2240,64]{1,0:T(8,128)(2,1)S(1)} %get-tuple-element.14.back_ref, bf16[2240,256]{1,0:T(8,128)(2,1)} %bitcast.21, f32[64,1088]{1,0:T(8,128)} %params_ref.5), custom_call_target="tpu_custom_call" | custom-call | flops 36700160 | bytes 1290240 | tf_op jit(solution)/shard_map/input_grad/pallas_call | solution.py:240
  11.6 0.9 %collective-permute-done.1 = f32[4,8,1088]{2,1,0:T(8,128)S(1)} collective-permute-done((f32[4,8,1088]{2,1,0:T(8,128)S(1)}, f32[4,8,1088]{2,1,0:T(8,128)S(1)}, u32[]{:S(2)}, u32[]{:S(2)}) %collective-permute-start.1) | collective-permute-done | bytes 139296 | tf_op jit(solution)/shard_map/ppermute | solution.py:270
  12.5 2.2 %collective-permute-start.2 = (f32[4,8,1088]{2,1,0:T(8,128)S(1)}, f32[4,8,1088]{2,1,0:T(8,128)S(1)}, u32[]{:S(2)}, u32[]{:S(2)}) collective-permute-start(f32[4,8,1088]{2,1,0:T(8,128)S(1)} %add.16), channel_id=1, source_target_pairs={{0,1},{1,0},{2,3},{3,2},{4,12},{5,13},{6,14},{7,15},{8,9},{9,8},{1... | collective-permute-start | bytes 417800 | tf_op jit(solution)/shard_map/ppermute | solution.py:270
  14.6 0.0 copy-done.1
  14.6 1.5 %collective-permute-start.6 = (f32[1,8,1088]{2,1,0:T(8,128)S(1)}, f32[1,8,1088]{2,1,0:T(8,128)S(1)}, u32[]{:S(2)}, u32[]{:S(2)}) collective-permute-start(f32[1,8,1088]{2,1,0:T(8,128)S(1)} %bitcast.28), channel_id=1, source_target_pairs={{0,16},{4,20},{8,24},{12,28},{16,0},{20,4},{24,8},{28,12},{1,17},{... | collective-permute-start | bytes 104456 | tf_op jit(solution)/shard_map/ppermute | solution.py:169
  16.2 1.6 %collective-permute-done.2 = f32[4,8,1088]{2,1,0:T(8,128)S(1)} collective-permute-done((f32[4,8,1088]{2,1,0:T(8,128)S(1)}, f32[4,8,1088]{2,1,0:T(8,128)S(1)}, u32[]{:S(2)}, u32[]{:S(2)}) %collective-permute-start.2) | collective-permute-done | bytes 139296 | tf_op jit(solution)/shard_map/ppermute | solution.py:270
  17.8 2.0 %collective-permute-start.3 = (f32[4,8,1088]{2,1,0:T(8,128)S(1)}, f32[4,8,1088]{2,1,0:T(8,128)S(1)}, u32[]{:S(2)}, u32[]{:S(2)}) collective-permute-start(f32[4,8,1088]{2,1,0:T(8,128)S(1)} %add.17), channel_id=1, source_target_pairs={{0,16},{1,17},{2,18},{3,19},{4,6},{5,7},{6,4},{7,5},{8,24},{9,25},... | collective-permute-start | bytes 417800 | tf_op jit(solution)/shard_map/ppermute | solution.py:270
  19.8 0.0 collective-permute-done.6
  19.8 1.6 %collective-permute-start.7 = (f32[2,8,1088]{2,1,0:T(8,128)S(1)}, f32[2,8,1088]{2,1,0:T(8,128)S(1)}, u32[]{:S(2)}, u32[]{:S(2)}) collective-permute-start(f32[2,8,1088]{2,1,0:T(8,128)S(1)} %get-tuple-element.22), channel_id=1, source_target_pairs={{0,8},{4,12},{8,0},{12,4},{16,24},{20,28},{24,16},{28,20},{1,9},{5... | collective-permute-start | bytes 208904 | tf_op jit(solution)/shard_map/ppermute | solution.py:169
  21.4 1.6 %collective-permute-done.3 = f32[4,8,1088]{2,1,0:T(8,128)S(1)} collective-permute-done((f32[4,8,1088]{2,1,0:T(8,128)S(1)}, f32[4,8,1088]{2,1,0:T(8,128)S(1)}, u32[]{:S(2)}, u32[]{:S(2)}) %collective-permute-start.3) | collective-permute-done | bytes 139296 | tf_op jit(solution)/shard_map/ppermute | solution.py:270
  23.0 3.1 %collective-permute-start.4 = (f32[4,8,1088]{2,1,0:T(8,128)S(1)}, f32[4,8,1088]{2,1,0:T(8,128)S(1)}, u32[]{:S(2)}, u32[]{:S(2)}) collective-permute-start(f32[4,8,1088]{2,1,0:T(8,128)S(1)} %add.18), channel_id=1, source_target_pairs={{0,2},{1,3},{2,0},{3,1},{4,20},{5,21},{6,22},{7,23},{8,10},{9,11},... | collective-permute-start | bytes 417800 | tf_op jit(solution)/shard_map/ppermute | solution.py:270
  26.1 0.0 collective-permute-done.7
  26.2 0.0 copy-start
  26.2 0.1 collective-permute-start.8
  26.2 2.2 %input_grad.3 = bf16[2240,256]{1,0:T(8,128)(2,1)} custom-call(bf16[2240,64]{1,0:T(8,128)(2,1)S(1)} %get-tuple-element.14.back_ref, bf16[2240,256]{1,0:T(8,128)(2,1)} %bitcast.22, f32[64,1088]{1,0:T(8,128)} %params_ref.5, bf16[2240,256]{1,0:T(8,128)(2,1)} %input_grad.2.rest_0_), custom_call_target="tpu_custom_call", output_to_operand_aliasing={{}: (3, {})} | custom-call | flops 36700160 | bytes 1290240 | tf_op jit(solution)/shard_map/input_grad/pallas_call | solution.py:240
  28.5 2.3 %collective-permute-done.4 = f32[4,8,1088]{2,1,0:T(8,128)S(1)} collective-permute-done((f32[4,8,1088]{2,1,0:T(8,128)S(1)}, f32[4,8,1088]{2,1,0:T(8,128)S(1)}, u32[]{:S(2)}, u32[]{:S(2)}) %collective-permute-start.4) | collective-permute-done | bytes 139296 | tf_op jit(solution)/shard_map/ppermute | solution.py:270
  30.8 0.1 collective-permute-start.5
  30.9 0.0 collective-permute-done.8.other_speed_ref
  30.9 1.3 %collective-permute-done.5.other_ref = f32[4,8,1088]{2,1,0:T(8,128)S(1)} collective-permute-done((f32[4,8,1088]{2,1,0:T(8,128)S(1)}, f32[4,8,1088]{2,1,0:T(8,128)S(1)}, u32[]{:S(2)}, u32[]{:S(2)}) %collective-permute-start.5) | collective-permute-done | bytes 139296 | tf_op jit(solution)/shard_map/ppermute | solution.py:169
  32.3 0.0 copy-done
  32.3 0.9 %update.1 = (f32[8,1088]{1,0:T(8,128)}, f32[8,8,1088]{2,1,0:T(8,128)}) custom-call(s32[1]{0:T(128)} %bitcast.place_ref, f32[4,8,1088]{2,1,0:T(8,128)S(1)} %add.19.own_ref, f32[4,8,1088]{2,1,0:T(8,128)S(1)} %collective-permute-done.5.other_ref, f32[4,8,1088]{2,1,0:T(8,128)S(1)} %bitcast.19, f32[4,8,1088]{2,1,0:T(8,128)S(1)} %collective-permute-done.8.other_speed_ref, ...), custom_call_target="tpu_custom_call" | custom-call | tf_op jit(solution)/shard_map/update/pallas_call | solution.py:281
  (8 shorter events, 0.1 us)
Async XLA Ops:
  4.8 1.6 %collective-permute-start = (f32[4,8,1088]{2,1,0:T(8,128)S(1)}, f32[4,8,1088]{2,1,0:T(8,128)S(1)}, u32[]{:S(2)}, u32[]{:S(2)}) collective-permute-start(f32[4,8,1088]{2,1,0:T(8,128)S(1)} %get-tuple-element.13), channel_id=1, source_target_pairs={{0,4},{4,0},{8,12},{12,8},{16,20},{20,16},{24,28},{28,24},{1,5},{5... | collective-permute-start | bytes 417800 | tf_op jit(solution)/shard_map/ppermute | solution.py:169
  6.4 6.0 %collective-permute-start.1 = (f32[4,8,1088]{2,1,0:T(8,128)S(1)}, f32[4,8,1088]{2,1,0:T(8,128)S(1)}, u32[]{:S(2)}, u32[]{:S(2)}) collective-permute-start(f32[4,8,1088]{2,1,0:T(8,128)S(1)} %add.15), channel_id=1, source_target_pairs={{0,8},{1,9},{2,10},{3,11},{4,5},{5,4},{6,7},{7,6},{8,0},{9,1},{10,... | collective-permute-start | bytes 417800 | tf_op jit(solution)/shard_map/ppermute | solution.py:270
  9.3 5.3 %copy-start.1 = (f32[8,1088]{1,0:T(8,128)S(1)}, f32[8,1088]{1,0:T(8,128)}, u32[]{:S(2)}) copy-start(f32[8,1088]{1,0:T(8,128)} %param.11) | copy-start | bytes 104452
  12.5 5.3 %collective-permute-start.2 = (f32[4,8,1088]{2,1,0:T(8,128)S(1)}, f32[4,8,1088]{2,1,0:T(8,128)S(1)}, u32[]{:S(2)}, u32[]{:S(2)}) collective-permute-start(f32[4,8,1088]{2,1,0:T(8,128)S(1)} %add.16), channel_id=1, source_target_pairs={{0,1},{1,0},{2,3},{3,2},{4,12},{5,13},{6,14},{7,15},{8,9},{9,8},{1... | collective-permute-start | bytes 417800 | tf_op jit(solution)/shard_map/ppermute | solution.py:270
  14.6 5.2 %collective-permute-start.6 = (f32[1,8,1088]{2,1,0:T(8,128)S(1)}, f32[1,8,1088]{2,1,0:T(8,128)S(1)}, u32[]{:S(2)}, u32[]{:S(2)}) collective-permute-start(f32[1,8,1088]{2,1,0:T(8,128)S(1)} %bitcast.28), channel_id=1, source_target_pairs={{0,16},{4,20},{8,24},{12,28},{16,0},{20,4},{24,8},{28,12},{1,17},{... | collective-permute-start | bytes 104456 | tf_op jit(solution)/shard_map/ppermute | solution.py:169
  17.8 5.2 %collective-permute-start.3 = (f32[4,8,1088]{2,1,0:T(8,128)S(1)}, f32[4,8,1088]{2,1,0:T(8,128)S(1)}, u32[]{:S(2)}, u32[]{:S(2)}) collective-permute-start(f32[4,8,1088]{2,1,0:T(8,128)S(1)} %add.17), channel_id=1, source_target_pairs={{0,16},{1,17},{2,18},{3,19},{4,6},{5,7},{6,4},{7,5},{8,24},{9,25},... | collective-permute-start | bytes 417800 | tf_op jit(solution)/shard_map/ppermute | solution.py:270
  19.8 6.3 %collective-permute-start.7 = (f32[2,8,1088]{2,1,0:T(8,128)S(1)}, f32[2,8,1088]{2,1,0:T(8,128)S(1)}, u32[]{:S(2)}, u32[]{:S(2)}) collective-permute-start(f32[2,8,1088]{2,1,0:T(8,128)S(1)} %get-tuple-element.22), channel_id=1, source_target_pairs={{0,8},{4,12},{8,0},{12,4},{16,24},{20,28},{24,16},{28,20},{1,9},{5... | collective-permute-start | bytes 208904 | tf_op jit(solution)/shard_map/ppermute | solution.py:169
  23.0 7.8 %collective-permute-start.4 = (f32[4,8,1088]{2,1,0:T(8,128)S(1)}, f32[4,8,1088]{2,1,0:T(8,128)S(1)}, u32[]{:S(2)}, u32[]{:S(2)}) collective-permute-start(f32[4,8,1088]{2,1,0:T(8,128)S(1)} %add.18), channel_id=1, source_target_pairs={{0,2},{1,3},{2,0},{3,1},{4,20},{5,21},{6,22},{7,23},{8,10},{9,11},... | collective-permute-start | bytes 417800 | tf_op jit(solution)/shard_map/ppermute | solution.py:270
  26.2 6.1 %copy-start = (f32[64,1088]{1,0:T(8,128)S(1)}, f32[64,1088]{1,0:T(8,128)}, u32[]{:S(2)}) copy-start(f32[64,1088]{1,0:T(8,128)} %params_ref.5) | copy-start | bytes 835588
  26.2 4.8 %collective-permute-start.8 = (f32[4,8,1088]{2,1,0:T(8,128)S(1)}, f32[4,8,1088]{2,1,0:T(8,128)S(1)}, u32[]{:S(2)}, u32[]{:S(2)}) collective-permute-start(f32[4,8,1088]{2,1,0:T(8,128)S(1)} %bitcast.18), channel_id=1, source_target_pairs={{0,4},{4,0},{8,12},{12,8},{16,20},{20,16},{24,28},{28,24},{1,5},{5... | collective-permute-start | bytes 417800 | tf_op jit(solution)/shard_map/ppermute | solution.py:169
  30.8 1.4 %collective-permute-start.5 = (f32[4,8,1088]{2,1,0:T(8,128)S(1)}, f32[4,8,1088]{2,1,0:T(8,128)S(1)}, u32[]{:S(2)}, u32[]{:S(2)}) collective-permute-start(f32[4,8,1088]{2,1,0:T(8,128)S(1)} %add.19.own_ref), channel_id=1, source_target_pairs={{0,4},{4,0},{8,12},{12,8},{16,20},{20,16},{24,28},{28,24},{1,5},{5... | collective-permute-start | bytes 417800 | tf_op jit(solution)/shard_map/ppermute | solution.py:169

commit v4 on v3

--- a/solution.py
+++ b/solution.py
@@ -30,11 +30,27 @@
 
 
 def grad_kernel(
-    place_ref, x_ref, first_ref, second_ref, out_ref, params_ref,
-    keep_ref, send_ref, back_ref,
-    first_px, second_px, bs_px, spread_px, bs_cols, first_rows, second_bf, taps_ref,
+    place_ref, x_hbm, first_hbm, second_hbm, out_hbm, params_hbm,
+    keep_ref, send_ref, back_ref, out_ref,
+    x_ref, first_ref, second_ref, params_ref,
+    first_px, second_px, bs_px, spread_px, bs_cols, first_rows, second_bf, taps_ref, arrived,
     *, height, width, strips, rows,
 ):
+    moves = [
+        pltpu.make_async_copy(source, target, arrived.at[n])
+        for n, (source, target) in enumerate(
+            (
+                (second_hbm, second_ref),
+                (first_hbm, first_ref),
+                (params_hbm, params_ref),
+                (out_hbm, out_ref),
+                (x_hbm, x_ref),
+            )
+        )
+    ]
+    for move in moves:
+        move.start()
+    got_second, got_first, got_params, got_out, got_x = moves
     c_in = x_ref.shape[1]
     mid = params_ref.shape[0]
     pixels = height * width
@@ -46,21 +62,25 @@
     low = lax.broadcasted_iota(jnp.int32, (step, 2 * mid), 1) < mid
     column = lax.broadcasted_iota(jnp.int32, (step, 2 * mid), 0) % width
 
-    w_all = params_ref[...].astype(BF16)
-    w_third = w_all[:, c_in + 9 * mid :]
+    first_px[:width, :] = jnp.zeros((width, 2 * mid), F32)
+    first_px[width + pixels :, :] = jnp.zeros((width, 2 * mid), F32)
+    spread_px[:width, :] = jnp.zeros((width, 4 * mid), F32)
+    spread_px[width + pixels :, :] = jnp.zeros((width, 4 * mid), F32)
+    taps_ref[...] = jnp.zeros_like(taps_ref)
+    got_second.wait()
+    spread_pixels(second_ref, second_px, 0, height, width, mid)
+    got_first.wait()
+    spread_pixels(first_ref, first_px, width, height, width, mid)
+    got_params.wait()
+    w_third = params_ref[:, c_in + 9 * mid :].astype(BF16)
     w_third = jnp.concatenate([w_third, w_third], axis=0)
-    taps_ref[...] = jnp.zeros_like(taps_ref)
     for r in range(3):
         for q in range(3):
             t = 3 * r + q
             taps_ref[q * mid : (q + 1) * mid, r * mid : (r + 1) * mid] = params_ref[
                 :, c_in + t * mid : c_in + (t + 1) * mid
             ].astype(BF16)
-
-    spread_pixels(second_ref, second_px, 0, height, width, mid)
-    first_px[:width, :] = jnp.zeros((width, 2 * mid), F32)
-    first_px[width + pixels :, :] = jnp.zeros((width, 2 * mid), F32)
-    spread_pixels(first_ref, first_px, width, height, width, mid)
+    got_out.wait()
 
     for c in chunks:
         back = lax.dot_general(out_ref[c, :], w_third, (((1,), (1,)), ((), ())), preferred_element_type=F32)
@@ -68,8 +88,6 @@
         bs_px[pad + c.start : pad + c.stop, :] = jnp.where(second > 0, back * s_three, 0.0)
         second_bf[c, :] = second.astype(BF16)
 
-    spread_px[:width, :] = jnp.zeros((width, 4 * mid), F32)
-    spread_px[width + pixels :, :] = jnp.zeros((width, 4 * mid), F32)
     for c in chunks:
         here = bs_px[pad + c.start : pad + c.stop, :]
         after = jnp.where(column < width - 1, bs_px[pad + 1 + c.start : pad + 1 + c.stop, :], 0.0)
@@ -93,9 +111,10 @@
     def outer(left, right):
         return lax.dot_general(left, right, (((0,), (0,)), ((), ())), preferred_element_type=F32)
 
-    grad_one = outer(back_ref[...], x_ref[...]) * (s_one / strips)
     grad_two = outer(bs_cols[...], first_rows[...]) * (s_two / strips)
     grad_three = outer(second_bf[...], out_ref[...])[:mid] * (s_three / strips)
+    got_x.wait()
+    grad_one = outer(back_ref[...], x_ref[...]) * (s_one / strips)
 
     def put(ref, parity):
         for k in range(mid // (2 * rows)):
@@ -117,8 +136,7 @@
             put(send_ref, 1 - own)
 
 
-def input_grad_kernel(back_ref, out_ref, params_ref, *rest):
-    result_ref = rest[-1]
+def input_grad_kernel(back_ref, out_ref, params_ref, result_ref):
     c_in = out_ref.shape[1]
     w_first = params_ref[:, :c_in].astype(BF16)
     change = jnp.dot(back_ref[...], w_first, preferred_element_type=F32)
@@ -206,12 +224,16 @@
     out_flat = out_grad.reshape(pixels, c_in)
     half = pltpu.VMEM((halves, rows, row), F32)
 
-    keep, send, back_first = pl.pallas_call(
+    keep, send, back_first, out_near = pl.pallas_call(
         functools.partial(grad_kernel, height=height, width=width, strips=strips, rows=rows),
-        out_shape=(half, half, pltpu.VMEM((pixels, mid), BF16)),
-        in_specs=[pl.BlockSpec(memory_space=pltpu.SMEM)] + full_vmem(5),
-        out_specs=tuple(full_vmem(3)),
+        out_shape=(half, half, pltpu.VMEM((pixels, mid), BF16), pltpu.VMEM((pixels, c_in), BF16)),
+        in_specs=[pl.BlockSpec(memory_space=pltpu.SMEM)] + [pl.BlockSpec(memory_space=pltpu.HBM)] * 5,
+        out_specs=tuple(full_vmem(4)),
         scratch_shapes=[
+            pltpu.VMEM((pixels, c_in), BF16),
+            pltpu.VMEM((height, width * mid), BF16),
+            pltpu.VMEM((height, width * mid), BF16),
+            pltpu.VMEM((mid, row), F32),
             pltpu.VMEM((pixels + 2 * width, 2 * mid), F32),
             pltpu.VMEM((pixels, 2 * mid), F32),
             pltpu.VMEM((pixels + 16, 2 * mid), F32),
@@ -220,6 +242,7 @@
             pltpu.VMEM((pixels, 4 * mid), BF16),
             pltpu.VMEM((pixels, 2 * mid), BF16),
             pltpu.VMEM((4 * mid, 4 * mid), BF16),
+            pltpu.SemaphoreType.DMA((5,)),
         ],
         name="grads",
     )(
@@ -231,31 +254,16 @@
         params,
     )
 
-    pieces = 2
-    block = pixels // (2 * pieces)
-
-    def input_grad_piece(piece, earlier):
-        first = 2 * piece
-        operands = [*in_vmem(back_first), out_flat, params] + ([] if earlier is None else [earlier])
-        return pl.pallas_call(
-            input_grad_kernel,
-            out_shape=jax.ShapeDtypeStruct((pixels, c_in), BF16),
-            grid=(2,),
-            in_specs=[
-                pl.BlockSpec((block, mid), lambda i: (first + i, 0)),
-                pl.BlockSpec((block, c_in), lambda i: (first + i, 0)),
-                pl.BlockSpec((mid, row), lambda i: (0, 0)),
-                pl.BlockSpec(memory_space=pl.ANY),
-            ][: len(operands)],
-            out_specs=pl.BlockSpec((block, c_in), lambda i: (first + i, 0)),
-            input_output_aliases={} if earlier is None else {3: 0},
-            cost_estimate=pl.CostEstimate(
-                flops=2 * pixels * mid * c_in // pieces,
-                bytes_accessed=2 * pixels * (2 * c_in + mid) // pieces,
-                transcendentals=0,
-            ),
-            name="input_grad",
-        )(*operands)
+    input_grad = pl.pallas_call(
+        input_grad_kernel,
+        out_shape=pltpu.VMEM((pixels, c_in), BF16),
+        in_specs=full_vmem(3),
+        out_specs=full_vmem(1)[0],
+        cost_estimate=pl.CostEstimate(
+            flops=2 * pixels * mid * c_in, bytes_accessed=2 * pixels * (2 * c_in + mid), transcendentals=0
+        ),
+        name="input_grad",
+    )(*in_vmem(back_first, out_near, params))
 
     total = keep + flip(send, "gx", 1)
     speeds = velocity.reshape(1, rows, row)
@@ -264,12 +272,10 @@
         speeds = jnp.stack([speeds, flip(speeds, "gx", bit)], axis=1).reshape(-1, rows, row)
         bit //= 2
     other_speeds = flip(speeds, "gx", 1)
-    input_grad = None
     steps, bit = exchange_steps(group, depth)
     for number, table in enumerate(steps):
         total = total + lax.ppermute(total, ("gx", "gy"), table)
-        if number in (0, len(steps) - 1):
-            input_grad = input_grad_piece(min(number, 1), input_grad)
+        if number == 0:
             total, input_grad = lax.optimization_barrier((total, input_grad))
     turned = [
         lax.ppermute(total, "gy", [(i, (i + turn * bit) % depth) for i in range(depth)])

time: 33.4 us -> 33.2 us (level)
  Pallas kernels: 9.56 us -> 5.4 us
  waiting for transfers between devices: 8.81 us -> 11.8 us
  local copies, waits for them, and re-layouts: 0.02 us -> 1.02 us
    ppermute x4, waiting for transfers between devices: 6.44 us -> 10.5 us  [shards(): total = total + lax.ppermute(total, ('gx', 'gy'), table)]
    pallas_call x2 -> x1, Pallas kernels: 4.45 us -> 0.43 us  [shards(): pl.pallas_call(input_grad_kernel, out_shape=pltpu.VMEM((pixels, c_in), BF...]
    unnamed x4 -> x5, local copies, waits for them, and re-layouts: 0.01 us -> 1.01 us
    ppermute x5, waiting for transfers between devices: 2.36 us -> 1.36 us  [flip(): lax.ppermute(value, axis, [(i, i ^ bit) for i in range(lax.axis_size(axis...]
  transfers between devices with their start and end apart: 9 -> 9, of which waited for: 6 -> 6; matrix products, arithmetic and copies ran while one was open for 0% -> 3% of each run, Pallas kernels for 13% -> 1%
where the time goes in v4:
time: 33.2 us; the launch traced here: 33.1 us
  starting transfers between devices  14 us (42%)
  waiting for transfers between devices  11.8 us (36%)
  Pallas kernels  5.4 us (16%)
  local copies, waits for them, and re-layouts  1.02 us (3%)
  between operations  0.72 us (2%)
    ppermute x4, waiting for transfers between devices, shards(): total = total + lax.ppermute(total, ('gx', 'gy'), table)  10.5 us
    ppermute x4, starting transfers between devices, shards(): total = total + lax.ppermute(total, ('gx', 'gy'), table)  10.2 us
    pallas_call x1, Pallas kernels, shards(): pl.pallas_call(functools.partial(grad_kernel, height=height, width=width,...  4.06 us
    ppermute x5, starting transfers between devices, flip(): lax.ppermute(value, axis, [(i, i ^ bit) for i in range(lax.axis_size(axis...  3.78 us
    ppermute x5, waiting for transfers between devices, flip(): lax.ppermute(value, axis, [(i, i ^ bit) for i in range(lax.axis_size(axis...  1.36 us
    unnamed x5, local copies, waits for them, and re-layouts  1.01 us
    pallas_call x1, Pallas kernels, shards(): pl.pallas_call(functools.partial(update_kernel, c_in=c_in, mid=mid), out_...  0.91 us
  transfers between devices with their start and end apart: 9, of which 6 were waited for; matrix products, arithmetic and copies ran while one was open for 3% of the time, Pallas kernels for 1%

profile of v4, /device:TPU:0, one launch (start us, length us, event | category | flops | bytes accessed | tf_op | source)
XLA Modules:
  0.0 33.1 jit_solution(13519487671831435472)
XLA Ops:
  0.6 0.0 copy-start
  0.6 4.1 %grads.1 = (f32[4,8,1088]{2,1,0:T(8,128)S(1)}, f32[4,8,1088]{2,1,0:T(8,128)S(1)}, bf16[2240,64]{1,0:T(8,128)(2,1)S(1)}, bf16[2240,256]{1,0:T(8,128)(2,1)S(1)}) custom-call(s32[1]{0:T(128)} %bitcast.place_ref, bf16[2240,256]{1,0:T(8,128)(2,1)} %bitcast.21, bf16[40,3584]{1,0:T(8,128)(2,1)} %bitcast.23, bf16[40,3584]{1,0:T(8,128)(2,1)} %bitcast.24, ...), custom_call_target="tpu_custom_call" | custom-call | tf_op jit(solution)/shard_map/grads/pallas_call | solution.py:227
  4.7 0.6 %collective-permute-start = (f32[4,8,1088]{2,1,0:T(8,128)S(1)}, f32[4,8,1088]{2,1,0:T(8,128)S(1)}, u32[]{:S(2)}, u32[]{:S(2)}) collective-permute-start(f32[4,8,1088]{2,1,0:T(8,128)S(1)} %get-tuple-element.12), channel_id=1, source_target_pairs={{0,4},{4,0},{8,12},{12,8},{16,20},{20,16},{24,28},{28,24},{1,5},{5... | collective-permute-start | bytes 417800 | tf_op jit(solution)/shard_map/ppermute | solution.py:187
  5.3 1.0 %collective-permute-done = f32[4,8,1088]{2,1,0:T(8,128)S(1)} collective-permute-done((f32[4,8,1088]{2,1,0:T(8,128)S(1)}, f32[4,8,1088]{2,1,0:T(8,128)S(1)}, u32[]{:S(2)}, u32[]{:S(2)}) %collective-permute-start) | collective-permute-done | bytes 139296 | tf_op jit(solution)/shard_map/ppermute | solution.py:187
  6.3 2.9 %collective-permute-start.1 = (f32[4,8,1088]{2,1,0:T(8,128)S(1)}, f32[4,8,1088]{2,1,0:T(8,128)S(1)}, u32[]{:S(2)}, u32[]{:S(2)}) collective-permute-start(f32[4,8,1088]{2,1,0:T(8,128)S(1)} %add.15), channel_id=1, source_target_pairs={{0,8},{1,9},{2,10},{3,11},{4,5},{5,4},{6,7},{7,6},{8,0},{9,1},{10,... | collective-permute-start | bytes 417800 | tf_op jit(solution)/shard_map/ppermute | solution.py:277
  9.2 0.0 copy-done
  9.2 0.0 copy-start.1
  9.2 0.4 %input_grad.1 = bf16[2240,256]{1,0:T(8,128)(2,1)S(1)} custom-call(bf16[2240,64]{1,0:T(8,128)(2,1)S(1)} %get-tuple-element.13.back_ref, bf16[2240,256]{1,0:T(8,128)(2,1)S(1)} %get-tuple-element.14.out_ref, f32[64,1088]{1,0:T(8,128)S(1)} %copy-done), custom_call_target="tpu_custom_call" | custom-call | flops 73400320 | bytes 2580480 | tf_op jit(solution)/shard_map/input_grad/pallas_call | solution.py:257
  9.7 2.7 %collective-permute-done.1 = f32[4,8,1088]{2,1,0:T(8,128)S(1)} collective-permute-done((f32[4,8,1088]{2,1,0:T(8,128)S(1)}, f32[4,8,1088]{2,1,0:T(8,128)S(1)}, u32[]{:S(2)}, u32[]{:S(2)}) %collective-permute-start.1) | collective-permute-done | bytes 139296 | tf_op jit(solution)/shard_map/ppermute | solution.py:277
  12.4 2.2 %collective-permute-start.2 = (f32[4,8,1088]{2,1,0:T(8,128)S(1)}, f32[4,8,1088]{2,1,0:T(8,128)S(1)}, u32[]{:S(2)}, u32[]{:S(2)}) collective-permute-start(f32[4,8,1088]{2,1,0:T(8,128)S(1)} %add.16), channel_id=1, source_target_pairs={{0,1},{1,0},{2,3},{3,2},{4,12},{5,13},{6,14},{7,15},{8,9},{9,8},{1... | collective-permute-start | bytes 417800 | tf_op jit(solution)/shard_map/ppermute | solution.py:277
  14.5 0.0 copy-done.1
  14.5 1.5 %collective-permute-start.6 = (f32[1,8,1088]{2,1,0:T(8,128)S(1)}, f32[1,8,1088]{2,1,0:T(8,128)S(1)}, u32[]{:S(2)}, u32[]{:S(2)}) collective-permute-start(f32[1,8,1088]{2,1,0:T(8,128)S(1)} %bitcast.26), channel_id=1, source_target_pairs={{0,16},{4,20},{8,24},{12,28},{16,0},{20,4},{24,8},{28,12},{1,17},{... | collective-permute-start | bytes 104456 | tf_op jit(solution)/shard_map/ppermute | solution.py:187
  16.1 1.6 %collective-permute-done.2 = f32[4,8,1088]{2,1,0:T(8,128)S(1)} collective-permute-done((f32[4,8,1088]{2,1,0:T(8,128)S(1)}, f32[4,8,1088]{2,1,0:T(8,128)S(1)}, u32[]{:S(2)}, u32[]{:S(2)}) %collective-permute-start.2) | collective-permute-done | bytes 139296 | tf_op jit(solution)/shard_map/ppermute | solution.py:277
  17.7 2.0 %collective-permute-start.3 = (f32[4,8,1088]{2,1,0:T(8,128)S(1)}, f32[4,8,1088]{2,1,0:T(8,128)S(1)}, u32[]{:S(2)}, u32[]{:S(2)}) collective-permute-start(f32[4,8,1088]{2,1,0:T(8,128)S(1)} %add.17), channel_id=1, source_target_pairs={{0,16},{1,17},{2,18},{3,19},{4,6},{5,7},{6,4},{7,5},{8,24},{9,25},... | collective-permute-start | bytes 417800 | tf_op jit(solution)/shard_map/ppermute | solution.py:277
  19.7 0.0 collective-permute-done.6
  19.7 1.6 %collective-permute-start.7 = (f32[2,8,1088]{2,1,0:T(8,128)S(1)}, f32[2,8,1088]{2,1,0:T(8,128)S(1)}, u32[]{:S(2)}, u32[]{:S(2)}) collective-permute-start(f32[2,8,1088]{2,1,0:T(8,128)S(1)} %get-tuple-element.20), channel_id=1, source_target_pairs={{0,8},{4,12},{8,0},{12,4},{16,24},{20,28},{24,16},{28,20},{1,9},{5... | collective-permute-start | bytes 208904 | tf_op jit(solution)/shard_map/ppermute | solution.py:187
  21.3 1.6 %collective-permute-done.3 = f32[4,8,1088]{2,1,0:T(8,128)S(1)} collective-permute-done((f32[4,8,1088]{2,1,0:T(8,128)S(1)}, f32[4,8,1088]{2,1,0:T(8,128)S(1)}, u32[]{:S(2)}, u32[]{:S(2)}) %collective-permute-start.3) | collective-permute-done | bytes 139296 | tf_op jit(solution)/shard_map/ppermute | solution.py:277
  22.9 3.1 %collective-permute-start.4 = (f32[4,8,1088]{2,1,0:T(8,128)S(1)}, f32[4,8,1088]{2,1,0:T(8,128)S(1)}, u32[]{:S(2)}, u32[]{:S(2)}) collective-permute-start(f32[4,8,1088]{2,1,0:T(8,128)S(1)} %add.18), channel_id=1, source_target_pairs={{0,2},{1,3},{2,0},{3,1},{4,20},{5,21},{6,22},{7,23},{8,10},{9,11},... | collective-permute-start | bytes 417800 | tf_op jit(solution)/shard_map/ppermute | solution.py:277
  26.0 0.0 collective-permute-done.7
  26.0 0.1 collective-permute-start.8
  26.1 4.6 %collective-permute-done.4 = f32[4,8,1088]{2,1,0:T(8,128)S(1)} collective-permute-done((f32[4,8,1088]{2,1,0:T(8,128)S(1)}, f32[4,8,1088]{2,1,0:T(8,128)S(1)}, u32[]{:S(2)}, u32[]{:S(2)}) %collective-permute-start.4) | collective-permute-done | bytes 139296 | tf_op jit(solution)/shard_map/ppermute | solution.py:277
  30.7 0.1 collective-permute-start.5
  30.8 1.0 %copy.10 = bf16[1,40,56,256]{3,2,1,0:T(8,128)(2,1)} copy(bf16[1,40,56,256]{3,2,1,0:T(8,128)(2,1)S(1)} %bitcast.17) | data formatting | bytes 2293760
  31.8 0.0 collective-permute-done.8.other_speed_ref
  31.8 0.3 %collective-permute-done.5.other_ref = f32[4,8,1088]{2,1,0:T(8,128)S(1)} collective-permute-done((f32[4,8,1088]{2,1,0:T(8,128)S(1)}, f32[4,8,1088]{2,1,0:T(8,128)S(1)}, u32[]{:S(2)}, u32[]{:S(2)}) %collective-permute-start.5) | collective-permute-done | bytes 139296 | tf_op jit(solution)/shard_map/ppermute | solution.py:187
  32.2 0.9 %update.1 = (f32[8,1088]{1,0:T(8,128)}, f32[8,8,1088]{2,1,0:T(8,128)}) custom-call(s32[1]{0:T(128)} %bitcast.place_ref, f32[4,8,1088]{2,1,0:T(8,128)S(1)} %add.19.own_ref, f32[4,8,1088]{2,1,0:T(8,128)S(1)} %collective-permute-done.5.other_ref, f32[4,8,1088]{2,1,0:T(8,128)S(1)} %bitcast.20, f32[4,8,1088]{2,1,0:T(8,128)S(1)} %collective-permute-done.8.other_speed_ref, ...), custom_call_target="tpu_custom_call" | custom-call | tf_op jit(solution)/shard_map/update/pallas_call | solution.py:287
  (8 shorter events, 0.1 us)
Async XLA Ops:
  0.6 8.6 %copy-start = (f32[64,1088]{1,0:T(8,128)S(1)}, f32[64,1088]{1,0:T(8,128)}, u32[]{:S(2)}) copy-start(f32[64,1088]{1,0:T(8,128)} %params_ref.1) | copy-start | bytes 835588
  4.7 1.6 %collective-permute-start = (f32[4,8,1088]{2,1,0:T(8,128)S(1)}, f32[4,8,1088]{2,1,0:T(8,128)S(1)}, u32[]{:S(2)}, u32[]{:S(2)}) collective-permute-start(f32[4,8,1088]{2,1,0:T(8,128)S(1)} %get-tuple-element.12), channel_id=1, source_target_pairs={{0,4},{4,0},{8,12},{12,8},{16,20},{20,16},{24,28},{28,24},{1,5},{5... | collective-permute-start | bytes 417800 | tf_op jit(solution)/shard_map/ppermute | solution.py:187
  6.3 6.0 %collective-permute-start.1 = (f32[4,8,1088]{2,1,0:T(8,128)S(1)}, f32[4,8,1088]{2,1,0:T(8,128)S(1)}, u32[]{:S(2)}, u32[]{:S(2)}) collective-permute-start(f32[4,8,1088]{2,1,0:T(8,128)S(1)} %add.15), channel_id=1, source_target_pairs={{0,8},{1,9},{2,10},{3,11},{4,5},{5,4},{6,7},{7,6},{8,0},{9,1},{10,... | collective-permute-start | bytes 417800 | tf_op jit(solution)/shard_map/ppermute | solution.py:277
  9.2 5.3 %copy-start.1 = (f32[8,1088]{1,0:T(8,128)S(1)}, f32[8,1088]{1,0:T(8,128)}, u32[]{:S(2)}) copy-start(f32[8,1088]{1,0:T(8,128)} %param.11) | copy-start | bytes 104452
  12.4 5.3 %collective-permute-start.2 = (f32[4,8,1088]{2,1,0:T(8,128)S(1)}, f32[4,8,1088]{2,1,0:T(8,128)S(1)}, u32[]{:S(2)}, u32[]{:S(2)}) collective-permute-start(f32[4,8,1088]{2,1,0:T(8,128)S(1)} %add.16), channel_id=1, source_target_pairs={{0,1},{1,0},{2,3},{3,2},{4,12},{5,13},{6,14},{7,15},{8,9},{9,8},{1... | collective-permute-start | bytes 417800 | tf_op jit(solution)/shard_map/ppermute | solution.py:277
  14.5 5.2 %collective-permute-start.6 = (f32[1,8,1088]{2,1,0:T(8,128)S(1)}, f32[1,8,1088]{2,1,0:T(8,128)S(1)}, u32[]{:S(2)}, u32[]{:S(2)}) collective-permute-start(f32[1,8,1088]{2,1,0:T(8,128)S(1)} %bitcast.26), channel_id=1, source_target_pairs={{0,16},{4,20},{8,24},{12,28},{16,0},{20,4},{24,8},{28,12},{1,17},{... | collective-permute-start | bytes 104456 | tf_op jit(solution)/shard_map/ppermute | solution.py:187
  17.7 5.2 %collective-permute-start.3 = (f32[4,8,1088]{2,1,0:T(8,128)S(1)}, f32[4,8,1088]{2,1,0:T(8,128)S(1)}, u32[]{:S(2)}, u32[]{:S(2)}) collective-permute-start(f32[4,8,1088]{2,1,0:T(8,128)S(1)} %add.17), channel_id=1, source_target_pairs={{0,16},{1,17},{2,18},{3,19},{4,6},{5,7},{6,4},{7,5},{8,24},{9,25},... | collective-permute-start | bytes 417800 | tf_op jit(solution)/shard_map/ppermute | solution.py:277
  19.7 6.3 %collective-permute-start.7 = (f32[2,8,1088]{2,1,0:T(8,128)S(1)}, f32[2,8,1088]{2,1,0:T(8,128)S(1)}, u32[]{:S(2)}, u32[]{:S(2)}) collective-permute-start(f32[2,8,1088]{2,1,0:T(8,128)S(1)} %get-tuple-element.20), channel_id=1, source_target_pairs={{0,8},{4,12},{8,0},{12,4},{16,24},{20,28},{24,16},{28,20},{1,9},{5... | collective-permute-start | bytes 208904 | tf_op jit(solution)/shard_map/ppermute | solution.py:187
  22.9 7.8 %collective-permute-start.4 = (f32[4,8,1088]{2,1,0:T(8,128)S(1)}, f32[4,8,1088]{2,1,0:T(8,128)S(1)}, u32[]{:S(2)}, u32[]{:S(2)}) collective-permute-start(f32[4,8,1088]{2,1,0:T(8,128)S(1)} %add.18), channel_id=1, source_target_pairs={{0,2},{1,3},{2,0},{3,1},{4,20},{5,21},{6,22},{7,23},{8,10},{9,11},... | collective-permute-start | bytes 417800 | tf_op jit(solution)/shard_map/ppermute | solution.py:277
  26.0 5.8 %collective-permute-start.8 = (f32[4,8,1088]{2,1,0:T(8,128)S(1)}, f32[4,8,1088]{2,1,0:T(8,128)S(1)}, u32[]{:S(2)}, u32[]{:S(2)}) collective-permute-start(f32[4,8,1088]{2,1,0:T(8,128)S(1)} %bitcast.19), channel_id=1, source_target_pairs={{0,4},{4,0},{8,12},{12,8},{16,20},{20,16},{24,28},{28,24},{1,5},{5... | collective-permute-start | bytes 417800 | tf_op jit(solution)/shard_map/ppermute | solution.py:187
  30.7 1.4 %collective-permute-start.5 = (f32[4,8,1088]{2,1,0:T(8,128)S(1)}, f32[4,8,1088]{2,1,0:T(8,128)S(1)}, u32[]{:S(2)}, u32[]{:S(2)}) collective-permute-start(f32[4,8,1088]{2,1,0:T(8,128)S(1)} %add.19.own_ref), channel_id=1, source_target_pairs={{0,4},{4,0},{8,12},{12,8},{16,20},{20,16},{24,28},{28,24},{1,5},{5... | collective-permute-start | bytes 417800 | tf_op jit(solution)/shard_map/ppermute | solution.py:187

commit v5 on v4

--- a/solution.py
+++ b/solution.py
@@ -20,22 +20,19 @@
     return max(d for d in range(1, limit + 1) if number % d == 0)
 
 
-def spread_pixels(src_ref, dst_ref, base, height, width, mid):
-    low = lax.broadcasted_iota(jnp.int32, (height, 2 * mid), 1) < mid
-    for pair in range(width // 2):
-        slab = src_ref[:, 2 * mid * pair : 2 * mid * (pair + 1)].astype(F32)
-        turned = pltpu.roll(slab, mid, 1)
-        dst_ref[pl.ds(base + 2 * pair, height, stride=width), :] = jnp.where(low, slab, turned)
-        dst_ref[pl.ds(base + 2 * pair + 1, height, stride=width), :] = jnp.where(low, turned, slab)
+def round_up(number, multiple):
+    return -(-number // multiple) * multiple
 
 
 def grad_kernel(
     place_ref, x_hbm, first_hbm, second_hbm, out_hbm, params_hbm,
     keep_ref, send_ref, back_ref, out_ref,
     x_ref, first_ref, second_ref, params_ref,
-    first_px, second_px, bs_px, spread_px, bs_cols, first_rows, second_bf, taps_ref, arrived,
-    *, height, width, strips, rows,
+    bs_cols, first_rows, second_bf, taps_ref, arrived, *blocks,
+    height, width, strips, rows,
 ):
+    count = len(blocks) // 4
+    second_px, first_px, bs_px, spread_px = (blocks[n * count : (n + 1) * count] for n in range(4))
     moves = [
         pltpu.make_async_copy(source, target, arrived.at[n])
         for n, (source, target) in enumerate(
@@ -60,17 +57,63 @@
     step = block_rows * width
     chunks = [slice(k * step, (k + 1) * step) for k in range(height // block_rows)]
     low = lax.broadcasted_iota(jnp.int32, (step, 2 * mid), 1) < mid
+    low_slab = lax.broadcasted_iota(jnp.int32, (block_rows, 2 * mid), 1) < mid
     column = lax.broadcasted_iota(jnp.int32, (step, 2 * mid), 0) % width
 
-    first_px[:width, :] = jnp.zeros((width, 2 * mid), F32)
-    first_px[width + pixels :, :] = jnp.zeros((width, 2 * mid), F32)
-    spread_px[:width, :] = jnp.zeros((width, 4 * mid), F32)
-    spread_px[width + pixels :, :] = jnp.zeros((width, 4 * mid), F32)
     taps_ref[...] = jnp.zeros_like(taps_ref)
     got_second.wait()
-    spread_pixels(second_ref, second_px, 0, height, width, mid)
     got_first.wait()
-    spread_pixels(first_ref, first_px, width, height, width, mid)
+
+    def to_pixels(number):
+        for ref, px in ((second_ref, second_px[number]), (first_ref, first_px[number])):
+            for k in range(width // 2):
+                slab = ref[
+                    number * block_rows : (number + 1) * block_rows, 2 * mid * k : 2 * mid * (k + 1)
+                ].astype(F32)
+                turned = pltpu.roll(slab, mid, 1)
+                px[pl.ds(2 * k, block_rows, stride=width), :] = jnp.where(low_slab, slab, turned)
+                px[pl.ds(2 * k + 1, block_rows, stride=width), :] = jnp.where(low_slab, turned, slab)
+
+    def enter(number):
+        c = chunks[number]
+        second = second_px[number][...]
+        second_bf[c, :] = second[:, :mid].astype(BF16)
+        back = lax.dot_general(out_ref[c, :], w_third, (((1,), (1,)), ((), ())), preferred_element_type=F32)
+        here = jnp.where(second > 0, back * s_three, 0.0)
+        px = bs_px[number]
+        px[pad : pad + step, :] = here
+        after = jnp.where(column < width - 1, px[pad + 1 : pad + 1 + step, :], 0.0)
+        before = jnp.where(column > 0, px[pad - 1 : pad - 1 + step, :], 0.0)
+        cols = jnp.concatenate([jnp.where(low, after, here), before], axis=1).astype(BF16)
+        bs_cols[c, :] = cols
+        spread_px[number][...] = jnp.dot(cols, taps_ref[...], preferred_element_type=F32)
+
+    def row_above(blocks, number, lanes):
+        head = blocks[number - 1][step - width :, lanes] if number else jnp.zeros((width, 2 * mid), F32)
+        return jnp.concatenate([head, blocks[number][: step - width, lanes]], axis=0)
+
+    def row_below(blocks, number, lanes):
+        last = number + 1 == len(chunks)
+        tail = jnp.zeros((width, 2 * mid), F32) if last else blocks[number + 1][:width, lanes]
+        return jnp.concatenate([blocks[number][width:, lanes], tail], axis=0)
+
+    def leave(number):
+        c = chunks[number]
+        front, rear = slice(0, 2 * mid), slice(2 * mid, 4 * mid)
+        level = first_px[number][...]
+        above = row_above(first_px, number, front)
+        below = row_below(first_px, number, front)
+        first_rows[c, :] = jnp.concatenate([jnp.where(low, above, level), below], axis=1).astype(BF16)
+        top = row_below(spread_px, number, front)
+        centre = pltpu.roll(spread_px[number][:, front], mid, 1)
+        bottom = row_above(spread_px, number, rear)
+        total = jnp.where(level > 0, (top + centre + bottom) * s_two, 0.0)
+        back_ref[c, :] = total[:, :mid].astype(BF16)
+
+    for number in range(len(chunks)):
+        to_pixels(number)
+    got_out.wait()
+    got_x.wait()
     got_params.wait()
     w_third = params_ref[:, c_in + 9 * mid :].astype(BF16)
     w_third = jnp.concatenate([w_third, w_third], axis=0)
@@ -80,60 +123,37 @@
             taps_ref[q * mid : (q + 1) * mid, r * mid : (r + 1) * mid] = params_ref[
                 :, c_in + t * mid : c_in + (t + 1) * mid
             ].astype(BF16)
-    got_out.wait()
-
-    for c in chunks:
-        back = lax.dot_general(out_ref[c, :], w_third, (((1,), (1,)), ((), ())), preferred_element_type=F32)
-        second = second_px[c, :]
-        bs_px[pad + c.start : pad + c.stop, :] = jnp.where(second > 0, back * s_three, 0.0)
-        second_bf[c, :] = second.astype(BF16)
-
-    for c in chunks:
-        here = bs_px[pad + c.start : pad + c.stop, :]
-        after = jnp.where(column < width - 1, bs_px[pad + 1 + c.start : pad + 1 + c.stop, :], 0.0)
-        before = jnp.where(column > 0, bs_px[pad - 1 + c.start : pad - 1 + c.stop, :], 0.0)
-        cols = jnp.concatenate([jnp.where(low, after, here), before], axis=1).astype(BF16)
-        bs_cols[c, :] = cols
-        spread_px[width + c.start : width + c.stop, :] = jnp.dot(cols, taps_ref[...], preferred_element_type=F32)
-        above = first_px[c, :]
-        level = first_px[width + c.start : width + c.stop, :]
-        below = first_px[2 * width + c.start : 2 * width + c.stop, :]
-        first_rows[c, :] = jnp.concatenate([jnp.where(low, above, level), below], axis=1).astype(BF16)
-
-    for c in chunks:
-        top = spread_px[2 * width + c.start : 2 * width + c.stop, : 2 * mid]
-        centre = pltpu.roll(spread_px[width + c.start : width + c.stop, : 2 * mid], mid, 1)
-        bottom = spread_px[c, 2 * mid :]
-        total = (top + centre + bottom) * s_two
-        total = jnp.where(first_px[width + c.start : width + c.stop, :] > 0, total, 0.0)
-        back_ref[c, :] = total[:, :mid].astype(BF16)
-
-    def outer(left, right):
-        return lax.dot_general(left, right, (((0,), (0,)), ((), ())), preferred_element_type=F32)
-
-    grad_two = outer(bs_cols[...], first_rows[...]) * (s_two / strips)
-    grad_three = outer(second_bf[...], out_ref[...])[:mid] * (s_three / strips)
-    got_x.wait()
-    grad_one = outer(back_ref[...], x_ref[...]) * (s_one / strips)
-
-    def put(ref, parity):
+    for number in range(len(chunks)):
+        enter(number)
+        if number:
+            leave(number - 1)
+    leave(len(chunks) - 1)
+
+    spans = [slice(0, pixels)]
+
+    def outer(left, wide, right):
+        terms = [
+            lax.dot_general(left[k, :wide], right[k, :], (((0,), (0,)), ((), ())), preferred_element_type=F32)
+            for k in spans
+        ]
+        return sum(terms[1:], terms[0])
+
+    even = place_ref[0] % 2 == 0
+
+    def put(grad, column):
+        columns = slice(column, column + grad.shape[1])
         for k in range(mid // (2 * rows)):
-            lo = (2 * k + parity) * rows
-            ref[k, :, :c_in] = grad_one[lo : lo + rows]
-            for r in range(3):
-                for q in range(3):
-                    t = 3 * r + q
-                    ref[k, :, c_in + t * mid : c_in + (t + 1) * mid] = grad_two[
-                        q * mid + lo : q * mid + lo + rows, r * mid : (r + 1) * mid
-                    ]
-            ref[k, :, c_in + 9 * mid :] = grad_three[lo : lo + rows]
-
-    for own in range(2):
-
-        @pl.when(place_ref[0] % 2 == own)
-        def _():
-            put(keep_ref, own)
-            put(send_ref, 1 - own)
+            lo = 2 * k * rows
+            one, two = grad[lo : lo + rows], grad[lo + rows : lo + 2 * rows]
+            keep_ref[k, :, columns] = jnp.where(even, one, two)
+            send_ref[k, :, columns] = jnp.where(even, two, one)
+
+    put(outer(second_bf, mid, out_ref) * (s_three / strips), c_in + 9 * mid)
+    grad_two = outer(bs_cols, 3 * mid, first_rows) * (s_two / strips)
+    for r in range(3):
+        for q in range(3):
+            put(grad_two[q * mid : (q + 1) * mid, r * mid : (r + 1) * mid], c_in + (3 * r + q) * mid)
+    put(outer(back_ref, mid, x_ref) * (s_one / strips), 0)
 
 
 def input_grad_kernel(back_ref, out_ref, params_ref, result_ref):
@@ -222,6 +242,7 @@
     strips = group * depth
     place = lax.axis_index("gx").reshape(1)
     out_flat = out_grad.reshape(pixels, c_in)
+    step = divisor_up_to(height, 8) * width
     half = pltpu.VMEM((halves, rows, row), F32)
 
     keep, send, back_first, out_near = pl.pallas_call(
@@ -234,15 +255,16 @@
             pltpu.VMEM((height, width * mid), BF16),
             pltpu.VMEM((height, width * mid), BF16),
             pltpu.VMEM((mid, row), F32),
-            pltpu.VMEM((pixels + 2 * width, 2 * mid), F32),
-            pltpu.VMEM((pixels, 2 * mid), F32),
-            pltpu.VMEM((pixels + 16, 2 * mid), F32),
-            pltpu.VMEM((pixels + 2 * width, 4 * mid), F32),
             pltpu.VMEM((pixels, 4 * mid), BF16),
             pltpu.VMEM((pixels, 4 * mid), BF16),
-            pltpu.VMEM((pixels, 2 * mid), BF16),
+            pltpu.VMEM((pixels, mid), BF16),
             pltpu.VMEM((4 * mid, 4 * mid), BF16),
             pltpu.SemaphoreType.DMA((5,)),
+        ]
+        + [
+            pltpu.VMEM(shape, F32)
+            for shape in ((step, 2 * mid), (step, 2 * mid), (step + 16, 2 * mid), (step, 4 * mid))
+            for _ in range(pixels // step)
         ],
         name="grads",
     )(

time: 33.2 us -> 33.1 us (level)
  no operation moved by 1% of the time
where the time goes in v5:
time: 33.1 us; the launch traced here: 32.9 us
  starting transfers between devices  14 us (42%)
  waiting for transfers between devices  11.8 us (36%)
  Pallas kernels  5.28 us (16%)
  local copies, waits for them, and re-layouts  1.02 us (3%)
  between operations  0.72 us (2%)
    ppermute x4, waiting for transfers between devices, shards(): total = total + lax.ppermute(total, ('gx', 'gy'), table)  10.5 us
    ppermute x4, starting transfers between devices, shards(): total = total + lax.ppermute(total, ('gx', 'gy'), table)  10.2 us
    pallas_call x1, Pallas kernels, shards(): pl.pallas_call(functools.partial(grad_kernel, height=height, width=width,...  3.94 us
    ppermute x5, starting transfers between devices, flip(): lax.ppermute(value, axis, [(i, i ^ bit) for i in range(lax.axis_size(axis...  3.77 us
    ppermute x5, waiting for transfers between devices, flip(): lax.ppermute(value, axis, [(i, i ^ bit) for i in range(lax.axis_size(axis...  1.36 us
    unnamed x5, local copies, waits for them, and re-layouts  1.01 us
    pallas_call x1, Pallas kernels, shards(): pl.pallas_call(functools.partial(update_kernel, c_in=c_in, mid=mid), out_...  0.91 us
  transfers between devices with their start and end apart: 9, of which 6 were waited for; matrix products, arithmetic and copies ran while one was open for 3% of the time, Pallas kernels for 1%

profile of v5, /device:TPU:0, one launch (start us, length us, event | category | flops | bytes accessed | tf_op | source)
XLA Modules:
  0.0 32.9 jit_solution(17504950648446826197)
XLA Ops:
  0.6 0.0 copy-start
  0.6 3.9 %grads.1 = (f32[4,8,1088]{2,1,0:T(8,128)S(1)}, f32[4,8,1088]{2,1,0:T(8,128)S(1)}, bf16[2240,64]{1,0:T(8,128)(2,1)S(1)}, bf16[2240,256]{1,0:T(8,128)(2,1)S(1)}) custom-call(s32[1]{0:T(128)} %bitcast.place_ref, bf16[2240,256]{1,0:T(8,128)(2,1)} %bitcast.21, bf16[40,3584]{1,0:T(8,128)(2,1)} %bitcast.23, bf16[40,3584]{1,0:T(8,128)(2,1)} %bitcast.24, ...), custom_call_target="tpu_custom_call" | custom-call | tf_op jit(solution)/shard_map/grads/pallas_call | solution.py:248
  4.6 0.6 %collective-permute-start = (f32[4,8,1088]{2,1,0:T(8,128)S(1)}, f32[4,8,1088]{2,1,0:T(8,128)S(1)}, u32[]{:S(2)}, u32[]{:S(2)}) collective-permute-start(f32[4,8,1088]{2,1,0:T(8,128)S(1)} %get-tuple-element.12), channel_id=1, source_target_pairs={{0,4},{4,0},{8,12},{12,8},{16,20},{20,16},{24,28},{28,24},{1,5},{5... | collective-permute-start | bytes 417800 | tf_op jit(solution)/shard_map/ppermute | solution.py:207
  5.1 1.0 %collective-permute-done = f32[4,8,1088]{2,1,0:T(8,128)S(1)} collective-permute-done((f32[4,8,1088]{2,1,0:T(8,128)S(1)}, f32[4,8,1088]{2,1,0:T(8,128)S(1)}, u32[]{:S(2)}, u32[]{:S(2)}) %collective-permute-start) | collective-permute-done | bytes 139296 | tf_op jit(solution)/shard_map/ppermute | solution.py:207
  6.2 2.9 %collective-permute-start.1 = (f32[4,8,1088]{2,1,0:T(8,128)S(1)}, f32[4,8,1088]{2,1,0:T(8,128)S(1)}, u32[]{:S(2)}, u32[]{:S(2)}) collective-permute-start(f32[4,8,1088]{2,1,0:T(8,128)S(1)} %add.15), channel_id=1, source_target_pairs={{0,8},{1,9},{2,10},{3,11},{4,5},{5,4},{6,7},{7,6},{8,0},{9,1},{10,... | collective-permute-start | bytes 417800 | tf_op jit(solution)/shard_map/ppermute | solution.py:299
  9.1 0.0 copy-done
  9.1 0.0 copy-start.1
  9.1 0.4 %input_grad.1 = bf16[2240,256]{1,0:T(8,128)(2,1)S(1)} custom-call(bf16[2240,64]{1,0:T(8,128)(2,1)S(1)} %get-tuple-element.13.back_ref, bf16[2240,256]{1,0:T(8,128)(2,1)S(1)} %get-tuple-element.14.out_ref, f32[64,1088]{1,0:T(8,128)S(1)} %copy-done), custom_call_target="tpu_custom_call" | custom-call | flops 73400320 | bytes 2580480 | tf_op jit(solution)/shard_map/input_grad/pallas_call | solution.py:279
  9.5 2.7 %collective-permute-done.1 = f32[4,8,1088]{2,1,0:T(8,128)S(1)} collective-permute-done((f32[4,8,1088]{2,1,0:T(8,128)S(1)}, f32[4,8,1088]{2,1,0:T(8,128)S(1)}, u32[]{:S(2)}, u32[]{:S(2)}) %collective-permute-start.1) | collective-permute-done | bytes 139296 | tf_op jit(solution)/shard_map/ppermute | solution.py:299
  12.2 2.2 %collective-permute-start.2 = (f32[4,8,1088]{2,1,0:T(8,128)S(1)}, f32[4,8,1088]{2,1,0:T(8,128)S(1)}, u32[]{:S(2)}, u32[]{:S(2)}) collective-permute-start(f32[4,8,1088]{2,1,0:T(8,128)S(1)} %add.16), channel_id=1, source_target_pairs={{0,1},{1,0},{2,3},{3,2},{4,12},{5,13},{6,14},{7,15},{8,9},{9,8},{1... | collective-permute-start | bytes 417800 | tf_op jit(solution)/shard_map/ppermute | solution.py:299
  14.4 0.0 copy-done.1
  14.4 1.5 %collective-permute-start.6 = (f32[1,8,1088]{2,1,0:T(8,128)S(1)}, f32[1,8,1088]{2,1,0:T(8,128)S(1)}, u32[]{:S(2)}, u32[]{:S(2)}) collective-permute-start(f32[1,8,1088]{2,1,0:T(8,128)S(1)} %bitcast.26), channel_id=1, source_target_pairs={{0,16},{4,20},{8,24},{12,28},{16,0},{20,4},{24,8},{28,12},{1,17},{... | collective-permute-start | bytes 104456 | tf_op jit(solution)/shard_map/ppermute | solution.py:207
  15.9 1.6 %collective-permute-done.2 = f32[4,8,1088]{2,1,0:T(8,128)S(1)} collective-permute-done((f32[4,8,1088]{2,1,0:T(8,128)S(1)}, f32[4,8,1088]{2,1,0:T(8,128)S(1)}, u32[]{:S(2)}, u32[]{:S(2)}) %collective-permute-start.2) | collective-permute-done | bytes 139296 | tf_op jit(solution)/shard_map/ppermute | solution.py:299
  17.5 2.0 %collective-permute-start.3 = (f32[4,8,1088]{2,1,0:T(8,128)S(1)}, f32[4,8,1088]{2,1,0:T(8,128)S(1)}, u32[]{:S(2)}, u32[]{:S(2)}) collective-permute-start(f32[4,8,1088]{2,1,0:T(8,128)S(1)} %add.17), channel_id=1, source_target_pairs={{0,16},{1,17},{2,18},{3,19},{4,6},{5,7},{6,4},{7,5},{8,24},{9,25},... | collective-permute-start | bytes 417800 | tf_op jit(solution)/shard_map/ppermute | solution.py:299
  19.6 0.0 collective-permute-done.6
  19.6 1.6 %collective-permute-start.7 = (f32[2,8,1088]{2,1,0:T(8,128)S(1)}, f32[2,8,1088]{2,1,0:T(8,128)S(1)}, u32[]{:S(2)}, u32[]{:S(2)}) collective-permute-start(f32[2,8,1088]{2,1,0:T(8,128)S(1)} %get-tuple-element.20), channel_id=1, source_target_pairs={{0,8},{4,12},{8,0},{12,4},{16,24},{20,28},{24,16},{28,20},{1,9},{5... | collective-permute-start | bytes 208904 | tf_op jit(solution)/shard_map/ppermute | solution.py:207
  21.1 1.6 %collective-permute-done.3 = f32[4,8,1088]{2,1,0:T(8,128)S(1)} collective-permute-done((f32[4,8,1088]{2,1,0:T(8,128)S(1)}, f32[4,8,1088]{2,1,0:T(8,128)S(1)}, u32[]{:S(2)}, u32[]{:S(2)}) %collective-permute-start.3) | collective-permute-done | bytes 139296 | tf_op jit(solution)/shard_map/ppermute | solution.py:299
  22.8 3.1 %collective-permute-start.4 = (f32[4,8,1088]{2,1,0:T(8,128)S(1)}, f32[4,8,1088]{2,1,0:T(8,128)S(1)}, u32[]{:S(2)}, u32[]{:S(2)}) collective-permute-start(f32[4,8,1088]{2,1,0:T(8,128)S(1)} %add.18), channel_id=1, source_target_pairs={{0,2},{1,3},{2,0},{3,1},{4,20},{5,21},{6,22},{7,23},{8,10},{9,11},... | collective-permute-start | bytes 417800 | tf_op jit(solution)/shard_map/ppermute | solution.py:299
  25.9 0.0 collective-permute-done.7
  25.9 0.1 collective-permute-start.8
  26.0 4.6 %collective-permute-done.4 = f32[4,8,1088]{2,1,0:T(8,128)S(1)} collective-permute-done((f32[4,8,1088]{2,1,0:T(8,128)S(1)}, f32[4,8,1088]{2,1,0:T(8,128)S(1)}, u32[]{:S(2)}, u32[]{:S(2)}) %collective-permute-start.4) | collective-permute-done | bytes 139296 | tf_op jit(solution)/shard_map/ppermute | solution.py:299
  30.6 0.1 collective-permute-start.5
  30.7 1.0 %copy.10 = bf16[1,40,56,256]{3,2,1,0:T(8,128)(2,1)} copy(bf16[1,40,56,256]{3,2,1,0:T(8,128)(2,1)S(1)} %bitcast.17) | data formatting | bytes 2293760
  31.7 0.0 collective-permute-done.8.other_speed_ref
  31.7 0.3 %collective-permute-done.5.other_ref = f32[4,8,1088]{2,1,0:T(8,128)S(1)} collective-permute-done((f32[4,8,1088]{2,1,0:T(8,128)S(1)}, f32[4,8,1088]{2,1,0:T(8,128)S(1)}, u32[]{:S(2)}, u32[]{:S(2)}) %collective-permute-start.5) | collective-permute-done | bytes 139296 | tf_op jit(solution)/shard_map/ppermute | solution.py:207
  32.0 0.9 %update.1 = (f32[8,1088]{1,0:T(8,128)}, f32[8,8,1088]{2,1,0:T(8,128)}) custom-call(s32[1]{0:T(128)} %bitcast.place_ref, f32[4,8,1088]{2,1,0:T(8,128)S(1)} %add.19.own_ref, f32[4,8,1088]{2,1,0:T(8,128)S(1)} %collective-permute-done.5.other_ref, f32[4,8,1088]{2,1,0:T(8,128)S(1)} %bitcast.20, f32[4,8,1088]{2,1,0:T(8,128)S(1)} %collective-permute-done.8.other_speed_ref, ...), custom_call_target="tpu_custom_call" | custom-call | tf_op jit(solution)/shard_map/update/pallas_call | solution.py:309
  (8 shorter events, 0.1 us)
Async XLA Ops:
  0.6 8.5 %copy-start = (f32[64,1088]{1,0:T(8,128)S(1)}, f32[64,1088]{1,0:T(8,128)}, u32[]{:S(2)}) copy-start(f32[64,1088]{1,0:T(8,128)} %params_ref.1) | copy-start | bytes 835588
  4.6 1.6 %collective-permute-start = (f32[4,8,1088]{2,1,0:T(8,128)S(1)}, f32[4,8,1088]{2,1,0:T(8,128)S(1)}, u32[]{:S(2)}, u32[]{:S(2)}) collective-permute-start(f32[4,8,1088]{2,1,0:T(8,128)S(1)} %get-tuple-element.12), channel_id=1, source_target_pairs={{0,4},{4,0},{8,12},{12,8},{16,20},{20,16},{24,28},{28,24},{1,5},{5... | collective-permute-start | bytes 417800 | tf_op jit(solution)/shard_map/ppermute | solution.py:207
  6.2 6.0 %collective-permute-start.1 = (f32[4,8,1088]{2,1,0:T(8,128)S(1)}, f32[4,8,1088]{2,1,0:T(8,128)S(1)}, u32[]{:S(2)}, u32[]{:S(2)}) collective-permute-start(f32[4,8,1088]{2,1,0:T(8,128)S(1)} %add.15), channel_id=1, source_target_pairs={{0,8},{1,9},{2,10},{3,11},{4,5},{5,4},{6,7},{7,6},{8,0},{9,1},{10,... | collective-permute-start | bytes 417800 | tf_op jit(solution)/shard_map/ppermute | solution.py:299
  9.1 5.3 %copy-start.1 = (f32[8,1088]{1,0:T(8,128)S(1)}, f32[8,1088]{1,0:T(8,128)}, u32[]{:S(2)}) copy-start(f32[8,1088]{1,0:T(8,128)} %param.11) | copy-start | bytes 104452
  12.2 5.3 %collective-permute-start.2 = (f32[4,8,1088]{2,1,0:T(8,128)S(1)}, f32[4,8,1088]{2,1,0:T(8,128)S(1)}, u32[]{:S(2)}, u32[]{:S(2)}) collective-permute-start(f32[4,8,1088]{2,1,0:T(8,128)S(1)} %add.16), channel_id=1, source_target_pairs={{0,1},{1,0},{2,3},{3,2},{4,12},{5,13},{6,14},{7,15},{8,9},{9,8},{1... | collective-permute-start | bytes 417800 | tf_op jit(solution)/shard_map/ppermute | solution.py:299
  14.4 5.2 %collective-permute-start.6 = (f32[1,8,1088]{2,1,0:T(8,128)S(1)}, f32[1,8,1088]{2,1,0:T(8,128)S(1)}, u32[]{:S(2)}, u32[]{:S(2)}) collective-permute-start(f32[1,8,1088]{2,1,0:T(8,128)S(1)} %bitcast.26), channel_id=1, source_target_pairs={{0,16},{4,20},{8,24},{12,28},{16,0},{20,4},{24,8},{28,12},{1,17},{... | collective-permute-start | bytes 104456 | tf_op jit(solution)/shard_map/ppermute | solution.py:207
  17.5 5.2 %collective-permute-start.3 = (f32[4,8,1088]{2,1,0:T(8,128)S(1)}, f32[4,8,1088]{2,1,0:T(8,128)S(1)}, u32[]{:S(2)}, u32[]{:S(2)}) collective-permute-start(f32[4,8,1088]{2,1,0:T(8,128)S(1)} %add.17), channel_id=1, source_target_pairs={{0,16},{1,17},{2,18},{3,19},{4,6},{5,7},{6,4},{7,5},{8,24},{9,25},... | collective-permute-start | bytes 417800 | tf_op jit(solution)/shard_map/ppermute | solution.py:299
  19.6 6.3 %collective-permute-start.7 = (f32[2,8,1088]{2,1,0:T(8,128)S(1)}, f32[2,8,1088]{2,1,0:T(8,128)S(1)}, u32[]{:S(2)}, u32[]{:S(2)}) collective-permute-start(f32[2,8,1088]{2,1,0:T(8,128)S(1)} %get-tuple-element.20), channel_id=1, source_target_pairs={{0,8},{4,12},{8,0},{12,4},{16,24},{20,28},{24,16},{28,20},{1,9},{5... | collective-permute-start | bytes 208904 | tf_op jit(solution)/shard_map/ppermute | solution.py:207
  22.8 7.8 %collective-permute-start.4 = (f32[4,8,1088]{2,1,0:T(8,128)S(1)}, f32[4,8,1088]{2,1,0:T(8,128)S(1)}, u32[]{:S(2)}, u32[]{:S(2)}) collective-permute-start(f32[4,8,1088]{2,1,0:T(8,128)S(1)} %add.18), channel_id=1, source_target_pairs={{0,2},{1,3},{2,0},{3,1},{4,20},{5,21},{6,22},{7,23},{8,10},{9,11},... | collective-permute-start | bytes 417800 | tf_op jit(solution)/shard_map/ppermute | solution.py:299
  25.9 5.8 %collective-permute-start.8 = (f32[4,8,1088]{2,1,0:T(8,128)S(1)}, f32[4,8,1088]{2,1,0:T(8,128)S(1)}, u32[]{:S(2)}, u32[]{:S(2)}) collective-permute-start(f32[4,8,1088]{2,1,0:T(8,128)S(1)} %bitcast.19), channel_id=1, source_target_pairs={{0,4},{4,0},{8,12},{12,8},{16,20},{20,16},{24,28},{28,24},{1,5},{5... | collective-permute-start | bytes 417800 | tf_op jit(solution)/shard_map/ppermute | solution.py:207
  30.6 1.4 %collective-permute-start.5 = (f32[4,8,1088]{2,1,0:T(8,128)S(1)}, f32[4,8,1088]{2,1,0:T(8,128)S(1)}, u32[]{:S(2)}, u32[]{:S(2)}) collective-permute-start(f32[4,8,1088]{2,1,0:T(8,128)S(1)} %add.19.own_ref), channel_id=1, source_target_pairs={{0,4},{4,0},{8,12},{12,8},{16,20},{20,16},{24,28},{28,24},{1,5},{5... | collective-permute-start | bytes 417800 | tf_op jit(solution)/shard_map/ppermute | solution.py:207

commit v6 on v5

--- a/solution.py
+++ b/solution.py
@@ -26,11 +26,10 @@
 
 def grad_kernel(
     place_ref, x_hbm, first_hbm, second_hbm, out_hbm, params_hbm,
-    keep_ref, send_ref, back_ref, out_ref,
-    x_ref, first_ref, second_ref, params_ref,
-    bs_cols, first_rows, second_bf, taps_ref, arrived, *blocks,
-    height, width, strips, rows,
+    back_ref, out_ref, *rest, height, width, strips, rows, streams,
 ):
+    keep_refs, send_refs, rest = rest[:streams], rest[streams : 2 * streams], rest[2 * streams :]
+    x_ref, first_ref, second_ref, params_ref, bs_cols, first_rows, second_bf, taps_ref, arrived, *blocks = rest
     count = len(blocks) // 4
     second_px, first_px, bs_px, spread_px = (blocks[n * count : (n + 1) * count] for n in range(4))
     moves = [
@@ -145,8 +144,9 @@
         for k in range(mid // (2 * rows)):
             lo = 2 * k * rows
             one, two = grad[lo : lo + rows], grad[lo + rows : lo + 2 * rows]
-            keep_ref[k, :, columns] = jnp.where(even, one, two)
-            send_ref[k, :, columns] = jnp.where(even, two, one)
+            stream, tile = divmod(k, keep_refs[0].shape[0])
+            keep_refs[stream][tile, :, columns] = jnp.where(even, one, two)
+            send_refs[stream][tile, :, columns] = jnp.where(even, two, one)
 
     put(outer(second_bf, mid, out_ref) * (s_three / strips), c_in + 9 * mid)
     grad_two = outer(bs_cols, 3 * mid, first_rows) * (s_two / strips)
@@ -164,19 +164,21 @@
 
 
 def update_kernel(
-    place_ref, own_ref, other_ref, own_speed_ref, other_speed_ref, params_ref,
-    velocity_ref, weights_ref, *, c_in, mid,
+    place_ref, own_speed_ref, other_speed_ref, params_ref, *rest, c_in, mid,
 ):
+    *grads, velocity_ref, weights_ref = rest
+    streams = len(grads) // 2
+    own_refs, other_refs = grads[:streams], grads[streams:]
     core = place_ref[0] % 2
     pair = place_ref[0] // 2
-    halves, rows, width = own_ref.shape
+    tiles, rows, width = own_refs[0].shape
     lane = lax.broadcasted_iota(jnp.int32, (1, 1, width), 2)
     edges = (0, c_in, c_in + 9 * mid, width)
 
     def column_squares(ref):
         return jnp.sum(jnp.sum(ref[...] ** 2, axis=0, keepdims=True), axis=1, keepdims=True)
 
-    grad_squares = column_squares(own_ref) + column_squares(other_ref)
+    grad_squares = sum(column_squares(ref) for ref in grads)
     param_squares = column_squares(params_ref)
     factor = jnp.zeros((1, 1, width), F32)
     for start, stop in zip(edges[:-1], edges[1:]):
@@ -188,11 +190,15 @@
         trust = jnp.sqrt(total(param_squares)) / (jnp.sqrt(total(grad_squares)) + norm_eps)
         factor = jnp.where(inside, learn_rate * trust, factor)
     factor = factor[0]
-    for k in range(halves):
-        for parity, grad, speed in ((core, own_ref, own_speed_ref), (1 - core, other_ref, other_speed_ref)):
+    for k in range(tiles * streams):
+        for parity, refs, speed in ((core, own_refs, own_speed_ref), (1 - core, other_refs, other_speed_ref)):
             tile = 2 * k + parity
-            weights_ref[tile] = params_ref[tile] - (momentum * speed[k ^ pair] + factor * grad[k])
-    velocity_ref[...] = momentum * own_speed_ref[0] + factor * own_ref[pair]
+            grad = refs[k // tiles][k % tiles]
+            weights_ref[tile] = params_ref[tile] - (momentum * speed[k ^ pair] + factor * grad)
+    mine = own_refs[0][pair % tiles]
+    for number in range(1, streams):
+        mine = jnp.where(pair // tiles == number, own_refs[number][pair % tiles], mine)
+    velocity_ref[...] = momentum * own_speed_ref[0] + factor * mine
 
 
 def full_vmem(count):
@@ -243,13 +249,14 @@
     place = lax.axis_index("gx").reshape(1)
     out_flat = out_grad.reshape(pixels, c_in)
     step = divisor_up_to(height, 8) * width
-    half = pltpu.VMEM((halves, rows, row), F32)
-
-    keep, send, back_first, out_near = pl.pallas_call(
-        functools.partial(grad_kernel, height=height, width=width, strips=strips, rows=rows),
-        out_shape=(half, half, pltpu.VMEM((pixels, mid), BF16), pltpu.VMEM((pixels, c_in), BF16)),
+    streams = 2 if halves % 2 == 0 else 1
+    part = pltpu.VMEM((halves // streams, rows, row), F32)
+
+    back_first, out_near, *parts = pl.pallas_call(
+        functools.partial(grad_kernel, height=height, width=width, strips=strips, rows=rows, streams=streams),
+        out_shape=(pltpu.VMEM((pixels, mid), BF16), pltpu.VMEM((pixels, c_in), BF16), *[part] * (2 * streams)),
         in_specs=[pl.BlockSpec(memory_space=pltpu.SMEM)] + [pl.BlockSpec(memory_space=pltpu.HBM)] * 5,
-        out_specs=tuple(full_vmem(4)),
+        out_specs=tuple(full_vmem(2 + 2 * streams)),
         scratch_shapes=[
             pltpu.VMEM((pixels, c_in), BF16),
             pltpu.VMEM((height, width * mid), BF16),
@@ -287,7 +294,7 @@
         name="input_grad",
     )(*in_vmem(back_first, out_near, params))
 
-    total = keep + flip(send, "gx", 1)
+    totals = [keep + flip(send, "gx", 1) for keep, send in zip(parts[:streams], parts[streams:])]
     speeds = velocity.reshape(1, rows, row)
     bit = group // 2
     while bit > 1:
@@ -296,15 +303,16 @@
     other_speeds = flip(speeds, "gx", 1)
     steps, bit = exchange_steps(group, depth)
     for number, table in enumerate(steps):
-        total = total + lax.ppermute(total, ("gx", "gy"), table)
+        totals = [total + lax.ppermute(total, ("gx", "gy"), table) for total in totals]
         if number == 0:
-            total, input_grad = lax.optimization_barrier((total, input_grad))
-    turned = [
-        lax.ppermute(total, "gy", [(i, (i + turn * bit) % depth) for i in range(depth)])
-        for turn in range(1, depth // bit)
-    ]
-    total = sum(turned, total)
-    other = flip(total, "gx", 1)
+            totals[0], input_grad = lax.optimization_barrier((totals[0], input_grad))
+    for turn in range(1, depth // bit):
+        table = [(i, (i + turn * bit) % depth) for i in range(depth)]
+        terms = [lax.ppermute(total, "gy", table) for total in totals]
+        sums = terms if turn == 1 else [a + b for a, b in zip(sums, terms)]
+    if depth > bit:
+        totals = [a + b for a, b in zip(totals, sums)]
+    others = [flip(total, "gx", 1) for total in totals]
 
     new_velocity, next_weights = pl.pallas_call(
         functools.partial(update_kernel, c_in=c_in, mid=mid),
@@ -312,10 +320,10 @@
             jax.ShapeDtypeStruct((rows, row), F32),
             jax.ShapeDtypeStruct((group, rows, row), F32),
         ),
-        in_specs=[pl.BlockSpec(memory_space=pltpu.SMEM)] + full_vmem(5),
+        in_specs=[pl.BlockSpec(memory_space=pltpu.SMEM)] + full_vmem(3 + 2 * streams),
         out_specs=tuple(full_vmem(2)),
         name="update",
-    )(place, *in_vmem(total, other, speeds, other_speeds, params.reshape(group, rows, row)))
+    )(place, *in_vmem(speeds, other_speeds, params.reshape(group, rows, row), *totals, *others))
     return (input_grad.reshape(1, height, width, c_in), new_velocity, next_weights.reshape(mid, row))
 
 

time: 33.1 us -> 33.3 us (level)
  waiting for transfers between devices: 11.8 us -> 6.88 us
  local copies, waits for them, and re-layouts: 1.02 us -> 3.28 us
  starting transfers between devices: 14 us -> 15.9 us
  other arithmetic: 0.11 us -> 0.91 us
    ppermute x4 -> x8, waiting for transfers between devices: 10.5 us -> 5.02 us  [shards(): lax.ppermute(total, ('gx', 'gy'), table)]
    unnamed x5 -> x7, local copies, waits for them, and re-layouts: 1.01 us -> 3.26 us
    ppermute x4 -> x8, starting transfers between devices: 10.2 us -> 11.7 us  [shards(): lax.ppermute(total, ('gx', 'gy'), table)]
    another operation x2, other arithmetic: 0.02 us -> 0.81 us  [shards(): jnp.stack([speeds, flip(speeds, 'gx', bit)], axis=1).reshape(-1, rows, row)]
    ppermute x5 -> x7, waiting for transfers between devices: 1.36 us -> 1.86 us  [flip(): lax.ppermute(value, axis, [(i, i ^ bit) for i in range(lax.axis_size(axis...]
    ppermute x5 -> x7, starting transfers between devices: 3.77 us -> 4.21 us  [flip(): lax.ppermute(value, axis, [(i, i ^ bit) for i in range(lax.axis_size(axis...]
  transfers between devices with their start and end apart: 9 -> 15, of which waited for: 6 -> 7; matrix products, arithmetic and copies ran while one was open for 3% -> 6% of each run, Pallas kernels for 1% -> 1%
where the time goes in v6:
time: 33.3 us; the launch traced here: 33 us
  starting transfers between devices  15.9 us (48%)
  waiting for transfers between devices  6.88 us (21%)
  Pallas kernels  5.31 us (16%)
  local copies, waits for them, and re-layouts  3.28 us (10%)
  other arithmetic  0.91 us (3%)
  between operations  0.76 us (2%)
    ppermute x8, starting transfers between devices, shards(): lax.ppermute(total, ('gx', 'gy'), table)  11.7 us
    ppermute x8, waiting for transfers between devices, shards(): lax.ppermute(total, ('gx', 'gy'), table)  5.02 us
    ppermute x7, starting transfers between devices, flip(): lax.ppermute(value, axis, [(i, i ^ bit) for i in range(lax.axis_size(axis...  4.21 us
    pallas_call x1, Pallas kernels, shards(): pl.pallas_call(functools.partial(grad_kernel, height=height, width=width,...  3.94 us
    unnamed x7, local copies, waits for them, and re-layouts  3.26 us
    ppermute x7, waiting for transfers between devices, flip(): lax.ppermute(value, axis, [(i, i ^ bit) for i in range(lax.axis_size(axis...  1.86 us
    pallas_call x1, Pallas kernels, shards(): pl.pallas_call(functools.partial(update_kernel, c_in=c_in, mid=mid), out_...  0.93 us
    another operation x2, other arithmetic, shards(): jnp.stack([speeds, flip(speeds, 'gx', bit)], axis=1).reshape(-1, rows, row)  0.81 us
  transfers between devices with their start and end apart: 15, of which 7 were waited for; matrix products, arithmetic and copies ran while one was open for 6% of the time, Pallas kernels for 1%

profile of v6, /device:TPU:0, one launch (start us, length us, event | category | flops | bytes accessed | tf_op | source)
XLA Modules:
  0.0 33.0 jit_solution(3978098514165209772)
XLA Ops:
  0.6 0.0 copy-start
  0.6 3.9 %grads.1 = (bf16[2240,64]{1,0:T(8,128)(2,1)S(1)}, bf16[2240,256]{1,0:T(8,128)(2,1)S(1)}, f32[2,8,1088]{2,1,0:T(8,128)S(1)}, f32[2,8,1088]{2,1,0:T(8,128)S(1)}, f...) custom-call(s32[1]{0:T(128)} %bitcast.place_ref, bf16[2240,256]{1,0:T(8,128)(2,1)} %bitcast.21, ...), custom_call_target="tpu_custom_call" | custom-call | tf_op jit(solution)/shard_map/grads/pallas_call | solution.py:255
  4.6 0.0 copy-start.1
  4.6 1.0 %copy-done.1 = bf16[2240,256]{1,0:T(8,128)(2,1)} copy-done((bf16[2240,256]{1,0:T(8,128)(2,1)}, bf16[2240,256]{1,0:T(8,128)(2,1)S(1)}, u32[]{:S(2)}) %copy-start.1) | copy-done | bytes 1146904
  5.6 0.5 %collective-permute-start.8 = (f32[2,8,1088]{2,1,0:T(8,128)S(1)}, f32[2,8,1088]{2,1,0:T(8,128)S(1)}, u32[]{:S(2)}, u32[]{:S(2)}) collective-permute-start(f32[2,8,1088]{2,1,0:T(8,128)S(1)} %get-tuple-element.20), channel_id=1, source_target_pairs={{0,4},{4,0},{8,12},{12,8},{16,20},{20,16},{24,28},{28,24},{1,5},{5... | collective-permute-start | bytes 208904 | tf_op jit(solution)/shard_map/ppermute | solution.py:213
  6.1 0.0 collective-permute-start
  6.1 0.9 %collective-permute-done.8 = f32[2,8,1088]{2,1,0:T(8,128)S(1)} collective-permute-done((f32[2,8,1088]{2,1,0:T(8,128)S(1)}, f32[2,8,1088]{2,1,0:T(8,128)S(1)}, u32[]{:S(2)}, u32[]{:S(2)}) %collective-permute-start.8) | collective-permute-done | bytes 69664 | tf_op jit(solution)/shard_map/ppermute | solution.py:213
  7.0 2.9 %collective-permute-start.9 = (f32[2,8,1088]{2,1,0:T(8,128)S(1)}, f32[2,8,1088]{2,1,0:T(8,128)S(1)}, u32[]{:S(2)}, u32[]{:S(2)}) collective-permute-start(f32[2,8,1088]{2,1,0:T(8,128)S(1)} %add.35), channel_id=1, source_target_pairs={{0,8},{1,9},{2,10},{3,11},{4,5},{5,4},{6,7},{7,6},{8,0},{9,1},{10,... | collective-permute-start | bytes 208904 | tf_op jit(solution)/shard_map/ppermute | solution.py:306
  9.9 0.0 collective-permute-done
  9.9 0.1 collective-permute-start.1
  10.1 2.0 %collective-permute-start.2 = (f32[1,8,1088]{2,1,0:T(8,128)}, f32[1,8,1088]{2,1,0:T(8,128)}, u32[]{:S(2)}, u32[]{:S(2)}) collective-permute-start(f32[1,8,1088]{2,1,0:T(8,128)} %bitcast.7), channel_id=1, source_target_pairs={{0,16},{4,20},{8,24},{12,28},{16,0},{20,4},{24,8},{28,12},{1,17},{... | collective-permute-start | bytes 104456 | tf_op jit(solution)/shard_map/ppermute | solution.py:213
  12.1 0.0 copy-done
  12.1 0.0 copy-start.2
  12.1 1.3 %copy-done.2 = bf16[2240,256]{1,0:T(8,128)(2,1)S(1)} copy-done((bf16[2240,256]{1,0:T(8,128)(2,1)S(1)}, bf16[2240,256]{1,0:T(8,128)(2,1)}, u32[]{:S(2)}) %copy-start.2) | copy-done | bytes 1146904
  13.3 0.4 %input_grad.1 = bf16[2240,256]{1,0:T(8,128)(2,1)S(1)} custom-call(bf16[2240,64]{1,0:T(8,128)(2,1)S(1)} %get-tuple-element.15.back_ref, bf16[2240,256]{1,0:T(8,128)(2,1)S(1)} %copy-done.2, f32[64,1088]{1,0:T(8,128)S(1)} %copy-done), custom_call_target="tpu_custom_call" | custom-call | flops 73400320 | bytes 2580480 | tf_op jit(solution)/shard_map/input_grad/pallas_call | solution.py:286
  13.8 0.0 collective-permute-done.9
  13.8 1.6 %collective-permute-start.10 = (f32[2,8,1088]{2,1,0:T(8,128)S(1)}, f32[2,8,1088]{2,1,0:T(8,128)S(1)}, u32[]{:S(2)}, u32[]{:S(2)}) collective-permute-start(f32[2,8,1088]{2,1,0:T(8,128)S(1)} %add.36), channel_id=1, source_target_pairs={{0,1},{1,0},{2,3},{3,2},{4,12},{5,13},{6,14},{7,15},{8,9},{9,8},{1... | collective-permute-start | bytes 208904 | tf_op jit(solution)/shard_map/ppermute | solution.py:306
  15.4 0.0 collective-permute-done.1
  15.4 0.6 %collective-permute-start.5 = (f32[2,8,1088]{2,1,0:T(8,128)S(1)}, f32[2,8,1088]{2,1,0:T(8,128)S(1)}, u32[]{:S(2)}, u32[]{:S(2)}) collective-permute-start(f32[2,8,1088]{2,1,0:T(8,128)S(1)} %add.31), channel_id=1, source_target_pairs={{0,1},{1,0},{2,3},{3,2},{4,12},{5,13},{6,14},{7,15},{8,9},{9,8},{1... | collective-permute-start | bytes 208904 | tf_op jit(solution)/shard_map/ppermute | solution.py:306
  16.0 0.0 collective-permute-done.2
  16.0 0.8 %fusion.1 = (f32[2,1,8,1088]{3,2,0,1:T(8,128)S(1)}, f32[2,8,1088]{2,1,0:T(8,128)S(1)}) fusion(f32[1,1,8,1088]{3,2,1,0:T(8,128)} %bitcast.8, f32[1,1,8,1088]{3,2,1,0:T(8,128)} %bitcast.6), kind=kLoop, calls=%fused_computation.3 | loop fusion | flops 17408 | bytes 208896 | tf_op jit(solution)/shard_map/stack;reshape | solution.py:301
  16.8 1.5 %collective-permute-start.3 = (f32[2,8,1088]{2,1,0:T(8,128)S(1)}, f32[2,8,1088]{2,1,0:T(8,128)S(1)}, u32[]{:S(2)}, u32[]{:S(2)}) collective-permute-start(f32[2,8,1088]{2,1,0:T(8,128)S(1)} %get-tuple-element.24), channel_id=1, source_target_pairs={{0,8},{4,12},{8,0},{12,4},{16,24},{20,28},{24,16},{28,20},{1,9},{5... | collective-permute-start | bytes 208904 | tf_op jit(solution)/shard_map/ppermute | solution.py:213
  18.3 0.0 collective-permute-done.10
  18.3 0.8 %collective-permute-start.11 = (f32[2,8,1088]{2,1,0:T(8,128)S(1)}, f32[2,8,1088]{2,1,0:T(8,128)S(1)}, u32[]{:S(2)}, u32[]{:S(2)}) collective-permute-start(f32[2,8,1088]{2,1,0:T(8,128)S(1)} %add.37), channel_id=1, source_target_pairs={{0,16},{1,17},{2,18},{3,19},{4,6},{5,7},{6,4},{7,5},{8,24},{9,25},... | collective-permute-start | bytes 208904 | tf_op jit(solution)/shard_map/ppermute | solution.py:306
  19.2 0.7 %collective-permute-done.5 = f32[2,8,1088]{2,1,0:T(8,128)S(1)} collective-permute-done((f32[2,8,1088]{2,1,0:T(8,128)S(1)}, f32[2,8,1088]{2,1,0:T(8,128)S(1)}, u32[]{:S(2)}, u32[]{:S(2)}) %collective-permute-start.5) | collective-permute-done | bytes 69664 | tf_op jit(solution)/shard_map/ppermute | solution.py:306
  19.9 0.6 %collective-permute-start.6 = (f32[2,8,1088]{2,1,0:T(8,128)S(1)}, f32[2,8,1088]{2,1,0:T(8,128)S(1)}, u32[]{:S(2)}, u32[]{:S(2)}) collective-permute-start(f32[2,8,1088]{2,1,0:T(8,128)S(1)} %add.32), channel_id=1, source_target_pairs={{0,16},{1,17},{2,18},{3,19},{4,6},{5,7},{6,4},{7,5},{8,24},{9,25},... | collective-permute-start | bytes 208904 | tf_op jit(solution)/shard_map/ppermute | solution.py:306
  20.5 0.7 %collective-permute-done.3 = f32[2,8,1088]{2,1,0:T(8,128)S(1)} collective-permute-done((f32[2,8,1088]{2,1,0:T(8,128)S(1)}, f32[2,8,1088]{2,1,0:T(8,128)S(1)}, u32[]{:S(2)}, u32[]{:S(2)}) %collective-permute-start.3) | collective-permute-done | bytes 69664 | tf_op jit(solution)/shard_map/ppermute | solution.py:213
  21.3 0.1 collective-permute-start.4
  21.3 1.4 %collective-permute-done.11 = f32[2,8,1088]{2,1,0:T(8,128)S(1)} collective-permute-done((f32[2,8,1088]{2,1,0:T(8,128)S(1)}, f32[2,8,1088]{2,1,0:T(8,128)S(1)}, u32[]{:S(2)}, u32[]{:S(2)}) %collective-permute-start.11) | collective-permute-done | bytes 69664 | tf_op jit(solution)/shard_map/ppermute | solution.py:306
  22.8 2.7 %collective-permute-start.12 = (f32[2,8,1088]{2,1,0:T(8,128)S(1)}, f32[2,8,1088]{2,1,0:T(8,128)S(1)}, u32[]{:S(2)}, u32[]{:S(2)}) collective-permute-start(f32[2,8,1088]{2,1,0:T(8,128)S(1)} %add.38), channel_id=1, source_target_pairs={{0,2},{1,3},{2,0},{3,1},{4,20},{5,21},{6,22},{7,23},{8,10},{9,11},... | collective-permute-start | bytes 208904 | tf_op jit(solution)/shard_map/ppermute | solution.py:306
  25.4 0.0 collective-permute-done.6
  25.4 2.3 %collective-permute-start.7 = (f32[2,8,1088]{2,1,0:T(8,128)S(1)}, f32[2,8,1088]{2,1,0:T(8,128)S(1)}, u32[]{:S(2)}, u32[]{:S(2)}) collective-permute-start(f32[2,8,1088]{2,1,0:T(8,128)S(1)} %add.33), channel_id=1, source_target_pairs={{0,2},{1,3},{2,0},{3,1},{4,20},{5,21},{6,22},{7,23},{8,10},{9,11},... | collective-permute-start | bytes 208904 | tf_op jit(solution)/shard_map/ppermute | solution.py:306
  27.7 0.3 %collective-permute-done.12 = f32[2,8,1088]{2,1,0:T(8,128)S(1)} collective-permute-done((f32[2,8,1088]{2,1,0:T(8,128)S(1)}, f32[2,8,1088]{2,1,0:T(8,128)S(1)}, u32[]{:S(2)}, u32[]{:S(2)}) %collective-permute-start.12) | collective-permute-done | bytes 69664 | tf_op jit(solution)/shard_map/ppermute | solution.py:306
  28.1 0.1 collective-permute-start.14
  28.2 2.6 %collective-permute-done.7 = f32[2,8,1088]{2,1,0:T(8,128)S(1)} collective-permute-done((f32[2,8,1088]{2,1,0:T(8,128)S(1)}, f32[2,8,1088]{2,1,0:T(8,128)S(1)}, u32[]{:S(2)}, u32[]{:S(2)}) %collective-permute-start.7) | collective-permute-done | bytes 69664 | tf_op jit(solution)/shard_map/ppermute | solution.py:306
  30.8 0.1 collective-permute-start.13
  30.9 1.0 %copy.10 = bf16[1,40,56,256]{3,2,1,0:T(8,128)(2,1)} copy(bf16[1,40,56,256]{3,2,1,0:T(8,128)(2,1)S(1)} %bitcast.17) | data formatting | bytes 2293760
  31.9 0.0 collective-permute-done.4.other_speed_ref
  31.9 0.0 collective-permute-done.14.rest_3_
  31.9 0.2 collective-permute-done.13.rest_2_
  32.1 0.9 %update.1 = (f32[8,1088]{1,0:T(8,128)}, f32[8,8,1088]{2,1,0:T(8,128)}) custom-call(s32[1]{0:T(128)} %bitcast.place_ref, f32[4,8,1088]{2,1,0:T(8,128)S(1)} %bitcast.20, f32[4,8,1088]{2,1,0:T(8,128)S(1)} %collective-permute-done.4.other_speed_ref, f32[8,8,1088]{2,1,0:T(8,128)S(1)} %bitcast.18, f32[2,8,1088]{2,1,0:T(8,128)S(1)} %add.34.rest_0_, ...), custom_call_target="tpu_custom_call" | custom-call | tf_op jit(solution)/shard_map/update/pallas_call | solution.py:317
  (12 shorter events, 0.1 us)
Async XLA Ops:
  0.6 11.4 %copy-start = (f32[64,1088]{1,0:T(8,128)S(1)}, f32[64,1088]{1,0:T(8,128)}, u32[]{:S(2)}) copy-start(f32[64,1088]{1,0:T(8,128)} %params_ref.1) | copy-start | bytes 835588
  4.6 1.0 %copy-start.1 = (bf16[2240,256]{1,0:T(8,128)(2,1)}, bf16[2240,256]{1,0:T(8,128)(2,1)S(1)}, u32[]{:S(2)}) copy-start(bf16[2240,256]{1,0:T(8,128)(2,1)S(1)} %get-tuple-element.16.out_ref) | copy-start | bytes 3440644
  5.6 1.4 %collective-permute-start.8 = (f32[2,8,1088]{2,1,0:T(8,128)S(1)}, f32[2,8,1088]{2,1,0:T(8,128)S(1)}, u32[]{:S(2)}, u32[]{:S(2)}) collective-permute-start(f32[2,8,1088]{2,1,0:T(8,128)S(1)} %get-tuple-element.20), channel_id=1, source_target_pairs={{0,4},{4,0},{8,12},{12,8},{16,20},{20,16},{24,28},{28,24},{1,5},{5... | collective-permute-start | bytes 208904 | tf_op jit(solution)/shard_map/ppermute | solution.py:213
  6.1 3.8 %collective-permute-start = (f32[2,8,1088]{2,1,0:T(8,128)S(1)}, f32[2,8,1088]{2,1,0:T(8,128)S(1)}, u32[]{:S(2)}, u32[]{:S(2)}) collective-permute-start(f32[2,8,1088]{2,1,0:T(8,128)S(1)} %get-tuple-element.14), channel_id=1, source_target_pairs={{0,4},{4,0},{8,12},{12,8},{16,20},{20,16},{24,28},{28,24},{1,5},{5... | collective-permute-start | bytes 208904 | tf_op jit(solution)/shard_map/ppermute | solution.py:213
  7.0 6.7 %collective-permute-start.9 = (f32[2,8,1088]{2,1,0:T(8,128)S(1)}, f32[2,8,1088]{2,1,0:T(8,128)S(1)}, u32[]{:S(2)}, u32[]{:S(2)}) collective-permute-start(f32[2,8,1088]{2,1,0:T(8,128)S(1)} %add.35), channel_id=1, source_target_pairs={{0,8},{1,9},{2,10},{3,11},{4,5},{5,4},{6,7},{7,6},{8,0},{9,1},{10,... | collective-permute-start | bytes 208904 | tf_op jit(solution)/shard_map/ppermute | solution.py:306
  9.9 5.5 %collective-permute-start.1 = (f32[2,8,1088]{2,1,0:T(8,128)S(1)}, f32[2,8,1088]{2,1,0:T(8,128)S(1)}, u32[]{:S(2)}, u32[]{:S(2)}) collective-permute-start(f32[2,8,1088]{2,1,0:T(8,128)S(1)} %add.30), channel_id=1, source_target_pairs={{0,8},{1,9},{2,10},{3,11},{4,5},{5,4},{6,7},{7,6},{8,0},{9,1},{10,... | collective-permute-start | bytes 208904 | tf_op jit(solution)/shard_map/ppermute | solution.py:306
  10.1 5.9 %collective-permute-start.2 = (f32[1,8,1088]{2,1,0:T(8,128)}, f32[1,8,1088]{2,1,0:T(8,128)}, u32[]{:S(2)}, u32[]{:S(2)}) collective-permute-start(f32[1,8,1088]{2,1,0:T(8,128)} %bitcast.7), channel_id=1, source_target_pairs={{0,16},{4,20},{8,24},{12,28},{16,0},{20,4},{24,8},{28,12},{1,17},{... | collective-permute-start | bytes 104456 | tf_op jit(solution)/shard_map/ppermute | solution.py:213
  12.1 1.3 %copy-start.2 = (bf16[2240,256]{1,0:T(8,128)(2,1)S(1)}, bf16[2240,256]{1,0:T(8,128)(2,1)}, u32[]{:S(2)}) copy-start(bf16[2240,256]{1,0:T(8,128)(2,1)} %copy-done.1) | copy-start | bytes 3440644
  13.8 4.5 %collective-permute-start.10 = (f32[2,8,1088]{2,1,0:T(8,128)S(1)}, f32[2,8,1088]{2,1,0:T(8,128)S(1)}, u32[]{:S(2)}, u32[]{:S(2)}) collective-permute-start(f32[2,8,1088]{2,1,0:T(8,128)S(1)} %add.36), channel_id=1, source_target_pairs={{0,1},{1,0},{2,3},{3,2},{4,12},{5,13},{6,14},{7,15},{8,9},{9,8},{1... | collective-permute-start | bytes 208904 | tf_op jit(solution)/shard_map/ppermute | solution.py:306
  15.4 4.4 %collective-permute-start.5 = (f32[2,8,1088]{2,1,0:T(8,128)S(1)}, f32[2,8,1088]{2,1,0:T(8,128)S(1)}, u32[]{:S(2)}, u32[]{:S(2)}) collective-permute-start(f32[2,8,1088]{2,1,0:T(8,128)S(1)} %add.31), channel_id=1, source_target_pairs={{0,1},{1,0},{2,3},{3,2},{4,12},{5,13},{6,14},{7,15},{8,9},{9,8},{1... | collective-permute-start | bytes 208904 | tf_op jit(solution)/shard_map/ppermute | solution.py:306
  16.8 4.4 %collective-permute-start.3 = (f32[2,8,1088]{2,1,0:T(8,128)S(1)}, f32[2,8,1088]{2,1,0:T(8,128)S(1)}, u32[]{:S(2)}, u32[]{:S(2)}) collective-permute-start(f32[2,8,1088]{2,1,0:T(8,128)S(1)} %get-tuple-element.24), channel_id=1, source_target_pairs={{0,8},{4,12},{8,0},{12,4},{16,24},{20,28},{24,16},{28,20},{1,9},{5... | collective-permute-start | bytes 208904 | tf_op jit(solution)/shard_map/ppermute | solution.py:213
  18.3 4.4 %collective-permute-start.11 = (f32[2,8,1088]{2,1,0:T(8,128)S(1)}, f32[2,8,1088]{2,1,0:T(8,128)S(1)}, u32[]{:S(2)}, u32[]{:S(2)}) collective-permute-start(f32[2,8,1088]{2,1,0:T(8,128)S(1)} %add.37), channel_id=1, source_target_pairs={{0,16},{1,17},{2,18},{3,19},{4,6},{5,7},{6,4},{7,5},{8,24},{9,25},... | collective-permute-start | bytes 208904 | tf_op jit(solution)/shard_map/ppermute | solution.py:306
  19.9 5.6 %collective-permute-start.6 = (f32[2,8,1088]{2,1,0:T(8,128)S(1)}, f32[2,8,1088]{2,1,0:T(8,128)S(1)}, u32[]{:S(2)}, u32[]{:S(2)}) collective-permute-start(f32[2,8,1088]{2,1,0:T(8,128)S(1)} %add.32), channel_id=1, source_target_pairs={{0,16},{1,17},{2,18},{3,19},{4,6},{5,7},{6,4},{7,5},{8,24},{9,25},... | collective-permute-start | bytes 208904 | tf_op jit(solution)/shard_map/ppermute | solution.py:306
  21.3 10.6 %collective-permute-start.4 = (f32[4,8,1088]{2,1,0:T(8,128)S(1)}, f32[4,8,1088]{2,1,0:T(8,128)S(1)}, u32[]{:S(2)}, u32[]{:S(2)}) collective-permute-start(f32[4,8,1088]{2,1,0:T(8,128)S(1)} %bitcast.19), channel_id=1, source_target_pairs={{0,4},{4,0},{8,12},{12,8},{16,20},{20,16},{24,28},{28,24},{1,5},{5... | collective-permute-start | bytes 417800 | tf_op jit(solution)/shard_map/ppermute | solution.py:213
  22.8 5.3 %collective-permute-start.12 = (f32[2,8,1088]{2,1,0:T(8,128)S(1)}, f32[2,8,1088]{2,1,0:T(8,128)S(1)}, u32[]{:S(2)}, u32[]{:S(2)}) collective-permute-start(f32[2,8,1088]{2,1,0:T(8,128)S(1)} %add.38), channel_id=1, source_target_pairs={{0,2},{1,3},{2,0},{3,1},{4,20},{5,21},{6,22},{7,23},{8,10},{9,11},... | collective-permute-start | bytes 208904 | tf_op jit(solution)/shard_map/ppermute | solution.py:306
  25.4 5.3 %collective-permute-start.7 = (f32[2,8,1088]{2,1,0:T(8,128)S(1)}, f32[2,8,1088]{2,1,0:T(8,128)S(1)}, u32[]{:S(2)}, u32[]{:S(2)}) collective-permute-start(f32[2,8,1088]{2,1,0:T(8,128)S(1)} %add.33), channel_id=1, source_target_pairs={{0,2},{1,3},{2,0},{3,1},{4,20},{5,21},{6,22},{7,23},{8,10},{9,11},... | collective-permute-start | bytes 208904 | tf_op jit(solution)/shard_map/ppermute | solution.py:306
  28.1 3.8 %collective-permute-start.14 = (f32[2,8,1088]{2,1,0:T(8,128)S(1)}, f32[2,8,1088]{2,1,0:T(8,128)S(1)}, u32[]{:S(2)}, u32[]{:S(2)}) collective-permute-start(f32[2,8,1088]{2,1,0:T(8,128)S(1)} %add.39.rest_1_), channel_id=1, source_target_pairs={{0,4},{4,0},{8,12},{12,8},{16,20},{20,16},{24,28},{28,24},{1,5},{5... | collective-permute-start | bytes 208904 | tf_op jit(solution)/shard_map/ppermute | solution.py:213
  30.8 1.3 %collective-permute-start.13 = (f32[2,8,1088]{2,1,0:T(8,128)S(1)}, f32[2,8,1088]{2,1,0:T(8,128)S(1)}, u32[]{:S(2)}, u32[]{:S(2)}) collective-permute-start(f32[2,8,1088]{2,1,0:T(8,128)S(1)} %add.34.rest_0_), channel_id=1, source_target_pairs={{0,4},{4,0},{8,12},{12,8},{16,20},{20,16},{24,28},{28,24},{1,5},{5... | collective-permute-start | bytes 208904 | tf_op jit(solution)/shard_map/ppermute | solution.py:213

commit v7 on v6

--- a/solution.py
+++ b/solution.py
@@ -247,7 +247,6 @@
     halves = group // 2
     strips = group * depth
     place = lax.axis_index("gx").reshape(1)
-    out_flat = out_grad.reshape(pixels, c_in)
     step = divisor_up_to(height, 8) * width
     streams = 2 if halves % 2 == 0 else 1
     part = pltpu.VMEM((halves // streams, rows, row), F32)
@@ -273,14 +272,20 @@
             for shape in ((step, 2 * mid), (step, 2 * mid), (step + 16, 2 * mid), (step, 4 * mid))
             for _ in range(pixels // step)
         ],
+        compiler_params=pltpu.CompilerParams(vmem_limit_bytes=28 << 20),
         name="grads",
     )(
         place,
-        block_input.reshape(pixels, c_in),
-        mid_first.reshape(height, width * mid),
-        mid_second.reshape(height, width * mid),
-        out_flat,
-        params,
+        *(
+            pltpu.with_memory_space_constraint(operand, pltpu.HBM)
+            for operand in (
+                block_input.reshape(pixels, c_in),
+                mid_first.reshape(height, width * mid),
+                mid_second.reshape(height, width * mid),
+                out_grad.reshape(pixels, c_in),
+                params,
+            )
+        ),
     )
 
     input_grad = pl.pallas_call(
@@ -291,6 +296,7 @@
         cost_estimate=pl.CostEstimate(
             flops=2 * pixels * mid * c_in, bytes_accessed=2 * pixels * (2 * c_in + mid), transcendentals=0
         ),
+        compiler_params=pltpu.CompilerParams(vmem_limit_bytes=8 << 20),
         name="input_grad",
     )(*in_vmem(back_first, out_near, params))
 
@@ -322,6 +328,7 @@
         ),
         in_specs=[pl.BlockSpec(memory_space=pltpu.SMEM)] + full_vmem(3 + 2 * streams),
         out_specs=tuple(full_vmem(2)),
+        compiler_params=pltpu.CompilerParams(vmem_limit_bytes=8 << 20),
         name="update",
     )(place, *in_vmem(speeds, other_speeds, params.reshape(group, rows, row), *totals, *others))
     return (input_grad.reshape(1, height, width, c_in), new_velocity, next_weights.reshape(mid, row))

time: 33.3 us -> 31.5 us (0.946)
  starting transfers between devices: 15.9 us -> 19.2 us
  waiting for transfers between devices: 6.88 us -> 4.53 us
  local copies, waits for them, and re-layouts: 3.28 us -> 1.02 us
  other arithmetic: 0.91 us -> 0.13 us
    ppermute x8, starting transfers between devices: 11.7 us -> 15.6 us  [shards(): lax.ppermute(total, ('gx', 'gy'), table)]
    unnamed x7 -> x5, local copies, waits for them, and re-layouts: 3.26 us -> 1.01 us
    ppermute x8, waiting for transfers between devices: 5.02 us -> 3.45 us  [shards(): lax.ppermute(total, ('gx', 'gy'), table)]
    another operation x2, other arithmetic: 0.81 us -> 0.02 us  [shards(): jnp.stack([speeds, flip(speeds, 'gx', bit)], axis=1).reshape(-1, rows, row)]
    ppermute x7, waiting for transfers between devices: 1.86 us -> 1.09 us  [flip(): lax.ppermute(value, axis, [(i, i ^ bit) for i in range(lax.axis_size(axis...]
    ppermute x7, starting transfers between devices: 4.21 us -> 3.6 us  [flip(): lax.ppermute(value, axis, [(i, i ^ bit) for i in range(lax.axis_size(axis...]
  transfers between devices with their start and end apart: 15 -> 15, of which waited for: 7 -> 6; matrix products, arithmetic and copies ran while one was open for 6% -> 4% of each run, Pallas kernels for 1% -> 1%
where the time goes in v7:
time: 31.5 us; the launch traced here: 31.1 us
  starting transfers between devices  19.2 us (61%)
  Pallas kernels  5.39 us (17%)
  waiting for transfers between devices  4.53 us (14%)
  local copies, waits for them, and re-layouts  1.02 us (3%)
  between operations  0.76 us (2%)
    ppermute x8, starting transfers between devices, shards(): lax.ppermute(total, ('gx', 'gy'), table)  15.6 us
    pallas_call x1, Pallas kernels, shards(): pl.pallas_call(functools.partial(grad_kernel, height=height, width=width,...  4.02 us
    ppermute x7, starting transfers between devices, flip(): lax.ppermute(value, axis, [(i, i ^ bit) for i in range(lax.axis_size(axis...  3.6 us
    ppermute x8, waiting for transfers between devices, shards(): lax.ppermute(total, ('gx', 'gy'), table)  3.45 us
    ppermute x7, waiting for transfers between devices, flip(): lax.ppermute(value, axis, [(i, i ^ bit) for i in range(lax.axis_size(axis...  1.09 us
    unnamed x5, local copies, waits for them, and re-layouts  1.01 us
    pallas_call x1, Pallas kernels, shards(): pl.pallas_call(functools.partial(update_kernel, c_in=c_in, mid=mid), out_...  0.93 us
  transfers between devices with their start and end apart: 15, of which 6 were waited for; matrix products, arithmetic and copies ran while one was open for 4% of the time, Pallas kernels for 1%

profile of v7, /device:TPU:0, one launch (start us, length us, event | category | flops | bytes accessed | tf_op | source)
XLA Modules:
  0.0 31.1 jit_solution(9122596827757752506)
XLA Ops:
  0.6 0.0 copy-start.1
  0.6 0.0 copy-start
  0.7 4.0 %grads.1 = (bf16[2240,64]{1,0:T(8,128)(2,1)S(1)}, bf16[2240,256]{1,0:T(8,128)(2,1)S(1)}, f32[2,8,1088]{2,1,0:T(8,128)S(1)}, f32[2,8,1088]{2,1,0:T(8,128)S(1)}, f...) custom-call(s32[1]{0:T(128)} %bitcast.place_ref, bf16[2240,256]{1,0:T(8,128)(2,1)} %bitcast.21, ...), custom_call_target="tpu_custom_call" | custom-call | tf_op jit(solution)/shard_map/grads/pallas_call | solution.py:254
  4.7 0.6 %collective-permute-start.8 = (f32[2,8,1088]{2,1,0:T(8,128)S(1)}, f32[2,8,1088]{2,1,0:T(8,128)S(1)}, u32[]{:S(2)}, u32[]{:S(2)}) collective-permute-start(f32[2,8,1088]{2,1,0:T(8,128)S(1)} %get-tuple-element.20), channel_id=1, source_target_pairs={{0,4},{4,0},{8,12},{12,8},{16,20},{20,16},{24,28},{28,24},{1,5},{5... | collective-permute-start | bytes 208904 | tf_op jit(solution)/shard_map/ppermute | solution.py:213
  5.2 0.1 collective-permute-start
  5.3 0.8 %collective-permute-done.8 = f32[2,8,1088]{2,1,0:T(8,128)S(1)} collective-permute-done((f32[2,8,1088]{2,1,0:T(8,128)S(1)}, f32[2,8,1088]{2,1,0:T(8,128)S(1)}, u32[]{:S(2)}, u32[]{:S(2)}) %collective-permute-start.8) | collective-permute-done | bytes 69664 | tf_op jit(solution)/shard_map/ppermute | solution.py:213
  6.2 2.9 %collective-permute-start.9 = (f32[2,8,1088]{2,1,0:T(8,128)S(1)}, f32[2,8,1088]{2,1,0:T(8,128)S(1)}, u32[]{:S(2)}, u32[]{:S(2)}) collective-permute-start(f32[2,8,1088]{2,1,0:T(8,128)S(1)} %add.35), channel_id=1, source_target_pairs={{0,8},{1,9},{2,10},{3,11},{4,5},{5,4},{6,7},{7,6},{8,0},{9,1},{10,... | collective-permute-start | bytes 208904 | tf_op jit(solution)/shard_map/ppermute | solution.py:312
  9.1 0.0 collective-permute-done
  9.1 0.1 collective-permute-start.1
  9.2 0.0 copy-done.1
  9.2 2.0 %collective-permute-start.2 = (f32[1,8,1088]{2,1,0:T(8,128)S(1)}, f32[1,8,1088]{2,1,0:T(8,128)S(1)}, u32[]{:S(2)}, u32[]{:S(2)}) collective-permute-start(f32[1,8,1088]{2,1,0:T(8,128)S(1)} %bitcast.26), channel_id=1, source_target_pairs={{0,16},{4,20},{8,24},{12,28},{16,0},{20,4},{24,8},{28,12},{1,17},{... | collective-permute-start | bytes 104456 | tf_op jit(solution)/shard_map/ppermute | solution.py:213
  11.2 0.0 copy-done
  11.2 0.4 %input_grad.1 = bf16[2240,256]{1,0:T(8,128)(2,1)S(1)} custom-call(bf16[2240,64]{1,0:T(8,128)(2,1)S(1)} %get-tuple-element.15.back_ref, bf16[2240,256]{1,0:T(8,128)(2,1)S(1)} %get-tuple-element.16.out_ref, f32[64,1088]{1,0:T(8,128)S(1)} %copy-done), custom_call_target="tpu_custom_call" | custom-call | flops 73400320 | bytes 2580480 | tf_op jit(solution)/shard_map/input_grad/pallas_call | solution.py:291
  11.7 0.0 collective-permute-done.9
  11.7 1.9 %collective-permute-start.10 = (f32[2,8,1088]{2,1,0:T(8,128)S(1)}, f32[2,8,1088]{2,1,0:T(8,128)S(1)}, u32[]{:S(2)}, u32[]{:S(2)}) collective-permute-start(f32[2,8,1088]{2,1,0:T(8,128)S(1)} %add.36), channel_id=1, source_target_pairs={{0,1},{1,0},{2,3},{3,2},{4,12},{5,13},{6,14},{7,15},{8,9},{9,8},{1... | collective-permute-start | bytes 208904 | tf_op jit(solution)/shard_map/ppermute | solution.py:312
  13.6 0.0 collective-permute-done.1
  13.6 1.6 %collective-permute-start.5 = (f32[2,8,1088]{2,1,0:T(8,128)S(1)}, f32[2,8,1088]{2,1,0:T(8,128)S(1)}, u32[]{:S(2)}, u32[]{:S(2)}) collective-permute-start(f32[2,8,1088]{2,1,0:T(8,128)S(1)} %add.31), channel_id=1, source_target_pairs={{0,1},{1,0},{2,3},{3,2},{4,12},{5,13},{6,14},{7,15},{8,9},{9,8},{1... | collective-permute-start | bytes 208904 | tf_op jit(solution)/shard_map/ppermute | solution.py:312
  15.2 0.0 collective-permute-done.2
  15.2 0.8 %collective-permute-start.3 = (f32[2,8,1088]{2,1,0:T(8,128)S(1)}, f32[2,8,1088]{2,1,0:T(8,128)S(1)}, u32[]{:S(2)}, u32[]{:S(2)}) collective-permute-start(f32[2,8,1088]{2,1,0:T(8,128)S(1)} %get-tuple-element.24), channel_id=1, source_target_pairs={{0,8},{4,12},{8,0},{12,4},{16,24},{20,28},{24,16},{28,20},{1,9},{5... | collective-permute-start | bytes 208904 | tf_op jit(solution)/shard_map/ppermute | solution.py:213
  15.9 0.2 collective-permute-done.10
  16.1 1.8 %collective-permute-start.11 = (f32[2,8,1088]{2,1,0:T(8,128)S(1)}, f32[2,8,1088]{2,1,0:T(8,128)S(1)}, u32[]{:S(2)}, u32[]{:S(2)}) collective-permute-start(f32[2,8,1088]{2,1,0:T(8,128)S(1)} %add.37), channel_id=1, source_target_pairs={{0,16},{1,17},{2,18},{3,19},{4,6},{5,7},{6,4},{7,5},{8,24},{9,25},... | collective-permute-start | bytes 208904 | tf_op jit(solution)/shard_map/ppermute | solution.py:312
  18.0 0.1 collective-permute-done.5
  18.0 2.4 %collective-permute-start.6 = (f32[2,8,1088]{2,1,0:T(8,128)S(1)}, f32[2,8,1088]{2,1,0:T(8,128)S(1)}, u32[]{:S(2)}, u32[]{:S(2)}) collective-permute-start(f32[2,8,1088]{2,1,0:T(8,128)S(1)} %add.32), channel_id=1, source_target_pairs={{0,16},{1,17},{2,18},{3,19},{4,6},{5,7},{6,4},{7,5},{8,24},{9,25},... | collective-permute-start | bytes 208904 | tf_op jit(solution)/shard_map/ppermute | solution.py:312
  20.4 0.0 collective-permute-done.3
  20.4 0.1 collective-permute-start.4
  20.5 0.0 collective-permute-done.11
  20.5 2.9 %collective-permute-start.12 = (f32[2,8,1088]{2,1,0:T(8,128)S(1)}, f32[2,8,1088]{2,1,0:T(8,128)S(1)}, u32[]{:S(2)}, u32[]{:S(2)}) collective-permute-start(f32[2,8,1088]{2,1,0:T(8,128)S(1)} %add.38), channel_id=1, source_target_pairs={{0,2},{1,3},{2,0},{3,1},{4,20},{5,21},{6,22},{7,23},{8,10},{9,11},... | collective-permute-start | bytes 208904 | tf_op jit(solution)/shard_map/ppermute | solution.py:312
  23.5 0.0 collective-permute-done.6
  23.5 2.0 %collective-permute-start.7 = (f32[2,8,1088]{2,1,0:T(8,128)S(1)}, f32[2,8,1088]{2,1,0:T(8,128)S(1)}, u32[]{:S(2)}, u32[]{:S(2)}) collective-permute-start(f32[2,8,1088]{2,1,0:T(8,128)S(1)} %add.33), channel_id=1, source_target_pairs={{0,2},{1,3},{2,0},{3,1},{4,20},{5,21},{6,22},{7,23},{8,10},{9,11},... | collective-permute-start | bytes 208904 | tf_op jit(solution)/shard_map/ppermute | solution.py:312
  25.5 0.4 %collective-permute-done.12 = f32[2,8,1088]{2,1,0:T(8,128)S(1)} collective-permute-done((f32[2,8,1088]{2,1,0:T(8,128)S(1)}, f32[2,8,1088]{2,1,0:T(8,128)S(1)}, u32[]{:S(2)}, u32[]{:S(2)}) %collective-permute-start.12) | collective-permute-done | bytes 69664 | tf_op jit(solution)/shard_map/ppermute | solution.py:312
  25.9 0.1 collective-permute-start.14
  26.0 2.8 %collective-permute-done.7 = f32[2,8,1088]{2,1,0:T(8,128)S(1)} collective-permute-done((f32[2,8,1088]{2,1,0:T(8,128)S(1)}, f32[2,8,1088]{2,1,0:T(8,128)S(1)}, u32[]{:S(2)}, u32[]{:S(2)}) %collective-permute-start.7) | collective-permute-done | bytes 69664 | tf_op jit(solution)/shard_map/ppermute | solution.py:312
  28.8 0.1 collective-permute-start.13
  28.9 1.0 %copy.10 = bf16[1,40,56,256]{3,2,1,0:T(8,128)(2,1)} copy(bf16[1,40,56,256]{3,2,1,0:T(8,128)(2,1)S(1)} %bitcast.17) | data formatting | bytes 2293760
  29.9 0.0 collective-permute-done.4.other_speed_ref
  29.9 0.0 collective-permute-done.14.rest_3_
  29.9 0.2 collective-permute-done.13.rest_2_
  30.1 0.9 %update.1 = (f32[8,1088]{1,0:T(8,128)}, f32[8,8,1088]{2,1,0:T(8,128)}) custom-call(s32[1]{0:T(128)} %bitcast.place_ref, f32[4,8,1088]{2,1,0:T(8,128)S(1)} %bitcast.20, f32[4,8,1088]{2,1,0:T(8,128)S(1)} %collective-permute-done.4.other_speed_ref, f32[8,8,1088]{2,1,0:T(8,128)S(1)} %bitcast.18, f32[2,8,1088]{2,1,0:T(8,128)S(1)} %add.34.rest_0_, ...), custom_call_target="tpu_custom_call" | custom-call | tf_op jit(solution)/shard_map/update/pallas_call | solution.py:323
  (13 shorter events, 0.1 us)
Async XLA Ops:
  0.6 8.6 %copy-start.1 = (f32[8,1088]{1,0:T(8,128)S(1)}, f32[8,1088]{1,0:T(8,128)}, u32[]{:S(2)}) copy-start(f32[8,1088]{1,0:T(8,128)} %param.11) | copy-start | bytes 104452
  0.6 10.6 %copy-start = (f32[64,1088]{1,0:T(8,128)S(1)}, f32[64,1088]{1,0:T(8,128)}, u32[]{:S(2)}) copy-start(f32[64,1088]{1,0:T(8,128)} %params_ref.1) | copy-start | bytes 835588
  4.7 1.5 %collective-permute-start.8 = (f32[2,8,1088]{2,1,0:T(8,128)S(1)}, f32[2,8,1088]{2,1,0:T(8,128)S(1)}, u32[]{:S(2)}, u32[]{:S(2)}) collective-permute-start(f32[2,8,1088]{2,1,0:T(8,128)S(1)} %get-tuple-element.20), channel_id=1, source_target_pairs={{0,4},{4,0},{8,12},{12,8},{16,20},{20,16},{24,28},{28,24},{1,5},{5... | collective-permute-start | bytes 208904 | tf_op jit(solution)/shard_map/ppermute | solution.py:213
  5.2 3.8 %collective-permute-start = (f32[2,8,1088]{2,1,0:T(8,128)S(1)}, f32[2,8,1088]{2,1,0:T(8,128)S(1)}, u32[]{:S(2)}, u32[]{:S(2)}) collective-permute-start(f32[2,8,1088]{2,1,0:T(8,128)S(1)} %get-tuple-element.14), channel_id=1, source_target_pairs={{0,4},{4,0},{8,12},{12,8},{16,20},{20,16},{24,28},{28,24},{1,5},{5... | collective-permute-start | bytes 208904 | tf_op jit(solution)/shard_map/ppermute | solution.py:213
  6.2 5.5 %collective-permute-start.9 = (f32[2,8,1088]{2,1,0:T(8,128)S(1)}, f32[2,8,1088]{2,1,0:T(8,128)S(1)}, u32[]{:S(2)}, u32[]{:S(2)}) collective-permute-start(f32[2,8,1088]{2,1,0:T(8,128)S(1)} %add.35), channel_id=1, source_target_pairs={{0,8},{1,9},{2,10},{3,11},{4,5},{5,4},{6,7},{7,6},{8,0},{9,1},{10,... | collective-permute-start | bytes 208904 | tf_op jit(solution)/shard_map/ppermute | solution.py:312
  9.1 4.5 %collective-permute-start.1 = (f32[2,8,1088]{2,1,0:T(8,128)S(1)}, f32[2,8,1088]{2,1,0:T(8,128)S(1)}, u32[]{:S(2)}, u32[]{:S(2)}) collective-permute-start(f32[2,8,1088]{2,1,0:T(8,128)S(1)} %add.30), channel_id=1, source_target_pairs={{0,8},{1,9},{2,10},{3,11},{4,5},{5,4},{6,7},{7,6},{8,0},{9,1},{10,... | collective-permute-start | bytes 208904 | tf_op jit(solution)/shard_map/ppermute | solution.py:312
  9.2 5.9 %collective-permute-start.2 = (f32[1,8,1088]{2,1,0:T(8,128)S(1)}, f32[1,8,1088]{2,1,0:T(8,128)S(1)}, u32[]{:S(2)}, u32[]{:S(2)}) collective-permute-start(f32[1,8,1088]{2,1,0:T(8,128)S(1)} %bitcast.26), channel_id=1, source_target_pairs={{0,16},{4,20},{8,24},{12,28},{16,0},{20,4},{24,8},{28,12},{1,17},{... | collective-permute-start | bytes 104456 | tf_op jit(solution)/shard_map/ppermute | solution.py:213
  11.7 4.4 %collective-permute-start.10 = (f32[2,8,1088]{2,1,0:T(8,128)S(1)}, f32[2,8,1088]{2,1,0:T(8,128)S(1)}, u32[]{:S(2)}, u32[]{:S(2)}) collective-permute-start(f32[2,8,1088]{2,1,0:T(8,128)S(1)} %add.36), channel_id=1, source_target_pairs={{0,1},{1,0},{2,3},{3,2},{4,12},{5,13},{6,14},{7,15},{8,9},{9,8},{1... | collective-permute-start | bytes 208904 | tf_op jit(solution)/shard_map/ppermute | solution.py:312
  13.6 4.4 %collective-permute-start.5 = (f32[2,8,1088]{2,1,0:T(8,128)S(1)}, f32[2,8,1088]{2,1,0:T(8,128)S(1)}, u32[]{:S(2)}, u32[]{:S(2)}) collective-permute-start(f32[2,8,1088]{2,1,0:T(8,128)S(1)} %add.31), channel_id=1, source_target_pairs={{0,1},{1,0},{2,3},{3,2},{4,12},{5,13},{6,14},{7,15},{8,9},{9,8},{1... | collective-permute-start | bytes 208904 | tf_op jit(solution)/shard_map/ppermute | solution.py:312
  15.2 5.2 %collective-permute-start.3 = (f32[2,8,1088]{2,1,0:T(8,128)S(1)}, f32[2,8,1088]{2,1,0:T(8,128)S(1)}, u32[]{:S(2)}, u32[]{:S(2)}) collective-permute-start(f32[2,8,1088]{2,1,0:T(8,128)S(1)} %get-tuple-element.24), channel_id=1, source_target_pairs={{0,8},{4,12},{8,0},{12,4},{16,24},{20,28},{24,16},{28,20},{1,9},{5... | collective-permute-start | bytes 208904 | tf_op jit(solution)/shard_map/ppermute | solution.py:213
  16.1 4.4 %collective-permute-start.11 = (f32[2,8,1088]{2,1,0:T(8,128)S(1)}, f32[2,8,1088]{2,1,0:T(8,128)S(1)}, u32[]{:S(2)}, u32[]{:S(2)}) collective-permute-start(f32[2,8,1088]{2,1,0:T(8,128)S(1)} %add.37), channel_id=1, source_target_pairs={{0,16},{1,17},{2,18},{3,19},{4,6},{5,7},{6,4},{7,5},{8,24},{9,25},... | collective-permute-start | bytes 208904 | tf_op jit(solution)/shard_map/ppermute | solution.py:312
  18.0 5.4 %collective-permute-start.6 = (f32[2,8,1088]{2,1,0:T(8,128)S(1)}, f32[2,8,1088]{2,1,0:T(8,128)S(1)}, u32[]{:S(2)}, u32[]{:S(2)}) collective-permute-start(f32[2,8,1088]{2,1,0:T(8,128)S(1)} %add.32), channel_id=1, source_target_pairs={{0,16},{1,17},{2,18},{3,19},{4,6},{5,7},{6,4},{7,5},{8,24},{9,25},... | collective-permute-start | bytes 208904 | tf_op jit(solution)/shard_map/ppermute | solution.py:312
  20.4 9.5 %collective-permute-start.4 = (f32[4,8,1088]{2,1,0:T(8,128)S(1)}, f32[4,8,1088]{2,1,0:T(8,128)S(1)}, u32[]{:S(2)}, u32[]{:S(2)}) collective-permute-start(f32[4,8,1088]{2,1,0:T(8,128)S(1)} %bitcast.19), channel_id=1, source_target_pairs={{0,4},{4,0},{8,12},{12,8},{16,20},{20,16},{24,28},{28,24},{1,5},{5... | collective-permute-start | bytes 417800 | tf_op jit(solution)/shard_map/ppermute | solution.py:213
  20.5 5.3 %collective-permute-start.12 = (f32[2,8,1088]{2,1,0:T(8,128)S(1)}, f32[2,8,1088]{2,1,0:T(8,128)S(1)}, u32[]{:S(2)}, u32[]{:S(2)}) collective-permute-start(f32[2,8,1088]{2,1,0:T(8,128)S(1)} %add.38), channel_id=1, source_target_pairs={{0,2},{1,3},{2,0},{3,1},{4,20},{5,21},{6,22},{7,23},{8,10},{9,11},... | collective-permute-start | bytes 208904 | tf_op jit(solution)/shard_map/ppermute | solution.py:312
  23.5 5.3 %collective-permute-start.7 = (f32[2,8,1088]{2,1,0:T(8,128)S(1)}, f32[2,8,1088]{2,1,0:T(8,128)S(1)}, u32[]{:S(2)}, u32[]{:S(2)}) collective-permute-start(f32[2,8,1088]{2,1,0:T(8,128)S(1)} %add.33), channel_id=1, source_target_pairs={{0,2},{1,3},{2,0},{3,1},{4,20},{5,21},{6,22},{7,23},{8,10},{9,11},... | collective-permute-start | bytes 208904 | tf_op jit(solution)/shard_map/ppermute | solution.py:312
  25.9 4.0 %collective-permute-start.14 = (f32[2,8,1088]{2,1,0:T(8,128)S(1)}, f32[2,8,1088]{2,1,0:T(8,128)S(1)}, u32[]{:S(2)}, u32[]{:S(2)}) collective-permute-start(f32[2,8,1088]{2,1,0:T(8,128)S(1)} %add.39.rest_1_), channel_id=1, source_target_pairs={{0,4},{4,0},{8,12},{12,8},{16,20},{20,16},{24,28},{28,24},{1,5},{5... | collective-permute-start | bytes 208904 | tf_op jit(solution)/shard_map/ppermute | solution.py:213
  28.8 1.3 %collective-permute-start.13 = (f32[2,8,1088]{2,1,0:T(8,128)S(1)}, f32[2,8,1088]{2,1,0:T(8,128)S(1)}, u32[]{:S(2)}, u32[]{:S(2)}) collective-permute-start(f32[2,8,1088]{2,1,0:T(8,128)S(1)} %add.34.rest_0_), channel_id=1, source_target_pairs={{0,4},{4,0},{8,12},{12,8},{16,20},{20,16},{24,28},{28,24},{1,5},{5... | collective-permute-start | bytes 208904 | tf_op jit(solution)/shard_map/ppermute | solution.py:213

commit v8 on v7

--- a/solution.py
+++ b/solution.py
@@ -26,27 +26,27 @@
 
 def grad_kernel(
     place_ref, x_hbm, first_hbm, second_hbm, out_hbm, params_hbm,
-    back_ref, out_ref, *rest, height, width, strips, rows, streams,
+    back_ref, out_ref, params_ref, *rest, height, width, strips, rows, streams,
 ):
     keep_refs, send_refs, rest = rest[:streams], rest[streams : 2 * streams], rest[2 * streams :]
-    x_ref, first_ref, second_ref, params_ref, bs_cols, first_rows, second_bf, taps_ref, arrived, *blocks = rest
+    x_ref, first_ref, second_ref, bs_cols, first_rows, taps_ref, arrived, *blocks = rest
     count = len(blocks) // 4
     second_px, first_px, bs_px, spread_px = (blocks[n * count : (n + 1) * count] for n in range(4))
     moves = [
         pltpu.make_async_copy(source, target, arrived.at[n])
         for n, (source, target) in enumerate(
             (
+                (params_hbm, params_ref),
                 (second_hbm, second_ref),
                 (first_hbm, first_ref),
-                (params_hbm, params_ref),
                 (out_hbm, out_ref),
                 (x_hbm, x_ref),
             )
         )
     ]
-    for move in moves:
+    for move in moves[:-1]:
         move.start()
-    got_second, got_first, got_params, got_out, got_x = moves
+    got_params, got_second, got_first, got_out, got_x = moves
     c_in = x_ref.shape[1]
     mid = params_ref.shape[0]
     pixels = height * width
@@ -60,8 +60,18 @@
     column = lax.broadcasted_iota(jnp.int32, (step, 2 * mid), 0) % width
 
     taps_ref[...] = jnp.zeros_like(taps_ref)
+    got_params.wait()
+    w_third = params_ref[:, c_in + 9 * mid :].astype(BF16)
+    w_third = jnp.concatenate([w_third, w_third], axis=0)
+    for r in range(3):
+        for q in range(3):
+            t = 3 * r + q
+            taps_ref[q * mid : (q + 1) * mid, r * mid : (r + 1) * mid] = params_ref[
+                :, c_in + t * mid : c_in + (t + 1) * mid
+            ].astype(BF16)
     got_second.wait()
     got_first.wait()
+    got_x.start()
 
     def to_pixels(number):
         for ref, px in ((second_ref, second_px[number]), (first_ref, first_px[number])):
@@ -76,14 +86,13 @@
     def enter(number):
         c = chunks[number]
         second = second_px[number][...]
-        second_bf[c, :] = second[:, :mid].astype(BF16)
         back = lax.dot_general(out_ref[c, :], w_third, (((1,), (1,)), ((), ())), preferred_element_type=F32)
         here = jnp.where(second > 0, back * s_three, 0.0)
         px = bs_px[number]
         px[pad : pad + step, :] = here
         after = jnp.where(column < width - 1, px[pad + 1 : pad + 1 + step, :], 0.0)
         before = jnp.where(column > 0, px[pad - 1 : pad - 1 + step, :], 0.0)
-        cols = jnp.concatenate([jnp.where(low, after, here), before], axis=1).astype(BF16)
+        cols = jnp.concatenate([jnp.where(low, after, here), jnp.where(low, before, second)], axis=1).astype(BF16)
         bs_cols[c, :] = cols
         spread_px[number][...] = jnp.dot(cols, taps_ref[...], preferred_element_type=F32)
 
@@ -112,30 +121,14 @@
     for number in range(len(chunks)):
         to_pixels(number)
     got_out.wait()
-    got_x.wait()
-    got_params.wait()
-    w_third = params_ref[:, c_in + 9 * mid :].astype(BF16)
-    w_third = jnp.concatenate([w_third, w_third], axis=0)
-    for r in range(3):
-        for q in range(3):
-            t = 3 * r + q
-            taps_ref[q * mid : (q + 1) * mid, r * mid : (r + 1) * mid] = params_ref[
-                :, c_in + t * mid : c_in + (t + 1) * mid
-            ].astype(BF16)
     for number in range(len(chunks)):
         enter(number)
         if number:
             leave(number - 1)
     leave(len(chunks) - 1)
 
-    spans = [slice(0, pixels)]
-
-    def outer(left, wide, right):
-        terms = [
-            lax.dot_general(left[k, :wide], right[k, :], (((0,), (0,)), ((), ())), preferred_element_type=F32)
-            for k in spans
-        ]
-        return sum(terms[1:], terms[0])
+    def outer(turned, right):
+        return jnp.dot(turned, right, preferred_element_type=F32)
 
     even = place_ref[0] % 2 == 0
 
@@ -148,12 +141,14 @@
             keep_refs[stream][tile, :, columns] = jnp.where(even, one, two)
             send_refs[stream][tile, :, columns] = jnp.where(even, two, one)
 
-    put(outer(second_bf, mid, out_ref) * (s_three / strips), c_in + 9 * mid)
-    grad_two = outer(bs_cols, 3 * mid, first_rows) * (s_two / strips)
+    got_x.wait()
+    turned = bs_cols[...].T
+    put(outer(turned[3 * mid :], out_ref[...]) * (s_three / strips), c_in + 9 * mid)
+    grad_two = outer(turned[: 3 * mid], first_rows[...]) * (s_two / strips)
     for r in range(3):
         for q in range(3):
             put(grad_two[q * mid : (q + 1) * mid, r * mid : (r + 1) * mid], c_in + (3 * r + q) * mid)
-    put(outer(back_ref, mid, x_ref) * (s_one / strips), 0)
+    put(outer(back_ref[...].T, x_ref[...]) * (s_one / strips), 0)
 
 
 def input_grad_kernel(back_ref, out_ref, params_ref, result_ref):
@@ -251,19 +246,17 @@
     streams = 2 if halves % 2 == 0 else 1
     part = pltpu.VMEM((halves // streams, rows, row), F32)
 
-    back_first, out_near, *parts = pl.pallas_call(
+    back_first, out_near, params_near, *parts = pl.pallas_call(
         functools.partial(grad_kernel, height=height, width=width, strips=strips, rows=rows, streams=streams),
-        out_shape=(pltpu.VMEM((pixels, mid), BF16), pltpu.VMEM((pixels, c_in), BF16), *[part] * (2 * streams)),
+        out_shape=(pltpu.VMEM((pixels, mid), BF16), pltpu.VMEM((pixels, c_in), BF16), pltpu.VMEM((mid, row), F32), *[part] * (2 * streams)),
         in_specs=[pl.BlockSpec(memory_space=pltpu.SMEM)] + [pl.BlockSpec(memory_space=pltpu.HBM)] * 5,
-        out_specs=tuple(full_vmem(2 + 2 * streams)),
+        out_specs=tuple(full_vmem(3 + 2 * streams)),
         scratch_shapes=[
             pltpu.VMEM((pixels, c_in), BF16),
             pltpu.VMEM((height, width * mid), BF16),
             pltpu.VMEM((height, width * mid), BF16),
-            pltpu.VMEM((mid, row), F32),
             pltpu.VMEM((pixels, 4 * mid), BF16),
             pltpu.VMEM((pixels, 4 * mid), BF16),
-            pltpu.VMEM((pixels, mid), BF16),
             pltpu.VMEM((4 * mid, 4 * mid), BF16),
             pltpu.SemaphoreType.DMA((5,)),
         ]
@@ -290,7 +283,7 @@
 
     input_grad = pl.pallas_call(
         input_grad_kernel,
-        out_shape=pltpu.VMEM((pixels, c_in), BF16),
+        out_shape=jax.ShapeDtypeStruct((pixels, c_in), BF16),
         in_specs=full_vmem(3),
         out_specs=full_vmem(1)[0],
         cost_estimate=pl.CostEstimate(
@@ -298,7 +291,7 @@
         ),
         compiler_params=pltpu.CompilerParams(vmem_limit_bytes=8 << 20),
         name="input_grad",
-    )(*in_vmem(back_first, out_near, params))
+    )(*in_vmem(back_first, out_near, params_near))
 
     totals = [keep + flip(send, "gx", 1) for keep, send in zip(parts[:streams], parts[streams:])]
     speeds = velocity.reshape(1, rows, row)
@@ -310,8 +303,8 @@
     steps, bit = exchange_steps(group, depth)
     for number, table in enumerate(steps):
         totals = [total + lax.ppermute(total, ("gx", "gy"), table) for total in totals]
-        if number == 0:
-            totals[0], input_grad = lax.optimization_barrier((totals[0], input_grad))
+        if number + 1 == len(steps):
+            totals[-1], input_grad = lax.optimization_barrier((totals[-1], input_grad))
     for turn in range(1, depth // bit):
         table = [(i, (i + turn * bit) % depth) for i in range(depth)]
         terms = [lax.ppermute(total, "gy", table) for total in totals]
@@ -330,7 +323,7 @@
         out_specs=tuple(full_vmem(2)),
         compiler_params=pltpu.CompilerParams(vmem_limit_bytes=8 << 20),
         name="update",
-    )(place, *in_vmem(speeds, other_speeds, params.reshape(group, rows, row), *totals, *others))
+    )(place, *in_vmem(speeds, other_speeds, params_near.reshape(group, rows, row), *totals, *others))
     return (input_grad.reshape(1, height, width, c_in), new_velocity, next_weights.reshape(mid, row))
 
 

time: 31.5 us -> 31.1 us (0.987); the launches traced: 31.1 us -> 31 us
  local copies, waits for them, and re-layouts: 1.02 us -> 0.01 us
  starting transfers between devices: 19.2 us -> 20.2 us
  waiting for transfers between devices: 4.53 us -> 3.58 us
  Pallas kernels: 5.39 us -> 6.32 us
    ppermute x8, waiting for transfers between devices: 3.45 us -> 1.5 us  [shards(): lax.ppermute(total, ('gx', 'gy'), table)]
    unnamed x5 -> x2, local copies, waits for them, and re-layouts: 1.01 us -> 0.01 us
    pallas_call x1, Pallas kernels: 0.44 us -> 1.44 us  [shards(): pl.pallas_call(input_grad_kernel, out_shape=jax.ShapeDtypeStruct((pixels,...]
    ppermute x7, waiting for transfers between devices: 1.09 us -> 2.08 us  [flip(): lax.ppermute(value, axis, [(i, i ^ bit) for i in range(lax.axis_size(axis...]
    ppermute x7, starting transfers between devices: 3.6 us -> 4.1 us  [flip(): lax.ppermute(value, axis, [(i, i ^ bit) for i in range(lax.axis_size(axis...]
    ppermute x8, starting transfers between devices: 15.6 us -> 16.1 us  [shards(): lax.ppermute(total, ('gx', 'gy'), table)]
  transfers between devices with their start and end apart: 15 -> 15, of which waited for: 6 -> 5; matrix products, arithmetic and copies ran while one was open for 4% -> 0% of each run, Pallas kernels for 1% -> 5%
where the time goes in v8:
time: 31.1 us; the launch traced here: 31 us
  starting transfers between devices  20.2 us (65%)
  Pallas kernels  6.32 us (20%)
  waiting for transfers between devices  3.58 us (12%)
  between operations  0.75 us (2%)
    ppermute x8, starting transfers between devices, shards(): lax.ppermute(total, ('gx', 'gy'), table)  16.1 us
    ppermute x7, starting transfers between devices, flip(): lax.ppermute(value, axis, [(i, i ^ bit) for i in range(lax.axis_size(axis...  4.1 us
    pallas_call x1, Pallas kernels, shards(): pl.pallas_call(functools.partial(grad_kernel, height=height, width=width,...  3.95 us
    ppermute x7, waiting for transfers between devices, flip(): lax.ppermute(value, axis, [(i, i ^ bit) for i in range(lax.axis_size(axis...  2.08 us
    ppermute x8, waiting for transfers between devices, shards(): lax.ppermute(total, ('gx', 'gy'), table)  1.5 us
    pallas_call x1, Pallas kernels, shards(): pl.pallas_call(input_grad_kernel, out_shape=jax.ShapeDtypeStruct((pixels,...  1.44 us
    pallas_call x1, Pallas kernels, shards(): pl.pallas_call(functools.partial(update_kernel, c_in=c_in, mid=mid), out_...  0.93 us
  transfers between devices with their start and end apart: 15, of which 5 were waited for; matrix products, arithmetic and copies ran while one was open for 0% of the time, Pallas kernels for 5%

profile of v8, /device:TPU:0, one launch (start us, length us, event | category | flops | bytes accessed | tf_op | source)
XLA Modules:
  0.0 31.0 jit_solution(18146078061736427873)
XLA Ops:
  0.6 0.0 copy-start
  0.6 3.9 %grads.1 = (bf16[2240,64]{1,0:T(8,128)(2,1)S(1)}, bf16[2240,256]{1,0:T(8,128)(2,1)S(1)}, f32[64,1088]{1,0:T(8,128)S(1)}, f32[2,8,1088]{2,1,0:T(8,128)S(1)}, f32[...) custom-call(s32[1]{0:T(128)} %bitcast.place_ref, bf16[2240,256]{1,0:T(8,128)(2,1)} %bitcast.21, ...), custom_call_target="tpu_custom_call" | custom-call | tf_op jit(solution)/shard_map/grads/pallas_call | solution.py:249
  4.6 0.6 %collective-permute-start.8 = (f32[2,8,1088]{2,1,0:T(8,128)S(1)}, f32[2,8,1088]{2,1,0:T(8,128)S(1)}, u32[]{:S(2)}, u32[]{:S(2)}) collective-permute-start(f32[2,8,1088]{2,1,0:T(8,128)S(1)} %get-tuple-element.21), channel_id=1, source_target_pairs={{0,4},{4,0},{8,12},{12,8},{16,20},{20,16},{24,28},{28,24},{1,5},{5... | collective-permute-start | bytes 208904 | tf_op jit(solution)/shard_map/ppermute | solution.py:208
  5.2 0.1 collective-permute-start
  5.2 0.8 %collective-permute-done.8 = f32[2,8,1088]{2,1,0:T(8,128)S(1)} collective-permute-done((f32[2,8,1088]{2,1,0:T(8,128)S(1)}, f32[2,8,1088]{2,1,0:T(8,128)S(1)}, u32[]{:S(2)}, u32[]{:S(2)}) %collective-permute-start.8) | collective-permute-done | bytes 69664 | tf_op jit(solution)/shard_map/ppermute | solution.py:208
  6.1 2.9 %collective-permute-start.9 = (f32[2,8,1088]{2,1,0:T(8,128)S(1)}, f32[2,8,1088]{2,1,0:T(8,128)S(1)}, u32[]{:S(2)}, u32[]{:S(2)}) collective-permute-start(f32[2,8,1088]{2,1,0:T(8,128)S(1)} %add.35), channel_id=1, source_target_pairs={{0,8},{1,9},{2,10},{3,11},{4,5},{5,4},{6,7},{7,6},{8,0},{9,1},{10,... | collective-permute-start | bytes 208904 | tf_op jit(solution)/shard_map/ppermute | solution.py:305
  9.0 0.0 collective-permute-done
  9.0 0.1 collective-permute-start.1
  9.1 0.0 copy-done
  9.1 2.0 %collective-permute-start.5 = (f32[1,8,1088]{2,1,0:T(8,128)S(1)}, f32[1,8,1088]{2,1,0:T(8,128)S(1)}, u32[]{:S(2)}, u32[]{:S(2)}) collective-permute-start(f32[1,8,1088]{2,1,0:T(8,128)S(1)} %bitcast.26), channel_id=1, source_target_pairs={{0,16},{4,20},{8,24},{12,28},{16,0},{20,4},{24,8},{28,12},{1,17},{... | collective-permute-start | bytes 104456 | tf_op jit(solution)/shard_map/ppermute | solution.py:208
  11.1 0.2 collective-permute-done.9
  11.3 2.2 %collective-permute-start.10 = (f32[2,8,1088]{2,1,0:T(8,128)S(1)}, f32[2,8,1088]{2,1,0:T(8,128)S(1)}, u32[]{:S(2)}, u32[]{:S(2)}) collective-permute-start(f32[2,8,1088]{2,1,0:T(8,128)S(1)} %add.36), channel_id=1, source_target_pairs={{0,1},{1,0},{2,3},{3,2},{4,12},{5,13},{6,14},{7,15},{8,9},{9,8},{1... | collective-permute-start | bytes 208904 | tf_op jit(solution)/shard_map/ppermute | solution.py:305
  13.5 0.0 collective-permute-done.1
  13.5 1.6 %collective-permute-start.2 = (f32[2,8,1088]{2,1,0:T(8,128)S(1)}, f32[2,8,1088]{2,1,0:T(8,128)S(1)}, u32[]{:S(2)}, u32[]{:S(2)}) collective-permute-start(f32[2,8,1088]{2,1,0:T(8,128)S(1)} %add.31), channel_id=1, source_target_pairs={{0,1},{1,0},{2,3},{3,2},{4,12},{5,13},{6,14},{7,15},{8,9},{9,8},{1... | collective-permute-start | bytes 208904 | tf_op jit(solution)/shard_map/ppermute | solution.py:305
  15.1 0.0 collective-permute-done.5
  15.1 0.8 %collective-permute-start.6 = (f32[2,8,1088]{2,1,0:T(8,128)S(1)}, f32[2,8,1088]{2,1,0:T(8,128)S(1)}, u32[]{:S(2)}, u32[]{:S(2)}) collective-permute-start(f32[2,8,1088]{2,1,0:T(8,128)S(1)} %get-tuple-element.26), channel_id=1, source_target_pairs={{0,8},{4,12},{8,0},{12,4},{16,24},{20,28},{24,16},{28,20},{1,9},{5... | collective-permute-start | bytes 208904 | tf_op jit(solution)/shard_map/ppermute | solution.py:208
  15.9 0.0 collective-permute-done.10
  15.9 2.0 %collective-permute-start.11 = (f32[2,8,1088]{2,1,0:T(8,128)S(1)}, f32[2,8,1088]{2,1,0:T(8,128)S(1)}, u32[]{:S(2)}, u32[]{:S(2)}) collective-permute-start(f32[2,8,1088]{2,1,0:T(8,128)S(1)} %add.37), channel_id=1, source_target_pairs={{0,16},{1,17},{2,18},{3,19},{4,6},{5,7},{6,4},{7,5},{8,24},{9,25},... | collective-permute-start | bytes 208904 | tf_op jit(solution)/shard_map/ppermute | solution.py:305
  17.9 0.1 collective-permute-done.2
  17.9 2.4 %collective-permute-start.3 = (f32[2,8,1088]{2,1,0:T(8,128)S(1)}, f32[2,8,1088]{2,1,0:T(8,128)S(1)}, u32[]{:S(2)}, u32[]{:S(2)}) collective-permute-start(f32[2,8,1088]{2,1,0:T(8,128)S(1)} %add.32), channel_id=1, source_target_pairs={{0,16},{1,17},{2,18},{3,19},{4,6},{5,7},{6,4},{7,5},{8,24},{9,25},... | collective-permute-start | bytes 208904 | tf_op jit(solution)/shard_map/ppermute | solution.py:305
  20.3 0.0 collective-permute-done.6
  20.3 0.0 collective-permute-done.11
  20.4 3.0 %collective-permute-start.12 = (f32[2,8,1088]{2,1,0:T(8,128)S(1)}, f32[2,8,1088]{2,1,0:T(8,128)S(1)}, u32[]{:S(2)}, u32[]{:S(2)}) collective-permute-start(f32[2,8,1088]{2,1,0:T(8,128)S(1)} %add.38), channel_id=1, source_target_pairs={{0,2},{1,3},{2,0},{3,1},{4,20},{5,21},{6,22},{7,23},{8,10},{9,11},... | collective-permute-start | bytes 208904 | tf_op jit(solution)/shard_map/ppermute | solution.py:305
  23.4 0.0 collective-permute-done.3
  23.4 2.0 %collective-permute-start.4 = (f32[2,8,1088]{2,1,0:T(8,128)S(1)}, f32[2,8,1088]{2,1,0:T(8,128)S(1)}, u32[]{:S(2)}, u32[]{:S(2)}) collective-permute-start(f32[2,8,1088]{2,1,0:T(8,128)S(1)} %add.33), channel_id=1, source_target_pairs={{0,2},{1,3},{2,0},{3,1},{4,20},{5,21},{6,22},{7,23},{8,10},{9,11},... | collective-permute-start | bytes 208904 | tf_op jit(solution)/shard_map/ppermute | solution.py:305
  25.4 0.1 collective-permute-start.7
  25.5 1.4 %input_grad.1 = bf16[2240,256]{1,0:T(8,128)(2,1)} custom-call(bf16[2240,64]{1,0:T(8,128)(2,1)S(1)} %get-tuple-element.16.back_ref, bf16[2240,256]{1,0:T(8,128)(2,1)S(1)} %get-tuple-element.17.out_ref, f32[64,1088]{1,0:T(8,128)S(1)} %get-tuple-element.18.params_ref), custom_call_target="tpu_custom_call" | custom-call | flops 73400320 | bytes 2580480 | tf_op jit(solution)/shard_map/input_grad/pallas_call | solution.py:284
  26.9 0.0 collective-permute-done.12
  26.9 0.6 %collective-permute-start.13 = (f32[2,8,1088]{2,1,0:T(8,128)S(1)}, f32[2,8,1088]{2,1,0:T(8,128)S(1)}, u32[]{:S(2)}, u32[]{:S(2)}) collective-permute-start(f32[2,8,1088]{2,1,0:T(8,128)S(1)} %add.39.rest_0_), channel_id=1, source_target_pairs={{0,4},{4,0},{8,12},{12,8},{16,20},{20,16},{24,28},{28,24},{1,5},{5... | collective-permute-start | bytes 208904 | tf_op jit(solution)/shard_map/ppermute | solution.py:208
  27.5 1.2 %collective-permute-done.4 = f32[2,8,1088]{2,1,0:T(8,128)S(1)} collective-permute-done((f32[2,8,1088]{2,1,0:T(8,128)S(1)}, f32[2,8,1088]{2,1,0:T(8,128)S(1)}, u32[]{:S(2)}, u32[]{:S(2)}) %collective-permute-start.4) | collective-permute-done | bytes 69664 | tf_op jit(solution)/shard_map/ppermute | solution.py:305
  28.7 0.1 collective-permute-start.14
  28.8 0.0 collective-permute-done.7.other_speed_ref
  28.8 0.0 collective-permute-done.13.rest_2_
  28.8 1.2 %collective-permute-done.14.rest_3_ = f32[2,8,1088]{2,1,0:T(8,128)S(1)} collective-permute-done((f32[2,8,1088]{2,1,0:T(8,128)S(1)}, f32[2,8,1088]{2,1,0:T(8,128)S(1)}, u32[]{:S(2)}, u32[]{:S(2)}) %collective-permute-start.14) | collective-permute-done | bytes 69664 | tf_op jit(solution)/shard_map/ppermute | solution.py:208
  30.1 0.9 %update.1 = (f32[8,1088]{1,0:T(8,128)}, f32[8,8,1088]{2,1,0:T(8,128)}) custom-call(s32[1]{0:T(128)} %bitcast.place_ref, f32[4,8,1088]{2,1,0:T(8,128)S(1)} %bitcast.19, f32[4,8,1088]{2,1,0:T(8,128)S(1)} %collective-permute-done.7.other_speed_ref, f32[8,8,1088]{2,1,0:T(8,128)S(1)} %bitcast.17, f32[2,8,1088]{2,1,0:T(8,128)S(1)} %add.39.rest_0_, ...), custom_call_target="tpu_custom_call" | custom-call | tf_op jit(solution)/shard_map/update/pallas_call | solution.py:316
  (13 shorter events, 0.1 us)
Async XLA Ops:
  0.6 8.5 %copy-start = (f32[8,1088]{1,0:T(8,128)S(1)}, f32[8,1088]{1,0:T(8,128)}, u32[]{:S(2)}) copy-start(f32[8,1088]{1,0:T(8,128)} %param.11) | copy-start | bytes 104452
  4.6 1.5 %collective-permute-start.8 = (f32[2,8,1088]{2,1,0:T(8,128)S(1)}, f32[2,8,1088]{2,1,0:T(8,128)S(1)}, u32[]{:S(2)}, u32[]{:S(2)}) collective-permute-start(f32[2,8,1088]{2,1,0:T(8,128)S(1)} %get-tuple-element.21), channel_id=1, source_target_pairs={{0,4},{4,0},{8,12},{12,8},{16,20},{20,16},{24,28},{28,24},{1,5},{5... | collective-permute-start | bytes 208904 | tf_op jit(solution)/shard_map/ppermute | solution.py:208
  5.2 3.8 %collective-permute-start = (f32[2,8,1088]{2,1,0:T(8,128)S(1)}, f32[2,8,1088]{2,1,0:T(8,128)S(1)}, u32[]{:S(2)}, u32[]{:S(2)}) collective-permute-start(f32[2,8,1088]{2,1,0:T(8,128)S(1)} %get-tuple-element.15), channel_id=1, source_target_pairs={{0,4},{4,0},{8,12},{12,8},{16,20},{20,16},{24,28},{28,24},{1,5},{5... | collective-permute-start | bytes 208904 | tf_op jit(solution)/shard_map/ppermute | solution.py:208
  6.1 5.2 %collective-permute-start.9 = (f32[2,8,1088]{2,1,0:T(8,128)S(1)}, f32[2,8,1088]{2,1,0:T(8,128)S(1)}, u32[]{:S(2)}, u32[]{:S(2)}) collective-permute-start(f32[2,8,1088]{2,1,0:T(8,128)S(1)} %add.35), channel_id=1, source_target_pairs={{0,8},{1,9},{2,10},{3,11},{4,5},{5,4},{6,7},{7,6},{8,0},{9,1},{10,... | collective-permute-start | bytes 208904 | tf_op jit(solution)/shard_map/ppermute | solution.py:305
  9.0 4.5 %collective-permute-start.1 = (f32[2,8,1088]{2,1,0:T(8,128)S(1)}, f32[2,8,1088]{2,1,0:T(8,128)S(1)}, u32[]{:S(2)}, u32[]{:S(2)}) collective-permute-start(f32[2,8,1088]{2,1,0:T(8,128)S(1)} %add.30), channel_id=1, source_target_pairs={{0,8},{1,9},{2,10},{3,11},{4,5},{5,4},{6,7},{7,6},{8,0},{9,1},{10,... | collective-permute-start | bytes 208904 | tf_op jit(solution)/shard_map/ppermute | solution.py:305
  9.1 5.9 %collective-permute-start.5 = (f32[1,8,1088]{2,1,0:T(8,128)S(1)}, f32[1,8,1088]{2,1,0:T(8,128)S(1)}, u32[]{:S(2)}, u32[]{:S(2)}) collective-permute-start(f32[1,8,1088]{2,1,0:T(8,128)S(1)} %bitcast.26), channel_id=1, source_target_pairs={{0,16},{4,20},{8,24},{12,28},{16,0},{20,4},{24,8},{28,12},{1,17},{... | collective-permute-start | bytes 104456 | tf_op jit(solution)/shard_map/ppermute | solution.py:208
  11.3 4.5 %collective-permute-start.10 = (f32[2,8,1088]{2,1,0:T(8,128)S(1)}, f32[2,8,1088]{2,1,0:T(8,128)S(1)}, u32[]{:S(2)}, u32[]{:S(2)}) collective-permute-start(f32[2,8,1088]{2,1,0:T(8,128)S(1)} %add.36), channel_id=1, source_target_pairs={{0,1},{1,0},{2,3},{3,2},{4,12},{5,13},{6,14},{7,15},{8,9},{9,8},{1... | collective-permute-start | bytes 208904 | tf_op jit(solution)/shard_map/ppermute | solution.py:305
  13.5 4.4 %collective-permute-start.2 = (f32[2,8,1088]{2,1,0:T(8,128)S(1)}, f32[2,8,1088]{2,1,0:T(8,128)S(1)}, u32[]{:S(2)}, u32[]{:S(2)}) collective-permute-start(f32[2,8,1088]{2,1,0:T(8,128)S(1)} %add.31), channel_id=1, source_target_pairs={{0,1},{1,0},{2,3},{3,2},{4,12},{5,13},{6,14},{7,15},{8,9},{9,8},{1... | collective-permute-start | bytes 208904 | tf_op jit(solution)/shard_map/ppermute | solution.py:305
  15.1 5.2 %collective-permute-start.6 = (f32[2,8,1088]{2,1,0:T(8,128)S(1)}, f32[2,8,1088]{2,1,0:T(8,128)S(1)}, u32[]{:S(2)}, u32[]{:S(2)}) collective-permute-start(f32[2,8,1088]{2,1,0:T(8,128)S(1)} %get-tuple-element.26), channel_id=1, source_target_pairs={{0,8},{4,12},{8,0},{12,4},{16,24},{20,28},{24,16},{28,20},{1,9},{5... | collective-permute-start | bytes 208904 | tf_op jit(solution)/shard_map/ppermute | solution.py:208
  15.9 4.5 %collective-permute-start.11 = (f32[2,8,1088]{2,1,0:T(8,128)S(1)}, f32[2,8,1088]{2,1,0:T(8,128)S(1)}, u32[]{:S(2)}, u32[]{:S(2)}) collective-permute-start(f32[2,8,1088]{2,1,0:T(8,128)S(1)} %add.37), channel_id=1, source_target_pairs={{0,16},{1,17},{2,18},{3,19},{4,6},{5,7},{6,4},{7,5},{8,24},{9,25},... | collective-permute-start | bytes 208904 | tf_op jit(solution)/shard_map/ppermute | solution.py:305
  17.9 5.4 %collective-permute-start.3 = (f32[2,8,1088]{2,1,0:T(8,128)S(1)}, f32[2,8,1088]{2,1,0:T(8,128)S(1)}, u32[]{:S(2)}, u32[]{:S(2)}) collective-permute-start(f32[2,8,1088]{2,1,0:T(8,128)S(1)} %add.32), channel_id=1, source_target_pairs={{0,16},{1,17},{2,18},{3,19},{4,6},{5,7},{6,4},{7,5},{8,24},{9,25},... | collective-permute-start | bytes 208904 | tf_op jit(solution)/shard_map/ppermute | solution.py:305
  20.4 6.5 %collective-permute-start.12 = (f32[2,8,1088]{2,1,0:T(8,128)S(1)}, f32[2,8,1088]{2,1,0:T(8,128)S(1)}, u32[]{:S(2)}, u32[]{:S(2)}) collective-permute-start(f32[2,8,1088]{2,1,0:T(8,128)S(1)} %add.38), channel_id=1, source_target_pairs={{0,2},{1,3},{2,0},{3,1},{4,20},{5,21},{6,22},{7,23},{8,10},{9,11},... | collective-permute-start | bytes 208904 | tf_op jit(solution)/shard_map/ppermute | solution.py:305
  23.4 5.3 %collective-permute-start.4 = (f32[2,8,1088]{2,1,0:T(8,128)S(1)}, f32[2,8,1088]{2,1,0:T(8,128)S(1)}, u32[]{:S(2)}, u32[]{:S(2)}) collective-permute-start(f32[2,8,1088]{2,1,0:T(8,128)S(1)} %add.33), channel_id=1, source_target_pairs={{0,2},{1,3},{2,0},{3,1},{4,20},{5,21},{6,22},{7,23},{8,10},{9,11},... | collective-permute-start | bytes 208904 | tf_op jit(solution)/shard_map/ppermute | solution.py:305
  25.4 3.4 %collective-permute-start.7 = (f32[4,8,1088]{2,1,0:T(8,128)S(1)}, f32[4,8,1088]{2,1,0:T(8,128)S(1)}, u32[]{:S(2)}, u32[]{:S(2)}) collective-permute-start(f32[4,8,1088]{2,1,0:T(8,128)S(1)} %bitcast.18), channel_id=1, source_target_pairs={{0,4},{4,0},{8,12},{12,8},{16,20},{20,16},{24,28},{28,24},{1,5},{5... | collective-permute-start | bytes 417800 | tf_op jit(solution)/shard_map/ppermute | solution.py:208
  26.9 1.9 %collective-permute-start.13 = (f32[2,8,1088]{2,1,0:T(8,128)S(1)}, f32[2,8,1088]{2,1,0:T(8,128)S(1)}, u32[]{:S(2)}, u32[]{:S(2)}) collective-permute-start(f32[2,8,1088]{2,1,0:T(8,128)S(1)} %add.39.rest_0_), channel_id=1, source_target_pairs={{0,4},{4,0},{8,12},{12,8},{16,20},{20,16},{24,28},{28,24},{1,5},{5... | collective-permute-start | bytes 208904 | tf_op jit(solution)/shard_map/ppermute | solution.py:208
  28.7 1.3 %collective-permute-start.14 = (f32[2,8,1088]{2,1,0:T(8,128)S(1)}, f32[2,8,1088]{2,1,0:T(8,128)S(1)}, u32[]{:S(2)}, u32[]{:S(2)}) collective-permute-start(f32[2,8,1088]{2,1,0:T(8,128)S(1)} %add.34.rest_1_), channel_id=1, source_target_pairs={{0,4},{4,0},{8,12},{12,8},{16,20},{20,16},{24,28},{28,24},{1,5},{5... | collective-permute-start | bytes 208904 | tf_op jit(solution)/shard_map/ppermute | solution.py:208

commit v9 on v8

--- a/solution.py
+++ b/solution.py
@@ -26,10 +26,10 @@
 
 def grad_kernel(
     place_ref, x_hbm, first_hbm, second_hbm, out_hbm, params_hbm,
-    back_ref, out_ref, params_ref, *rest, height, width, strips, rows, streams,
+    left_ref, x_ref, out_ref, params_ref, taps_grad_ref,
+    first_ref, second_ref, bs_cols, first_rows, taps_ref, arrived, *blocks,
+    height, width, strips, rows,
 ):
-    keep_refs, send_refs, rest = rest[:streams], rest[streams : 2 * streams], rest[2 * streams :]
-    x_ref, first_ref, second_ref, bs_cols, first_rows, taps_ref, arrived, *blocks = rest
     count = len(blocks) // 4
     second_px, first_px, bs_px, spread_px = (blocks[n * count : (n + 1) * count] for n in range(4))
     moves = [
@@ -51,7 +51,7 @@
     mid = params_ref.shape[0]
     pixels = height * width
     pad = 8
-    s_one, s_two, s_three = (1.0 / math.sqrt(n) for n in (c_in, 9 * mid, mid))
+    s_two, s_three = 1.0 / math.sqrt(9 * mid), 1.0 / math.sqrt(mid)
     block_rows = divisor_up_to(height, 8)
     step = block_rows * width
     chunks = [slice(k * step, (k + 1) * step) for k in range(height // block_rows)]
@@ -63,10 +63,10 @@
     got_params.wait()
     w_third = params_ref[:, c_in + 9 * mid :].astype(BF16)
     w_third = jnp.concatenate([w_third, w_third], axis=0)
-    for r in range(3):
+    for r, place in enumerate((1, 0, 3)):
         for q in range(3):
             t = 3 * r + q
-            taps_ref[q * mid : (q + 1) * mid, r * mid : (r + 1) * mid] = params_ref[
+            taps_ref[q * mid : (q + 1) * mid, place * mid : (place + 1) * mid] = params_ref[
                 :, c_in + t * mid : c_in + (t + 1) * mid
             ].astype(BF16)
     got_second.wait()
@@ -92,7 +92,7 @@
         px[pad : pad + step, :] = here
         after = jnp.where(column < width - 1, px[pad + 1 : pad + 1 + step, :], 0.0)
         before = jnp.where(column > 0, px[pad - 1 : pad - 1 + step, :], 0.0)
-        cols = jnp.concatenate([jnp.where(low, after, here), jnp.where(low, before, second)], axis=1).astype(BF16)
+        cols = jnp.concatenate([jnp.where(low, after, here), before], axis=1).astype(BF16)
         bs_cols[c, :] = cols
         spread_px[number][...] = jnp.dot(cols, taps_ref[...], preferred_element_type=F32)
 
@@ -116,7 +116,7 @@
         centre = pltpu.roll(spread_px[number][:, front], mid, 1)
         bottom = row_above(spread_px, number, rear)
         total = jnp.where(level > 0, (top + centre + bottom) * s_two, 0.0)
-        back_ref[c, :] = total[:, :mid].astype(BF16)
+        left_ref[c, :] = jnp.where(low, second_px[number][...], total).astype(BF16)
 
     for number in range(len(chunks)):
         to_pixels(number)
@@ -127,9 +127,16 @@
             leave(number - 1)
     leave(len(chunks) - 1)
 
-    def outer(turned, right):
-        return jnp.dot(turned, right, preferred_element_type=F32)
-
+    taps_grad_ref[...] = jnp.dot(bs_cols[...].T[: 3 * mid], first_rows[...], preferred_element_type=F32) * (
+        s_two / strips
+    )
+    got_x.wait()
+
+
+def outer_kernel(place_ref, left_ref, x_ref, out_ref, taps_grad_ref, *halves, strips, rows):
+    keep_refs, send_refs = halves[: len(halves) // 2], halves[len(halves) // 2 :]
+    c_in = x_ref.shape[1]
+    mid = left_ref.shape[1] // 2
     even = place_ref[0] % 2 == 0
 
     def put(grad, column):
@@ -141,20 +148,22 @@
             keep_refs[stream][tile, :, columns] = jnp.where(even, one, two)
             send_refs[stream][tile, :, columns] = jnp.where(even, two, one)
 
-    got_x.wait()
-    turned = bs_cols[...].T
-    put(outer(turned[3 * mid :], out_ref[...]) * (s_three / strips), c_in + 9 * mid)
-    grad_two = outer(turned[: 3 * mid], first_rows[...]) * (s_two / strips)
     for r in range(3):
         for q in range(3):
-            put(grad_two[q * mid : (q + 1) * mid, r * mid : (r + 1) * mid], c_in + (3 * r + q) * mid)
-    put(outer(back_ref[...].T, x_ref[...]) * (s_one / strips), 0)
-
-
-def input_grad_kernel(back_ref, out_ref, params_ref, result_ref):
+            tap = taps_grad_ref[q * mid : (q + 1) * mid, r * mid : (r + 1) * mid]
+            put(tap, c_in + (3 * r + q) * mid)
+    turned = left_ref[...].T
+    third = jnp.dot(turned[:mid], out_ref[...], preferred_element_type=F32)
+    put(third * (1.0 / math.sqrt(mid) / strips), c_in + 9 * mid)
+    first = jnp.dot(turned[mid:], x_ref[...], preferred_element_type=F32)
+    put(first * (1.0 / math.sqrt(c_in) / strips), 0)
+
+
+def input_grad_kernel(left_ref, out_ref, params_ref, result_ref):
     c_in = out_ref.shape[1]
     w_first = params_ref[:, :c_in].astype(BF16)
-    change = jnp.dot(back_ref[...], w_first, preferred_element_type=F32)
+    w_first = jnp.concatenate([jnp.zeros_like(w_first), w_first], axis=0)
+    change = jnp.dot(left_ref[...], w_first, preferred_element_type=F32)
     result_ref[...] = (out_ref[...].astype(F32) + (1.0 / math.sqrt(c_in)) * change).astype(BF16)
 
 
@@ -245,14 +254,20 @@
     step = divisor_up_to(height, 8) * width
     streams = 2 if halves % 2 == 0 else 1
     part = pltpu.VMEM((halves // streams, rows, row), F32)
-
-    back_first, out_near, params_near, *parts = pl.pallas_call(
-        functools.partial(grad_kernel, height=height, width=width, strips=strips, rows=rows, streams=streams),
-        out_shape=(pltpu.VMEM((pixels, mid), BF16), pltpu.VMEM((pixels, c_in), BF16), pltpu.VMEM((mid, row), F32), *[part] * (2 * streams)),
+    flat = pltpu.VMEM((pixels, c_in), BF16)
+
+    left, x_near, out_near, params_near, taps_grad = pl.pallas_call(
+        functools.partial(grad_kernel, height=height, width=width, strips=strips, rows=rows),
+        out_shape=(
+            pltpu.VMEM((pixels, 2 * mid), BF16),
+            flat,
+            flat,
+            pltpu.VMEM((mid, row), F32),
+            pltpu.VMEM((3 * mid, 4 * mid), F32),
+        ),
         in_specs=[pl.BlockSpec(memory_space=pltpu.SMEM)] + [pl.BlockSpec(memory_space=pltpu.HBM)] * 5,
-        out_specs=tuple(full_vmem(3 + 2 * streams)),
+        out_specs=tuple(full_vmem(5)),
         scratch_shapes=[
-            pltpu.VMEM((pixels, c_in), BF16),
             pltpu.VMEM((height, width * mid), BF16),
             pltpu.VMEM((height, width * mid), BF16),
             pltpu.VMEM((pixels, 4 * mid), BF16),
@@ -281,6 +296,18 @@
         ),
     )
 
+    parts = pl.pallas_call(
+        functools.partial(outer_kernel, strips=strips, rows=rows),
+        out_shape=(part,) * (2 * streams),
+        in_specs=[pl.BlockSpec(memory_space=pltpu.SMEM)] + full_vmem(4),
+        out_specs=tuple(full_vmem(2 * streams)),
+        compiler_params=pltpu.CompilerParams(vmem_limit_bytes=8 << 20),
+        cost_estimate=pl.CostEstimate(
+            flops=4 * pixels * mid * c_in, bytes_accessed=4 * pixels * (c_in + mid), transcendentals=0
+        ),
+        name="sides",
+    )(place, *in_vmem(left, x_near, out_near, taps_grad))
+
     input_grad = pl.pallas_call(
         input_grad_kernel,
         out_shape=jax.ShapeDtypeStruct((pixels, c_in), BF16),
@@ -291,7 +318,7 @@
         ),
         compiler_params=pltpu.CompilerParams(vmem_limit_bytes=8 << 20),
         name="input_grad",
-    )(*in_vmem(back_first, out_near, params_near))
+    )(*in_vmem(left, out_near, params_near))
 
     totals = [keep + flip(send, "gx", 1) for keep, send in zip(parts[:streams], parts[streams:])]
     speeds = velocity.reshape(1, rows, row)

time: 31.1 us -> 30.9 us (level)
    pallas_call x1, Pallas kernels: 3.95 us -> 3.15 us  [shards(): pl.pallas_call(functools.partial(grad_kernel, height=height, width=width,...]
    pallas_call x0 -> x1, Pallas kernels: none -> 0.59 us  [shards(): pl.pallas_call(functools.partial(outer_kernel, strips=strips, rows=rows),...]
where the time goes in v9:
time: 30.9 us; the launch traced here: 30.8 us
  starting transfers between devices  20.2 us (65%)
  Pallas kernels  6.13 us (20%)
  waiting for transfers between devices  3.58 us (12%)
  between operations  0.76 us (2%)
    ppermute x8, starting transfers between devices, shards(): lax.ppermute(total, ('gx', 'gy'), table)  16.1 us
    ppermute x7, starting transfers between devices, flip(): lax.ppermute(value, axis, [(i, i ^ bit) for i in range(lax.axis_size(axis...  4.08 us
    pallas_call x1, Pallas kernels, shards(): pl.pallas_call(functools.partial(grad_kernel, height=height, width=width,...  3.15 us
    ppermute x7, waiting for transfers between devices, flip(): lax.ppermute(value, axis, [(i, i ^ bit) for i in range(lax.axis_size(axis...  2.08 us
    ppermute x8, waiting for transfers between devices, shards(): lax.ppermute(total, ('gx', 'gy'), table)  1.5 us
    pallas_call x1, Pallas kernels, shards(): pl.pallas_call(input_grad_kernel, out_shape=jax.ShapeDtypeStruct((pixels,...  1.45 us
    pallas_call x1, Pallas kernels, shards(): pl.pallas_call(functools.partial(update_kernel, c_in=c_in, mid=mid), out_...  0.93 us
  transfers between devices with their start and end apart: 15, of which 5 were waited for; matrix products, arithmetic and copies ran while one was open for 0% of the time, Pallas kernels for 5%

profile of v9, /device:TPU:0, one launch (start us, length us, event | category | flops | bytes accessed | tf_op | source)
XLA Modules:
  0.0 30.8 jit_solution(17762566987314640631)
XLA Ops:
  0.6 3.2 %grads.1 = (bf16[2240,128]{1,0:T(8,128)(2,1)S(1)}, bf16[2240,256]{1,0:T(8,128)(2,1)S(1)}, bf16[2240,256]{1,0:T(8,128)(2,1)S(1)}, f32[64,1088]{1,0:T(8,128)S(1)}, f32[192,256]{1,0:T(8,128)S(1)}) custom-call(s32[1]{0:T(128)} %bitcast.place_ref, bf16[2240,256]{1,0:T(8,128)(2,1)} %bitcast.21, bf16[40,3584]{1,0:T(8,128)(2,1)} %bitcast.23, ...), custom_call_target="tpu_custom_call" | custom-call | tf_op jit(solution)/shard_map/grads/pallas_call | solution.py:259
  3.8 0.0 copy-start
  3.8 0.6 %sides.1 = (f32[2,8,1088]{2,1,0:T(8,128)S(1)}, f32[2,8,1088]{2,1,0:T(8,128)S(1)}, f32[2,8,1088]{2,1,0:T(8,128)S(1)}, f32[2,8,1088]{2,1,0:T(8,128)S(1)}) custom-call(s32[1]{0:T(128)} %bitcast.place_ref, bf16[2240,128]{1,0:T(8,128)(2,1)S(1)} %get-tuple-element.16.left_ref, bf16[2240,256]{1,0:T(8,128)(2,1)S(1)} %get-tuple-element.17.x_ref, ...), custom_call_target="tpu_custom_call" | custom-call | flops 146800640 | bytes 2867200 | tf_op jit(solution)/shard_map/sides/pallas_call | solution.py:299
  4.4 0.6 %collective-permute-start.8 = (f32[2,8,1088]{2,1,0:T(8,128)S(1)}, f32[2,8,1088]{2,1,0:T(8,128)S(1)}, u32[]{:S(2)}, u32[]{:S(2)}) collective-permute-start(f32[2,8,1088]{2,1,0:T(8,128)S(1)} %get-tuple-element.25), channel_id=1, source_target_pairs={{0,4},{4,0},{8,12},{12,8},{16,20},{20,16},{24,28},{28,24},{1,5},{5... | collective-permute-start | bytes 208904 | tf_op jit(solution)/shard_map/ppermute | solution.py:217
  5.0 0.1 collective-permute-start
  5.0 0.8 %collective-permute-done.8 = f32[2,8,1088]{2,1,0:T(8,128)S(1)} collective-permute-done((f32[2,8,1088]{2,1,0:T(8,128)S(1)}, f32[2,8,1088]{2,1,0:T(8,128)S(1)}, u32[]{:S(2)}, u32[]{:S(2)}) %collective-permute-start.8) | collective-permute-done | bytes 69664 | tf_op jit(solution)/shard_map/ppermute | solution.py:217
  5.9 2.9 %collective-permute-start.9 = (f32[2,8,1088]{2,1,0:T(8,128)S(1)}, f32[2,8,1088]{2,1,0:T(8,128)S(1)}, u32[]{:S(2)}, u32[]{:S(2)}) collective-permute-start(f32[2,8,1088]{2,1,0:T(8,128)S(1)} %add.35), channel_id=1, source_target_pairs={{0,8},{1,9},{2,10},{3,11},{4,5},{5,4},{6,7},{7,6},{8,0},{9,1},{10,... | collective-permute-start | bytes 208904 | tf_op jit(solution)/shard_map/ppermute | solution.py:332
  8.8 0.0 collective-permute-done
  8.8 0.1 collective-permute-start.1
  8.9 0.0 copy-done
  8.9 2.0 %collective-permute-start.5 = (f32[1,8,1088]{2,1,0:T(8,128)S(1)}, f32[1,8,1088]{2,1,0:T(8,128)S(1)}, u32[]{:S(2)}, u32[]{:S(2)}) collective-permute-start(f32[1,8,1088]{2,1,0:T(8,128)S(1)} %bitcast.26), channel_id=1, source_target_pairs={{0,16},{4,20},{8,24},{12,28},{16,0},{20,4},{24,8},{28,12},{1,17},{... | collective-permute-start | bytes 104456 | tf_op jit(solution)/shard_map/ppermute | solution.py:217
  10.9 0.2 collective-permute-done.9
  11.1 2.2 %collective-permute-start.10 = (f32[2,8,1088]{2,1,0:T(8,128)S(1)}, f32[2,8,1088]{2,1,0:T(8,128)S(1)}, u32[]{:S(2)}, u32[]{:S(2)}) collective-permute-start(f32[2,8,1088]{2,1,0:T(8,128)S(1)} %add.36), channel_id=1, source_target_pairs={{0,1},{1,0},{2,3},{3,2},{4,12},{5,13},{6,14},{7,15},{8,9},{9,8},{1... | collective-permute-start | bytes 208904 | tf_op jit(solution)/shard_map/ppermute | solution.py:332
  13.3 0.0 collective-permute-done.1
  13.3 1.6 %collective-permute-start.2 = (f32[2,8,1088]{2,1,0:T(8,128)S(1)}, f32[2,8,1088]{2,1,0:T(8,128)S(1)}, u32[]{:S(2)}, u32[]{:S(2)}) collective-permute-start(f32[2,8,1088]{2,1,0:T(8,128)S(1)} %add.31), channel_id=1, source_target_pairs={{0,1},{1,0},{2,3},{3,2},{4,12},{5,13},{6,14},{7,15},{8,9},{9,8},{1... | collective-permute-start | bytes 208904 | tf_op jit(solution)/shard_map/ppermute | solution.py:332
  14.9 0.0 collective-permute-done.5
  14.9 0.8 %collective-permute-start.6 = (f32[2,8,1088]{2,1,0:T(8,128)S(1)}, f32[2,8,1088]{2,1,0:T(8,128)S(1)}, u32[]{:S(2)}, u32[]{:S(2)}) collective-permute-start(f32[2,8,1088]{2,1,0:T(8,128)S(1)} %get-tuple-element.30), channel_id=1, source_target_pairs={{0,8},{4,12},{8,0},{12,4},{16,24},{20,28},{24,16},{28,20},{1,9},{5... | collective-permute-start | bytes 208904 | tf_op jit(solution)/shard_map/ppermute | solution.py:217
  15.7 0.0 collective-permute-done.10
  15.7 2.0 %collective-permute-start.11 = (f32[2,8,1088]{2,1,0:T(8,128)S(1)}, f32[2,8,1088]{2,1,0:T(8,128)S(1)}, u32[]{:S(2)}, u32[]{:S(2)}) collective-permute-start(f32[2,8,1088]{2,1,0:T(8,128)S(1)} %add.37), channel_id=1, source_target_pairs={{0,16},{1,17},{2,18},{3,19},{4,6},{5,7},{6,4},{7,5},{8,24},{9,25},... | collective-permute-start | bytes 208904 | tf_op jit(solution)/shard_map/ppermute | solution.py:332
  17.7 0.1 collective-permute-done.2
  17.8 2.4 %collective-permute-start.3 = (f32[2,8,1088]{2,1,0:T(8,128)S(1)}, f32[2,8,1088]{2,1,0:T(8,128)S(1)}, u32[]{:S(2)}, u32[]{:S(2)}) collective-permute-start(f32[2,8,1088]{2,1,0:T(8,128)S(1)} %add.32), channel_id=1, source_target_pairs={{0,16},{1,17},{2,18},{3,19},{4,6},{5,7},{6,4},{7,5},{8,24},{9,25},... | collective-permute-start | bytes 208904 | tf_op jit(solution)/shard_map/ppermute | solution.py:332
  20.1 0.0 collective-permute-done.6
  20.1 0.0 collective-permute-done.11
  20.2 3.0 %collective-permute-start.12 = (f32[2,8,1088]{2,1,0:T(8,128)S(1)}, f32[2,8,1088]{2,1,0:T(8,128)S(1)}, u32[]{:S(2)}, u32[]{:S(2)}) collective-permute-start(f32[2,8,1088]{2,1,0:T(8,128)S(1)} %add.38), channel_id=1, source_target_pairs={{0,2},{1,3},{2,0},{3,1},{4,20},{5,21},{6,22},{7,23},{8,10},{9,11},... | collective-permute-start | bytes 208904 | tf_op jit(solution)/shard_map/ppermute | solution.py:332
  23.2 0.0 collective-permute-done.3
  23.2 2.0 %collective-permute-start.4 = (f32[2,8,1088]{2,1,0:T(8,128)S(1)}, f32[2,8,1088]{2,1,0:T(8,128)S(1)}, u32[]{:S(2)}, u32[]{:S(2)}) collective-permute-start(f32[2,8,1088]{2,1,0:T(8,128)S(1)} %add.33), channel_id=1, source_target_pairs={{0,2},{1,3},{2,0},{3,1},{4,20},{5,21},{6,22},{7,23},{8,10},{9,11},... | collective-permute-start | bytes 208904 | tf_op jit(solution)/shard_map/ppermute | solution.py:332
  25.2 0.1 collective-permute-start.7
  25.3 1.5 %input_grad.1 = bf16[2240,256]{1,0:T(8,128)(2,1)} custom-call(bf16[2240,128]{1,0:T(8,128)(2,1)S(1)} %get-tuple-element.16.left_ref, bf16[2240,256]{1,0:T(8,128)(2,1)S(1)} %get-tuple-element.18.out_ref, f32[64,1088]{1,0:T(8,128)S(1)} %get-tuple-element.22.params_ref), custom_call_target="tpu_custom_call" | custom-call | flops 73400320 | bytes 2580480 | tf_op jit(solution)/shard_map/input_grad/pallas_call | solution.py:311
  26.7 0.0 collective-permute-done.12
  26.7 0.6 %collective-permute-start.13 = (f32[2,8,1088]{2,1,0:T(8,128)S(1)}, f32[2,8,1088]{2,1,0:T(8,128)S(1)}, u32[]{:S(2)}, u32[]{:S(2)}) collective-permute-start(f32[2,8,1088]{2,1,0:T(8,128)S(1)} %add.39.rest_0_), channel_id=1, source_target_pairs={{0,4},{4,0},{8,12},{12,8},{16,20},{20,16},{24,28},{28,24},{1,5},{5... | collective-permute-start | bytes 208904 | tf_op jit(solution)/shard_map/ppermute | solution.py:217
  27.3 1.2 %collective-permute-done.4 = f32[2,8,1088]{2,1,0:T(8,128)S(1)} collective-permute-done((f32[2,8,1088]{2,1,0:T(8,128)S(1)}, f32[2,8,1088]{2,1,0:T(8,128)S(1)}, u32[]{:S(2)}, u32[]{:S(2)}) %collective-permute-start.4) | collective-permute-done | bytes 69664 | tf_op jit(solution)/shard_map/ppermute | solution.py:332
  28.5 0.1 collective-permute-start.14
  28.6 0.0 collective-permute-done.7.other_speed_ref
  28.6 0.0 collective-permute-done.13.rest_2_
  28.6 1.2 %collective-permute-done.14.rest_3_ = f32[2,8,1088]{2,1,0:T(8,128)S(1)} collective-permute-done((f32[2,8,1088]{2,1,0:T(8,128)S(1)}, f32[2,8,1088]{2,1,0:T(8,128)S(1)}, u32[]{:S(2)}, u32[]{:S(2)}) %collective-permute-start.14) | collective-permute-done | bytes 69664 | tf_op jit(solution)/shard_map/ppermute | solution.py:217
  29.9 0.9 %update.1 = (f32[8,1088]{1,0:T(8,128)}, f32[8,8,1088]{2,1,0:T(8,128)}) custom-call(s32[1]{0:T(128)} %bitcast.place_ref, f32[4,8,1088]{2,1,0:T(8,128)S(1)} %bitcast.19, f32[4,8,1088]{2,1,0:T(8,128)S(1)} %collective-permute-done.7.other_speed_ref, f32[8,8,1088]{2,1,0:T(8,128)S(1)} %bitcast.17, f32[2,8,1088]{2,1,0:T(8,128)S(1)} %add.39.rest_0_, ...), custom_call_target="tpu_custom_call" | custom-call | tf_op jit(solution)/shard_map/update/pallas_call | solution.py:343
  (13 shorter events, 0.1 us)
Async XLA Ops:
  3.8 5.1 %copy-start = (f32[8,1088]{1,0:T(8,128)S(1)}, f32[8,1088]{1,0:T(8,128)}, u32[]{:S(2)}) copy-start(f32[8,1088]{1,0:T(8,128)} %param.11) | copy-start | bytes 104452
  4.4 1.5 %collective-permute-start.8 = (f32[2,8,1088]{2,1,0:T(8,128)S(1)}, f32[2,8,1088]{2,1,0:T(8,128)S(1)}, u32[]{:S(2)}, u32[]{:S(2)}) collective-permute-start(f32[2,8,1088]{2,1,0:T(8,128)S(1)} %get-tuple-element.25), channel_id=1, source_target_pairs={{0,4},{4,0},{8,12},{12,8},{16,20},{20,16},{24,28},{28,24},{1,5},{5... | collective-permute-start | bytes 208904 | tf_op jit(solution)/shard_map/ppermute | solution.py:217
  5.0 3.8 %collective-permute-start = (f32[2,8,1088]{2,1,0:T(8,128)S(1)}, f32[2,8,1088]{2,1,0:T(8,128)S(1)}, u32[]{:S(2)}, u32[]{:S(2)}) collective-permute-start(f32[2,8,1088]{2,1,0:T(8,128)S(1)} %get-tuple-element.21), channel_id=1, source_target_pairs={{0,4},{4,0},{8,12},{12,8},{16,20},{20,16},{24,28},{28,24},{1,5},{5... | collective-permute-start | bytes 208904 | tf_op jit(solution)/shard_map/ppermute | solution.py:217
  5.9 5.2 %collective-permute-start.9 = (f32[2,8,1088]{2,1,0:T(8,128)S(1)}, f32[2,8,1088]{2,1,0:T(8,128)S(1)}, u32[]{:S(2)}, u32[]{:S(2)}) collective-permute-start(f32[2,8,1088]{2,1,0:T(8,128)S(1)} %add.35), channel_id=1, source_target_pairs={{0,8},{1,9},{2,10},{3,11},{4,5},{5,4},{6,7},{7,6},{8,0},{9,1},{10,... | collective-permute-start | bytes 208904 | tf_op jit(solution)/shard_map/ppermute | solution.py:332
  8.8 4.5 %collective-permute-start.1 = (f32[2,8,1088]{2,1,0:T(8,128)S(1)}, f32[2,8,1088]{2,1,0:T(8,128)S(1)}, u32[]{:S(2)}, u32[]{:S(2)}) collective-permute-start(f32[2,8,1088]{2,1,0:T(8,128)S(1)} %add.30), channel_id=1, source_target_pairs={{0,8},{1,9},{2,10},{3,11},{4,5},{5,4},{6,7},{7,6},{8,0},{9,1},{10,... | collective-permute-start | bytes 208904 | tf_op jit(solution)/shard_map/ppermute | solution.py:332
  8.9 5.9 %collective-permute-start.5 = (f32[1,8,1088]{2,1,0:T(8,128)S(1)}, f32[1,8,1088]{2,1,0:T(8,128)S(1)}, u32[]{:S(2)}, u32[]{:S(2)}) collective-permute-start(f32[1,8,1088]{2,1,0:T(8,128)S(1)} %bitcast.26), channel_id=1, source_target_pairs={{0,16},{4,20},{8,24},{12,28},{16,0},{20,4},{24,8},{28,12},{1,17},{... | collective-permute-start | bytes 104456 | tf_op jit(solution)/shard_map/ppermute | solution.py:217
  11.1 4.5 %collective-permute-start.10 = (f32[2,8,1088]{2,1,0:T(8,128)S(1)}, f32[2,8,1088]{2,1,0:T(8,128)S(1)}, u32[]{:S(2)}, u32[]{:S(2)}) collective-permute-start(f32[2,8,1088]{2,1,0:T(8,128)S(1)} %add.36), channel_id=1, source_target_pairs={{0,1},{1,0},{2,3},{3,2},{4,12},{5,13},{6,14},{7,15},{8,9},{9,8},{1... | collective-permute-start | bytes 208904 | tf_op jit(solution)/shard_map/ppermute | solution.py:332
  13.3 4.4 %collective-permute-start.2 = (f32[2,8,1088]{2,1,0:T(8,128)S(1)}, f32[2,8,1088]{2,1,0:T(8,128)S(1)}, u32[]{:S(2)}, u32[]{:S(2)}) collective-permute-start(f32[2,8,1088]{2,1,0:T(8,128)S(1)} %add.31), channel_id=1, source_target_pairs={{0,1},{1,0},{2,3},{3,2},{4,12},{5,13},{6,14},{7,15},{8,9},{9,8},{1... | collective-permute-start | bytes 208904 | tf_op jit(solution)/shard_map/ppermute | solution.py:332
  14.9 5.2 %collective-permute-start.6 = (f32[2,8,1088]{2,1,0:T(8,128)S(1)}, f32[2,8,1088]{2,1,0:T(8,128)S(1)}, u32[]{:S(2)}, u32[]{:S(2)}) collective-permute-start(f32[2,8,1088]{2,1,0:T(8,128)S(1)} %get-tuple-element.30), channel_id=1, source_target_pairs={{0,8},{4,12},{8,0},{12,4},{16,24},{20,28},{24,16},{28,20},{1,9},{5... | collective-permute-start | bytes 208904 | tf_op jit(solution)/shard_map/ppermute | solution.py:217
  15.7 4.5 %collective-permute-start.11 = (f32[2,8,1088]{2,1,0:T(8,128)S(1)}, f32[2,8,1088]{2,1,0:T(8,128)S(1)}, u32[]{:S(2)}, u32[]{:S(2)}) collective-permute-start(f32[2,8,1088]{2,1,0:T(8,128)S(1)} %add.37), channel_id=1, source_target_pairs={{0,16},{1,17},{2,18},{3,19},{4,6},{5,7},{6,4},{7,5},{8,24},{9,25},... | collective-permute-start | bytes 208904 | tf_op jit(solution)/shard_map/ppermute | solution.py:332
  17.8 5.4 %collective-permute-start.3 = (f32[2,8,1088]{2,1,0:T(8,128)S(1)}, f32[2,8,1088]{2,1,0:T(8,128)S(1)}, u32[]{:S(2)}, u32[]{:S(2)}) collective-permute-start(f32[2,8,1088]{2,1,0:T(8,128)S(1)} %add.32), channel_id=1, source_target_pairs={{0,16},{1,17},{2,18},{3,19},{4,6},{5,7},{6,4},{7,5},{8,24},{9,25},... | collective-permute-start | bytes 208904 | tf_op jit(solution)/shard_map/ppermute | solution.py:332
  20.2 6.5 %collective-permute-start.12 = (f32[2,8,1088]{2,1,0:T(8,128)S(1)}, f32[2,8,1088]{2,1,0:T(8,128)S(1)}, u32[]{:S(2)}, u32[]{:S(2)}) collective-permute-start(f32[2,8,1088]{2,1,0:T(8,128)S(1)} %add.38), channel_id=1, source_target_pairs={{0,2},{1,3},{2,0},{3,1},{4,20},{5,21},{6,22},{7,23},{8,10},{9,11},... | collective-permute-start | bytes 208904 | tf_op jit(solution)/shard_map/ppermute | solution.py:332
  23.2 5.3 %collective-permute-start.4 = (f32[2,8,1088]{2,1,0:T(8,128)S(1)}, f32[2,8,1088]{2,1,0:T(8,128)S(1)}, u32[]{:S(2)}, u32[]{:S(2)}) collective-permute-start(f32[2,8,1088]{2,1,0:T(8,128)S(1)} %add.33), channel_id=1, source_target_pairs={{0,2},{1,3},{2,0},{3,1},{4,20},{5,21},{6,22},{7,23},{8,10},{9,11},... | collective-permute-start | bytes 208904 | tf_op jit(solution)/shard_map/ppermute | solution.py:332
  25.2 3.4 %collective-permute-start.7 = (f32[4,8,1088]{2,1,0:T(8,128)S(1)}, f32[4,8,1088]{2,1,0:T(8,128)S(1)}, u32[]{:S(2)}, u32[]{:S(2)}) collective-permute-start(f32[4,8,1088]{2,1,0:T(8,128)S(1)} %bitcast.18), channel_id=1, source_target_pairs={{0,4},{4,0},{8,12},{12,8},{16,20},{20,16},{24,28},{28,24},{1,5},{5... | collective-permute-start | bytes 417800 | tf_op jit(solution)/shard_map/ppermute | solution.py:217
  26.7 1.9 %collective-permute-start.13 = (f32[2,8,1088]{2,1,0:T(8,128)S(1)}, f32[2,8,1088]{2,1,0:T(8,128)S(1)}, u32[]{:S(2)}, u32[]{:S(2)}) collective-permute-start(f32[2,8,1088]{2,1,0:T(8,128)S(1)} %add.39.rest_0_), channel_id=1, source_target_pairs={{0,4},{4,0},{8,12},{12,8},{16,20},{20,16},{24,28},{28,24},{1,5},{5... | collective-permute-start | bytes 208904 | tf_op jit(solution)/shard_map/ppermute | solution.py:217
  28.5 1.3 %collective-permute-start.14 = (f32[2,8,1088]{2,1,0:T(8,128)S(1)}, f32[2,8,1088]{2,1,0:T(8,128)S(1)}, u32[]{:S(2)}, u32[]{:S(2)}) collective-permute-start(f32[2,8,1088]{2,1,0:T(8,128)S(1)} %add.34.rest_1_), channel_id=1, source_target_pairs={{0,4},{4,0},{8,12},{12,8},{16,20},{20,16},{24,28},{28,24},{1,5},{5... | collective-permute-start | bytes 208904 | tf_op jit(solution)/shard_map/ppermute | solution.py:217

commit v10 on v9

--- a/solution.py
+++ b/solution.py
@@ -182,7 +182,8 @@
     def column_squares(ref):
         return jnp.sum(jnp.sum(ref[...] ** 2, axis=0, keepdims=True), axis=1, keepdims=True)
 
-    grad_squares = sum(column_squares(ref) for ref in grads)
+    own_squares, other_squares = (sum(column_squares(ref) for ref in refs) for refs in (own_refs, other_refs))
+    grad_squares = own_squares + other_squares
     param_squares = column_squares(params_ref)
     factor = jnp.zeros((1, 1, width), F32)
     for start, stop in zip(edges[:-1], edges[1:]):

time: 30.9 us -> 31 us (level)
  no operation moved by 1% of the time
where the time goes in v10:
time: 31 us; the launch traced here: 30.8 us
  starting transfers between devices  20.2 us (65%)
  Pallas kernels  6.13 us (20%)
  waiting for transfers between devices  3.58 us (12%)
  between operations  0.76 us (2%)
    ppermute x8, starting transfers between devices, shards(): lax.ppermute(total, ('gx', 'gy'), table)  16.1 us
    ppermute x7, starting transfers between devices, flip(): lax.ppermute(value, axis, [(i, i ^ bit) for i in range(lax.axis_size(axis...  4.08 us
    pallas_call x1, Pallas kernels, shards(): pl.pallas_call(functools.partial(grad_kernel, height=height, width=width,...  3.15 us
    ppermute x7, waiting for transfers between devices, flip(): lax.ppermute(value, axis, [(i, i ^ bit) for i in range(lax.axis_size(axis...  2.08 us
    ppermute x8, waiting for transfers between devices, shards(): lax.ppermute(total, ('gx', 'gy'), table)  1.5 us
    pallas_call x1, Pallas kernels, shards(): pl.pallas_call(input_grad_kernel, out_shape=jax.ShapeDtypeStruct((pixels,...  1.45 us
    pallas_call x1, Pallas kernels, shards(): pl.pallas_call(functools.partial(update_kernel, c_in=c_in, mid=mid), out_...  0.94 us
  transfers between devices with their start and end apart: 15, of which 5 were waited for; matrix products, arithmetic and copies ran while one was open for 0% of the time, Pallas kernels for 5%

profile of v10, /device:TPU:0, one launch (start us, length us, event | category | flops | bytes accessed | tf_op | source)
XLA Modules:
  0.0 30.8 jit_solution(4917575289512723866)
XLA Ops:
  0.6 3.2 %grads.1 = (bf16[2240,128]{1,0:T(8,128)(2,1)S(1)}, bf16[2240,256]{1,0:T(8,128)(2,1)S(1)}, bf16[2240,256]{1,0:T(8,128)(2,1)S(1)}, f32[64,1088]{1,0:T(8,128)S(1)}, f32[192,256]{1,0:T(8,128)S(1)}) custom-call(s32[1]{0:T(128)} %bitcast.place_ref, bf16[2240,256]{1,0:T(8,128)(2,1)} %bitcast.21, bf16[40,3584]{1,0:T(8,128)(2,1)} %bitcast.23, ...), custom_call_target="tpu_custom_call" | custom-call | tf_op jit(solution)/shard_map/grads/pallas_call | solution.py:260
  3.8 0.0 copy-start
  3.8 0.6 %sides.1 = (f32[2,8,1088]{2,1,0:T(8,128)S(1)}, f32[2,8,1088]{2,1,0:T(8,128)S(1)}, f32[2,8,1088]{2,1,0:T(8,128)S(1)}, f32[2,8,1088]{2,1,0:T(8,128)S(1)}) custom-call(s32[1]{0:T(128)} %bitcast.place_ref, bf16[2240,128]{1,0:T(8,128)(2,1)S(1)} %get-tuple-element.16.left_ref, bf16[2240,256]{1,0:T(8,128)(2,1)S(1)} %get-tuple-element.17.x_ref, ...), custom_call_target="tpu_custom_call" | custom-call | flops 146800640 | bytes 2867200 | tf_op jit(solution)/shard_map/sides/pallas_call | solution.py:300
  4.4 0.6 %collective-permute-start.8 = (f32[2,8,1088]{2,1,0:T(8,128)S(1)}, f32[2,8,1088]{2,1,0:T(8,128)S(1)}, u32[]{:S(2)}, u32[]{:S(2)}) collective-permute-start(f32[2,8,1088]{2,1,0:T(8,128)S(1)} %get-tuple-element.25), channel_id=1, source_target_pairs={{0,4},{4,0},{8,12},{12,8},{16,20},{20,16},{24,28},{28,24},{1,5},{5... | collective-permute-start | bytes 208904 | tf_op jit(solution)/shard_map/ppermute | solution.py:218
  5.0 0.1 collective-permute-start
  5.0 0.8 %collective-permute-done.8 = f32[2,8,1088]{2,1,0:T(8,128)S(1)} collective-permute-done((f32[2,8,1088]{2,1,0:T(8,128)S(1)}, f32[2,8,1088]{2,1,0:T(8,128)S(1)}, u32[]{:S(2)}, u32[]{:S(2)}) %collective-permute-start.8) | collective-permute-done | bytes 69664 | tf_op jit(solution)/shard_map/ppermute | solution.py:218
  5.9 2.9 %collective-permute-start.9 = (f32[2,8,1088]{2,1,0:T(8,128)S(1)}, f32[2,8,1088]{2,1,0:T(8,128)S(1)}, u32[]{:S(2)}, u32[]{:S(2)}) collective-permute-start(f32[2,8,1088]{2,1,0:T(8,128)S(1)} %add.35), channel_id=1, source_target_pairs={{0,8},{1,9},{2,10},{3,11},{4,5},{5,4},{6,7},{7,6},{8,0},{9,1},{10,... | collective-permute-start | bytes 208904 | tf_op jit(solution)/shard_map/ppermute | solution.py:333
  8.8 0.0 collective-permute-done
  8.8 0.1 collective-permute-start.1
  8.9 0.0 copy-done
  8.9 2.0 %collective-permute-start.5 = (f32[1,8,1088]{2,1,0:T(8,128)S(1)}, f32[1,8,1088]{2,1,0:T(8,128)S(1)}, u32[]{:S(2)}, u32[]{:S(2)}) collective-permute-start(f32[1,8,1088]{2,1,0:T(8,128)S(1)} %bitcast.26), channel_id=1, source_target_pairs={{0,16},{4,20},{8,24},{12,28},{16,0},{20,4},{24,8},{28,12},{1,17},{... | collective-permute-start | bytes 104456 | tf_op jit(solution)/shard_map/ppermute | solution.py:218
  10.9 0.2 collective-permute-done.9
  11.1 2.2 %collective-permute-start.10 = (f32[2,8,1088]{2,1,0:T(8,128)S(1)}, f32[2,8,1088]{2,1,0:T(8,128)S(1)}, u32[]{:S(2)}, u32[]{:S(2)}) collective-permute-start(f32[2,8,1088]{2,1,0:T(8,128)S(1)} %add.36), channel_id=1, source_target_pairs={{0,1},{1,0},{2,3},{3,2},{4,12},{5,13},{6,14},{7,15},{8,9},{9,8},{1... | collective-permute-start | bytes 208904 | tf_op jit(solution)/shard_map/ppermute | solution.py:333
  13.3 0.0 collective-permute-done.1
  13.3 1.6 %collective-permute-start.2 = (f32[2,8,1088]{2,1,0:T(8,128)S(1)}, f32[2,8,1088]{2,1,0:T(8,128)S(1)}, u32[]{:S(2)}, u32[]{:S(2)}) collective-permute-start(f32[2,8,1088]{2,1,0:T(8,128)S(1)} %add.31), channel_id=1, source_target_pairs={{0,1},{1,0},{2,3},{3,2},{4,12},{5,13},{6,14},{7,15},{8,9},{9,8},{1... | collective-permute-start | bytes 208904 | tf_op jit(solution)/shard_map/ppermute | solution.py:333
  14.9 0.0 collective-permute-done.5
  14.9 0.8 %collective-permute-start.6 = (f32[2,8,1088]{2,1,0:T(8,128)S(1)}, f32[2,8,1088]{2,1,0:T(8,128)S(1)}, u32[]{:S(2)}, u32[]{:S(2)}) collective-permute-start(f32[2,8,1088]{2,1,0:T(8,128)S(1)} %get-tuple-element.30), channel_id=1, source_target_pairs={{0,8},{4,12},{8,0},{12,4},{16,24},{20,28},{24,16},{28,20},{1,9},{5... | collective-permute-start | bytes 208904 | tf_op jit(solution)/shard_map/ppermute | solution.py:218
  15.7 0.0 collective-permute-done.10
  15.7 2.0 %collective-permute-start.11 = (f32[2,8,1088]{2,1,0:T(8,128)S(1)}, f32[2,8,1088]{2,1,0:T(8,128)S(1)}, u32[]{:S(2)}, u32[]{:S(2)}) collective-permute-start(f32[2,8,1088]{2,1,0:T(8,128)S(1)} %add.37), channel_id=1, source_target_pairs={{0,16},{1,17},{2,18},{3,19},{4,6},{5,7},{6,4},{7,5},{8,24},{9,25},... | collective-permute-start | bytes 208904 | tf_op jit(solution)/shard_map/ppermute | solution.py:333
  17.7 0.1 collective-permute-done.2
  17.8 2.4 %collective-permute-start.3 = (f32[2,8,1088]{2,1,0:T(8,128)S(1)}, f32[2,8,1088]{2,1,0:T(8,128)S(1)}, u32[]{:S(2)}, u32[]{:S(2)}) collective-permute-start(f32[2,8,1088]{2,1,0:T(8,128)S(1)} %add.32), channel_id=1, source_target_pairs={{0,16},{1,17},{2,18},{3,19},{4,6},{5,7},{6,4},{7,5},{8,24},{9,25},... | collective-permute-start | bytes 208904 | tf_op jit(solution)/shard_map/ppermute | solution.py:333
  20.1 0.0 collective-permute-done.6
  20.1 0.0 collective-permute-done.11
  20.2 3.0 %collective-permute-start.12 = (f32[2,8,1088]{2,1,0:T(8,128)S(1)}, f32[2,8,1088]{2,1,0:T(8,128)S(1)}, u32[]{:S(2)}, u32[]{:S(2)}) collective-permute-start(f32[2,8,1088]{2,1,0:T(8,128)S(1)} %add.38), channel_id=1, source_target_pairs={{0,2},{1,3},{2,0},{3,1},{4,20},{5,21},{6,22},{7,23},{8,10},{9,11},... | collective-permute-start | bytes 208904 | tf_op jit(solution)/shard_map/ppermute | solution.py:333
  23.2 0.0 collective-permute-done.3
  23.2 2.0 %collective-permute-start.4 = (f32[2,8,1088]{2,1,0:T(8,128)S(1)}, f32[2,8,1088]{2,1,0:T(8,128)S(1)}, u32[]{:S(2)}, u32[]{:S(2)}) collective-permute-start(f32[2,8,1088]{2,1,0:T(8,128)S(1)} %add.33), channel_id=1, source_target_pairs={{0,2},{1,3},{2,0},{3,1},{4,20},{5,21},{6,22},{7,23},{8,10},{9,11},... | collective-permute-start | bytes 208904 | tf_op jit(solution)/shard_map/ppermute | solution.py:333
  25.2 0.1 collective-permute-start.7
  25.3 1.5 %input_grad.1 = bf16[2240,256]{1,0:T(8,128)(2,1)} custom-call(bf16[2240,128]{1,0:T(8,128)(2,1)S(1)} %get-tuple-element.16.left_ref, bf16[2240,256]{1,0:T(8,128)(2,1)S(1)} %get-tuple-element.18.out_ref, f32[64,1088]{1,0:T(8,128)S(1)} %get-tuple-element.22.params_ref), custom_call_target="tpu_custom_call" | custom-call | flops 73400320 | bytes 2580480 | tf_op jit(solution)/shard_map/input_grad/pallas_call | solution.py:312
  26.7 0.0 collective-permute-done.12
  26.7 0.6 %collective-permute-start.13 = (f32[2,8,1088]{2,1,0:T(8,128)S(1)}, f32[2,8,1088]{2,1,0:T(8,128)S(1)}, u32[]{:S(2)}, u32[]{:S(2)}) collective-permute-start(f32[2,8,1088]{2,1,0:T(8,128)S(1)} %add.39.rest_0_), channel_id=1, source_target_pairs={{0,4},{4,0},{8,12},{12,8},{16,20},{20,16},{24,28},{28,24},{1,5},{5... | collective-permute-start | bytes 208904 | tf_op jit(solution)/shard_map/ppermute | solution.py:218
  27.3 1.2 %collective-permute-done.4 = f32[2,8,1088]{2,1,0:T(8,128)S(1)} collective-permute-done((f32[2,8,1088]{2,1,0:T(8,128)S(1)}, f32[2,8,1088]{2,1,0:T(8,128)S(1)}, u32[]{:S(2)}, u32[]{:S(2)}) %collective-permute-start.4) | collective-permute-done | bytes 69664 | tf_op jit(solution)/shard_map/ppermute | solution.py:333
  28.5 0.1 collective-permute-start.14
  28.6 0.0 collective-permute-done.7.other_speed_ref
  28.6 0.0 collective-permute-done.13.rest_2_
  28.6 1.2 %collective-permute-done.14.rest_3_ = f32[2,8,1088]{2,1,0:T(8,128)S(1)} collective-permute-done((f32[2,8,1088]{2,1,0:T(8,128)S(1)}, f32[2,8,1088]{2,1,0:T(8,128)S(1)}, u32[]{:S(2)}, u32[]{:S(2)}) %collective-permute-start.14) | collective-permute-done | bytes 69664 | tf_op jit(solution)/shard_map/ppermute | solution.py:218
  29.9 0.9 %update.1 = (f32[8,1088]{1,0:T(8,128)}, f32[8,8,1088]{2,1,0:T(8,128)}) custom-call(s32[1]{0:T(128)} %bitcast.place_ref, f32[4,8,1088]{2,1,0:T(8,128)S(1)} %bitcast.19, f32[4,8,1088]{2,1,0:T(8,128)S(1)} %collective-permute-done.7.other_speed_ref, f32[8,8,1088]{2,1,0:T(8,128)S(1)} %bitcast.17, f32[2,8,1088]{2,1,0:T(8,128)S(1)} %add.39.rest_0_, ...), custom_call_target="tpu_custom_call" | custom-call | tf_op jit(solution)/shard_map/update/pallas_call | solution.py:344
  (13 shorter events, 0.1 us)
Async XLA Ops:
  3.8 5.1 %copy-start = (f32[8,1088]{1,0:T(8,128)S(1)}, f32[8,1088]{1,0:T(8,128)}, u32[]{:S(2)}) copy-start(f32[8,1088]{1,0:T(8,128)} %param.11) | copy-start | bytes 104452
  4.4 1.5 %collective-permute-start.8 = (f32[2,8,1088]{2,1,0:T(8,128)S(1)}, f32[2,8,1088]{2,1,0:T(8,128)S(1)}, u32[]{:S(2)}, u32[]{:S(2)}) collective-permute-start(f32[2,8,1088]{2,1,0:T(8,128)S(1)} %get-tuple-element.25), channel_id=1, source_target_pairs={{0,4},{4,0},{8,12},{12,8},{16,20},{20,16},{24,28},{28,24},{1,5},{5... | collective-permute-start | bytes 208904 | tf_op jit(solution)/shard_map/ppermute | solution.py:218
  5.0 3.8 %collective-permute-start = (f32[2,8,1088]{2,1,0:T(8,128)S(1)}, f32[2,8,1088]{2,1,0:T(8,128)S(1)}, u32[]{:S(2)}, u32[]{:S(2)}) collective-permute-start(f32[2,8,1088]{2,1,0:T(8,128)S(1)} %get-tuple-element.21), channel_id=1, source_target_pairs={{0,4},{4,0},{8,12},{12,8},{16,20},{20,16},{24,28},{28,24},{1,5},{5... | collective-permute-start | bytes 208904 | tf_op jit(solution)/shard_map/ppermute | solution.py:218
  5.9 5.2 %collective-permute-start.9 = (f32[2,8,1088]{2,1,0:T(8,128)S(1)}, f32[2,8,1088]{2,1,0:T(8,128)S(1)}, u32[]{:S(2)}, u32[]{:S(2)}) collective-permute-start(f32[2,8,1088]{2,1,0:T(8,128)S(1)} %add.35), channel_id=1, source_target_pairs={{0,8},{1,9},{2,10},{3,11},{4,5},{5,4},{6,7},{7,6},{8,0},{9,1},{10,... | collective-permute-start | bytes 208904 | tf_op jit(solution)/shard_map/ppermute | solution.py:333
  8.8 4.5 %collective-permute-start.1 = (f32[2,8,1088]{2,1,0:T(8,128)S(1)}, f32[2,8,1088]{2,1,0:T(8,128)S(1)}, u32[]{:S(2)}, u32[]{:S(2)}) collective-permute-start(f32[2,8,1088]{2,1,0:T(8,128)S(1)} %add.30), channel_id=1, source_target_pairs={{0,8},{1,9},{2,10},{3,11},{4,5},{5,4},{6,7},{7,6},{8,0},{9,1},{10,... | collective-permute-start | bytes 208904 | tf_op jit(solution)/shard_map/ppermute | solution.py:333
  8.9 5.9 %collective-permute-start.5 = (f32[1,8,1088]{2,1,0:T(8,128)S(1)}, f32[1,8,1088]{2,1,0:T(8,128)S(1)}, u32[]{:S(2)}, u32[]{:S(2)}) collective-permute-start(f32[1,8,1088]{2,1,0:T(8,128)S(1)} %bitcast.26), channel_id=1, source_target_pairs={{0,16},{4,20},{8,24},{12,28},{16,0},{20,4},{24,8},{28,12},{1,17},{... | collective-permute-start | bytes 104456 | tf_op jit(solution)/shard_map/ppermute | solution.py:218
  11.1 4.5 %collective-permute-start.10 = (f32[2,8,1088]{2,1,0:T(8,128)S(1)}, f32[2,8,1088]{2,1,0:T(8,128)S(1)}, u32[]{:S(2)}, u32[]{:S(2)}) collective-permute-start(f32[2,8,1088]{2,1,0:T(8,128)S(1)} %add.36), channel_id=1, source_target_pairs={{0,1},{1,0},{2,3},{3,2},{4,12},{5,13},{6,14},{7,15},{8,9},{9,8},{1... | collective-permute-start | bytes 208904 | tf_op jit(solution)/shard_map/ppermute | solution.py:333
  13.3 4.4 %collective-permute-start.2 = (f32[2,8,1088]{2,1,0:T(8,128)S(1)}, f32[2,8,1088]{2,1,0:T(8,128)S(1)}, u32[]{:S(2)}, u32[]{:S(2)}) collective-permute-start(f32[2,8,1088]{2,1,0:T(8,128)S(1)} %add.31), channel_id=1, source_target_pairs={{0,1},{1,0},{2,3},{3,2},{4,12},{5,13},{6,14},{7,15},{8,9},{9,8},{1... | collective-permute-start | bytes 208904 | tf_op jit(solution)/shard_map/ppermute | solution.py:333
  14.9 5.2 %collective-permute-start.6 = (f32[2,8,1088]{2,1,0:T(8,128)S(1)}, f32[2,8,1088]{2,1,0:T(8,128)S(1)}, u32[]{:S(2)}, u32[]{:S(2)}) collective-permute-start(f32[2,8,1088]{2,1,0:T(8,128)S(1)} %get-tuple-element.30), channel_id=1, source_target_pairs={{0,8},{4,12},{8,0},{12,4},{16,24},{20,28},{24,16},{28,20},{1,9},{5... | collective-permute-start | bytes 208904 | tf_op jit(solution)/shard_map/ppermute | solution.py:218
  15.7 4.5 %collective-permute-start.11 = (f32[2,8,1088]{2,1,0:T(8,128)S(1)}, f32[2,8,1088]{2,1,0:T(8,128)S(1)}, u32[]{:S(2)}, u32[]{:S(2)}) collective-permute-start(f32[2,8,1088]{2,1,0:T(8,128)S(1)} %add.37), channel_id=1, source_target_pairs={{0,16},{1,17},{2,18},{3,19},{4,6},{5,7},{6,4},{7,5},{8,24},{9,25},... | collective-permute-start | bytes 208904 | tf_op jit(solution)/shard_map/ppermute | solution.py:333
  17.8 5.4 %collective-permute-start.3 = (f32[2,8,1088]{2,1,0:T(8,128)S(1)}, f32[2,8,1088]{2,1,0:T(8,128)S(1)}, u32[]{:S(2)}, u32[]{:S(2)}) collective-permute-start(f32[2,8,1088]{2,1,0:T(8,128)S(1)} %add.32), channel_id=1, source_target_pairs={{0,16},{1,17},{2,18},{3,19},{4,6},{5,7},{6,4},{7,5},{8,24},{9,25},... | collective-permute-start | bytes 208904 | tf_op jit(solution)/shard_map/ppermute | solution.py:333
  20.2 6.5 %collective-permute-start.12 = (f32[2,8,1088]{2,1,0:T(8,128)S(1)}, f32[2,8,1088]{2,1,0:T(8,128)S(1)}, u32[]{:S(2)}, u32[]{:S(2)}) collective-permute-start(f32[2,8,1088]{2,1,0:T(8,128)S(1)} %add.38), channel_id=1, source_target_pairs={{0,2},{1,3},{2,0},{3,1},{4,20},{5,21},{6,22},{7,23},{8,10},{9,11},... | collective-permute-start | bytes 208904 | tf_op jit(solution)/shard_map/ppermute | solution.py:333
  23.2 5.3 %collective-permute-start.4 = (f32[2,8,1088]{2,1,0:T(8,128)S(1)}, f32[2,8,1088]{2,1,0:T(8,128)S(1)}, u32[]{:S(2)}, u32[]{:S(2)}) collective-permute-start(f32[2,8,1088]{2,1,0:T(8,128)S(1)} %add.33), channel_id=1, source_target_pairs={{0,2},{1,3},{2,0},{3,1},{4,20},{5,21},{6,22},{7,23},{8,10},{9,11},... | collective-permute-start | bytes 208904 | tf_op jit(solution)/shard_map/ppermute | solution.py:333
  25.2 3.4 %collective-permute-start.7 = (f32[4,8,1088]{2,1,0:T(8,128)S(1)}, f32[4,8,1088]{2,1,0:T(8,128)S(1)}, u32[]{:S(2)}, u32[]{:S(2)}) collective-permute-start(f32[4,8,1088]{2,1,0:T(8,128)S(1)} %bitcast.18), channel_id=1, source_target_pairs={{0,4},{4,0},{8,12},{12,8},{16,20},{20,16},{24,28},{28,24},{1,5},{5... | collective-permute-start | bytes 417800 | tf_op jit(solution)/shard_map/ppermute | solution.py:218
  26.7 1.9 %collective-permute-start.13 = (f32[2,8,1088]{2,1,0:T(8,128)S(1)}, f32[2,8,1088]{2,1,0:T(8,128)S(1)}, u32[]{:S(2)}, u32[]{:S(2)}) collective-permute-start(f32[2,8,1088]{2,1,0:T(8,128)S(1)} %add.39.rest_0_), channel_id=1, source_target_pairs={{0,4},{4,0},{8,12},{12,8},{16,20},{20,16},{24,28},{28,24},{1,5},{5... | collective-permute-start | bytes 208904 | tf_op jit(solution)/shard_map/ppermute | solution.py:218
  28.5 1.3 %collective-permute-start.14 = (f32[2,8,1088]{2,1,0:T(8,128)S(1)}, f32[2,8,1088]{2,1,0:T(8,128)S(1)}, u32[]{:S(2)}, u32[]{:S(2)}) collective-permute-start(f32[2,8,1088]{2,1,0:T(8,128)S(1)} %add.34.rest_1_), channel_id=1, source_target_pairs={{0,4},{4,0},{8,12},{12,8},{16,20},{20,16},{24,28},{28,24},{1,5},{5... | collective-permute-start | bytes 208904 | tf_op jit(solution)/shard_map/ppermute | solution.py:218
